TPU v7x, 512 devices: a whole 4x4x16 slice. The times are simulated.
512 devices in a mesh: tm: 16 (over x, y_lo, core), slab: 32 (over z, y_hi).
Axes of the slice: x: 4, y: 4 (y_hi: 2, y_lo: 2; y = y_hi * 2 + y_lo), z: 16, core: 2. Of those that a mesh axis runs over, the one named last changes fastest.
Arguments:
- starts: float32 [16, 4, 256, 64, 128], P('tm', None, 'slab'), may hold values from 0 to 1
- tissue: int32 [256, 64, 128], P('slab'), may hold values 0 or 1
- fibers: int32 [256, 64, 128], P('slab'), may hold values from 0 to 3
- pacing: int32 [256, 64, 128], P('slab'), may hold values 0 or 1
- conductances: float32 [4, 3], replicated, may hold values from 0.1 to 2, as said below
Outputs:
- defect: float32 [16, 4, 256, 64, 128], P('tm', None, 'slab')
- gradient: float32 [16, 4, 256, 64, 128], P('tm', None, 'slab')
Inputs may be any that keep to these rules, and one draw needn't show every extreme that they name: `conductances`: the apex-to-base column lies between 1.0 and 2.0, the two cross columns between 0.1 and 0.4.
All inputs are finite; a program needn't handle non-finite values. No bound on the sum of `tissue` or of `pacing` on one device may be relied on, other than what follows from the above.
Results may differ from a plain program's by a relative error of at most 0.00002.
Values sent between devices are 32-bit elements; how exact they have to be, the bound alone decides.
No kernel may reach another device: no remote copies, remote signals or barrier semaphores. Data moves between devices by JAX's collectives and lax.ppermute only.
A program may use at most 64 MiB of HBM per device.

v0:
```python
import jax
import jax.numpy as jnp
from jax import lax
from jax.sharding import PartitionSpec as P

STEPS = 4


TIME_STEP = 0.15
FAST_GAIN = 2.0
SLOW_GAIN = 1.0
STIM_GAIN = 4.0
GATE_SLOPE = 8.0
GATE_RATES = (0.3, 0.1, 0.03)
GATE_MIDDLES = (0.2, 0.5, 0.8)


def padded_2(block, sides, width):
    for axis, dim in sides:
        count = lax.axis_size(axis)
        forward = [(i, i + 1) for i in range(count - 1)]
        backward = [(target, source) for source, target in forward]
        low = lax.ppermute(
            lax.slice_in_dim(block, block.shape[dim] - width, None, axis=dim), axis, forward
        )
        high = lax.ppermute(lax.slice_in_dim(block, 0, width, axis=dim), axis, backward)
        block = jnp.concatenate([low, block, high], axis=dim)
    return block


def passed_along(value, axis, steps):
    count = lax.axis_size(axis)
    pairs = [(source, (source + steps) % count) for source in range(count)]
    return lax.ppermute(value, axis, pairs)


def pad_axis(operand, axis_index):
    widths = [(0, 0)] * operand.ndim
    widths[axis_index] = (1, 1)
    return jnp.pad(operand, widths)


def conductivity(fibers, conductances, axis_index):
    summed = jnp.zeros(fibers.shape, jnp.float32)
    for class_index in range(conductances.shape[0]):
        summed = summed + jnp.where(
            fibers == class_index, conductances[class_index, axis_index], jnp.zeros((), jnp.float32)
        )
    return summed


def pair_weight(sigma_padded, share_padded, axis_index):
    length = sigma_padded.shape[axis_index]
    low_sigma = lax.slice_in_dim(sigma_padded, 0, length - 1, axis=axis_index)
    high_sigma = lax.slice_in_dim(sigma_padded, 1, length, axis=axis_index)
    low_share = lax.slice_in_dim(share_padded, 0, length - 1, axis=axis_index)
    high_share = lax.slice_in_dim(share_padded, 1, length, axis=axis_index)
    return TIME_STEP * 0.5 * (low_sigma + high_sigma) * low_share * high_share


def diffuse(padded_depth, weights):
    voltage = padded_depth[1:-1]
    depth_flux = weights[0] * (padded_depth[1:] - padded_depth[:-1])
    across = pad_axis(voltage, 1)
    across_flux = weights[1] * (across[:, 1:] - across[:, :-1])
    lengthwise = pad_axis(voltage, 2)
    lengthwise_flux = weights[2] * (lengthwise[:, :, 1:] - lengthwise[:, :, :-1])
    return (
        depth_flux[1:]
        - depth_flux[:-1]
        + (across_flux[:, 1:] - across_flux[:, :-1])
        + (lengthwise_flux[:, :, 1:] - lengthwise_flux[:, :, :-1])
    )


def reaction_step(fields, stimulus):
    voltage, gate_one, gate_two, gate_three = (fields[0], fields[1], fields[2], fields[3])
    current = (
        FAST_GAIN * gate_one * gate_two * (1.0 - voltage)
        - SLOW_GAIN * gate_three * voltage
        + stimulus
    )
    target_one = jax.nn.sigmoid(GATE_SLOPE * (voltage - GATE_MIDDLES[0]))
    target_two = jax.nn.sigmoid(GATE_SLOPE * (GATE_MIDDLES[1] - voltage))
    target_three = jax.nn.sigmoid(GATE_SLOPE * (voltage - GATE_MIDDLES[2]))
    return jnp.stack(
        [
            voltage + TIME_STEP * current,
            gate_one + GATE_RATES[0] * (target_one - gate_one),
            gate_two + GATE_RATES[1] * (target_two - gate_two),
            gate_three + GATE_RATES[2] * (target_three - gate_three),
        ]
    )


def advance_once(fields, stimulus, weights):
    padded = padded_2(fields[0], (("slab", 0),), 1)
    reacted = reaction_step(fields, stimulus)
    return reacted.at[0].add(diffuse(padded, weights))


def pull_once(fields, adjoint, stimulus, weights):
    padded = padded_2(adjoint[0], (("slab", 0),), 1)
    local_pull = jax.vjp(lambda operand: reaction_step(operand, stimulus), fields)[1](adjoint)[0]
    return local_pull.at[0].add(diffuse(padded, weights))


def body(starts, tissue, fibers, pacing, conductances):
    share = tissue.astype(jnp.float32)
    first_flag = (lax.axis_index("tm") == 0).astype(jnp.float32)
    depth_edges = padded_2(
        jnp.stack([conductivity(fibers, conductances, 0), share]), (("slab", 1),), 1
    )
    weights = (
        pair_weight(depth_edges[0], depth_edges[1], 0),
        pair_weight(pad_axis(conductivity(fibers, conductances, 1), 1), pad_axis(share, 1), 1),
        pair_weight(pad_axis(conductivity(fibers, conductances, 2), 2), pad_axis(share, 2), 2),
    )
    stimulus = STIM_GAIN * pacing.astype(jnp.float32) * first_flag
    history = []
    fields = starts[0]
    for step_index in range(STEPS):
        history.append(fields)
        fields = advance_once(fields, stimulus, weights)
    ending = fields[None]
    before = passed_along(ending, "tm", 1)
    defect = before - starts
    upcoming = passed_along(defect, "tm", -1)
    adjoint = upcoming[0]
    for step_index in reversed(range(STEPS)):
        adjoint = pull_once(history[step_index], adjoint, stimulus, weights)
    gradient = adjoint[None] - defect
    return (defect, gradient)


def solution(mesh):
    placed = (
        P("tm", None, "slab", None, None),
        P("slab", None, None),
        P("slab", None, None),
        P("slab", None, None),
        P(),
    )
    return jax.shard_map(
        body,
        mesh=mesh,
        in_specs=placed,
        out_specs=(P("tm", None, "slab", None, None), P("tm", None, "slab", None, None)),
        check_vma=False,
    )
```

profile of v0, /device:TPU:16, one launch (start us, length us, event | category | flops | bytes accessed | tf_op | source)
XLA Modules:
  0.0 158.4 jit_solution(6772162045878744942)
XLA Ops:
  0.6 0.8 slice_bitcast_fusion.19
  1.4 3.7 %collective-permute-start.3 = (f32[1,64,128]{2,1,0:T(8,128)S(1)}, f32[1,64,128]{2,1,0:T(8,128)S(1)}, u32[]{:S(2)}, u32[]{:S(2)}) collective-permute-start(f32[1,64,128]{2,1,0:T(8,128)S(1)} %get-tuple-element.139), channel_id=1, source_target_pairs={{0,1},{1,2},{2,3},{3,4},{4,5},{5,6},{6,7},{7,8},{8,9},{9,10},{10,1... | collective-permute-start | bytes 98312 | tf_op jit(solution)/shard_map/ppermute | solution.py:23
  5.1 5.3 %collective-permute-start.2 = (f32[1,64,128]{2,1,0:T(8,128)S(1)}, f32[1,64,128]{2,1,0:T(8,128)S(1)}, u32[]{:S(2)}, u32[]{:S(2)}) collective-permute-start(f32[1,64,128]{2,1,0:T(8,128)S(1)} %get-tuple-element.140), channel_id=1, source_target_pairs={{1,0},{2,1},{3,2},{4,3},{5,4},{6,5},{7,6},{8,7},{9,8},{10,9},{11,1... | collective-permute-start | bytes 98312 | tf_op jit(solution)/shard_map/ppermute | solution.py:26
  10.5 0.7 fusion.165
  11.2 1.1 convert_bitcast_fusion
  12.3 2.7 %add_bitcast_fusion.6 = (f32[1,8,64,128]{3,2,1,0:T(8,128)S(1)}, pred[8,64,128]{2,1,0:T(8,128)(4,1)S(1)}, pred[8,64,128]{2,1,0:T(8,128)(4,1)S(1)}, pred[8,64,128]{2,1,0:T(8,128)(4,1)S(1)}, pred[8,64,128]{2,1,0:T(8,128)(4,1)S(1)}) fusion(f32[]{:T(128)} %bitcast.7, f32[]{:T(128)} %bitcast.6, f32[]{:T(128)} %bitcast.5, f32[]{:T(128)} %bitcast.4, ...), kind=kLoop, calls=%fused_computation.301 | loop fusion | flops 720896 | bytes 786448 | tf_op jit(solution)/shard_map/stack | solution.py:112
  15.0 2.9 %collective-permute-start = (f32[2,1,64,128]{3,2,1,0:T(8,128)S(1)}, f32[2,1,64,128]{3,2,1,0:T(8,128)S(1)}, u32[]{:S(2)}, u32[]{:S(2)}) collective-permute-start(f32[2,1,64,128]{3,2,1,0:T(8,128)S(1)} %get-tuple-element.143), channel_id=1, source_target_pairs={{0,1},{1,2},{2,3},{3,4},{4,5},{5,6},{6,7},{7,8},{8,9},{9,10},{10,1... | collective-permute-start | bytes 196616 | tf_op jit(solution)/shard_map/ppermute | solution.py:23
  18.0 4.4 %collective-permute-start.1 = (f32[2,1,64,128]{3,2,1,0:T(8,128)S(1)}, f32[2,1,64,128]{3,2,1,0:T(8,128)S(1)}, u32[]{:S(2)}, u32[]{:S(2)}) collective-permute-start(f32[2,1,64,128]{3,2,1,0:T(8,128)S(1)} %get-tuple-element.144), channel_id=1, source_target_pairs={{1,0},{2,1},{3,2},{4,3},{5,4},{6,5},{7,6},{8,7},{9,8},{10,9},{11,1... | collective-permute-start | bytes 196616 | tf_op jit(solution)/shard_map/ppermute | solution.py:26
  22.4 5.2 %select_add_fusion.1 = (f32[8,64,128]{2,1,0:T(8,128)S(1)}, f32[8,64,128]{2,1,0:T(8,128)S(1)}) fusion(pred[8,64,128]{2,1,0:T(8,128)(4,1)S(1)} %get-tuple-element.117, pred[8,64,128]{2,1,0:T(8,128)(4,1)S(1)} %get-tuple-element.116, pred[8,64,128]{2,1,0:T(8,128)(4,1)S(1)} %get-tuple-element.115, pred[8,64,128]{2,1,0:T(8,128)(4,1)S(1)} %get-tuple-element.114, ...), kind=kLoop, calls=%fused_computation.300 | loop fusion | flops 917504 | bytes 786464 | tf_op jit(solution)/shard_map/add | solution.py:46
  27.6 0.5 fusion.5
  28.1 0.1 subtract_multiply_fusion.19
  28.3 0.1 maximum_maximum_fusion
  28.4 0.1 fusion.22
  28.6 0.8 copy-done.2
  29.4 0.2 fusion.115
  29.6 3.8 %collective-permute-start.5 = (f32[1,64,128]{2,1,0:T(8,128)S(1)}, f32[1,64,128]{2,1,0:T(8,128)S(1)}, u32[]{:S(2)}, u32[]{:S(2)}) collective-permute-start(f32[1,64,128]{2,1,0:T(8,128)S(1)} %get-tuple-element.158), channel_id=1, source_target_pairs={{0,1},{1,2},{2,3},{3,4},{4,5},{5,6},{6,7},{7,8},{8,9},{9,10},{10,1... | collective-permute-start | bytes 98312 | tf_op jit(solution)/shard_map/ppermute | solution.py:23
  33.5 3.5 %collective-permute-start.4 = (f32[1,64,128]{2,1,0:T(8,128)S(1)}, f32[1,64,128]{2,1,0:T(8,128)S(1)}, u32[]{:S(2)}, u32[]{:S(2)}) collective-permute-start(f32[1,64,128]{2,1,0:T(8,128)S(1)} %get-tuple-element.159), channel_id=1, source_target_pairs={{1,0},{2,1},{3,2},{4,3},{5,4},{6,5},{7,6},{8,7},{9,8},{10,9},{11,1... | collective-permute-start | bytes 98312 | tf_op jit(solution)/shard_map/ppermute | solution.py:26
  37.0 0.2 fusion.7
  37.3 4.4 %collective-permute-done.4 = f32[1,64,128]{2,1,0:T(8,128)S(1)} collective-permute-done((f32[1,64,128]{2,1,0:T(8,128)S(1)}, f32[1,64,128]{2,1,0:T(8,128)S(1)}, u32[]{:S(2)}, u32[]{:S(2)}) %collective-permute-start.4) | collective-permute-done | bytes 32800 | tf_op jit(solution)/shard_map/ppermute | solution.py:26
  41.7 0.4 fusion.112
  42.2 0.2 fusion.9
  42.4 2.4 %collective-permute-start.7 = (f32[1,64,128]{2,1,0:T(8,128)S(1)}, f32[1,64,128]{2,1,0:T(8,128)S(1)}, u32[]{:S(2)}, u32[]{:S(2)}) collective-permute-start(f32[1,64,128]{2,1,0:T(8,128)S(1)} %get-tuple-element.156), channel_id=1, source_target_pairs={{0,1},{1,2},{2,3},{3,4},{4,5},{5,6},{6,7},{7,8},{8,9},{9,10},{10,1... | collective-permute-start | bytes 98312 | tf_op jit(solution)/shard_map/ppermute | solution.py:23
  44.8 4.9 %collective-permute-start.6 = (f32[1,64,128]{2,1,0:T(8,128)S(1)}, f32[1,64,128]{2,1,0:T(8,128)S(1)}, u32[]{:S(2)}, u32[]{:S(2)}) collective-permute-start(f32[1,64,128]{2,1,0:T(8,128)S(1)} %get-tuple-element.157), channel_id=1, source_target_pairs={{1,0},{2,1},{3,2},{4,3},{5,4},{6,5},{7,6},{8,7},{9,8},{10,9},{11,1... | collective-permute-start | bytes 98312 | tf_op jit(solution)/shard_map/ppermute | solution.py:26
  49.9 3.1 %collective-permute-done.6 = f32[1,64,128]{2,1,0:T(8,128)S(1)} collective-permute-done((f32[1,64,128]{2,1,0:T(8,128)S(1)}, f32[1,64,128]{2,1,0:T(8,128)S(1)}, u32[]{:S(2)}, u32[]{:S(2)}) %collective-permute-start.6) | collective-permute-done | bytes 32800 | tf_op jit(solution)/shard_map/ppermute | solution.py:26
  53.1 1.0 multiply_add_fusion.5
  54.1 0.2 fusion.11
  54.3 5.4 %collective-permute-start.9 = (f32[1,64,128]{2,1,0:T(8,128)S(1)}, f32[1,64,128]{2,1,0:T(8,128)S(1)}, u32[]{:S(2)}, u32[]{:S(2)}) collective-permute-start(f32[1,64,128]{2,1,0:T(8,128)S(1)} %get-tuple-element.151), channel_id=1, source_target_pairs={{0,1},{1,2},{2,3},{3,4},{4,5},{5,6},{6,7},{7,8},{8,9},{9,10},{10,1... | collective-permute-start | bytes 98312 | tf_op jit(solution)/shard_map/ppermute | solution.py:23
  59.7 1.9 %collective-permute-start.8 = (f32[1,64,128]{2,1,0:T(8,128)S(1)}, f32[1,64,128]{2,1,0:T(8,128)S(1)}, u32[]{:S(2)}, u32[]{:S(2)}) collective-permute-start(f32[1,64,128]{2,1,0:T(8,128)S(1)} %get-tuple-element.152), channel_id=1, source_target_pairs={{1,0},{2,1},{3,2},{4,3},{5,4},{6,5},{7,6},{8,7},{9,8},{10,9},{11,1... | collective-permute-start | bytes 98312 | tf_op jit(solution)/shard_map/ppermute | solution.py:26
  61.7 0.3 add_bitcast_fusion.5
  62.1 5.8 %collective-permute-done.8 = f32[1,64,128]{2,1,0:T(8,128)S(1)} collective-permute-done((f32[1,64,128]{2,1,0:T(8,128)S(1)}, f32[1,64,128]{2,1,0:T(8,128)S(1)}, u32[]{:S(2)}, u32[]{:S(2)}) %collective-permute-start.8) | collective-permute-done | bytes 32800 | tf_op jit(solution)/shard_map/ppermute | solution.py:26
  68.0 0.1 fusion.106
  68.1 1.9 %collective-permute-start.10 = (f32[1,4,8,64,128]{4,3,2,1,0:T(8,128)S(1)}, f32[1,4,8,64,128]{4,3,2,1,0:T(8,128)S(1)}, u32[]{:S(2)}, u32[]{:S(2)}) collective-permute-start(f32[1,4,8,64,128]{4,3,2,1,0:T(8,128)S(1)} %fusion.106), channel_id=1, source_target_pairs={{0,32},{32,64},{64,96},{96,128},{128,160},{160,192},{192,224},{224... | collective-permute-start | bytes 3145736 | tf_op jit(solution)/shard_map/ppermute | solution.py:34
  70.1 16.3 %collective-permute-done.10 = f32[1,4,8,64,128]{4,3,2,1,0:T(8,128)S(1)} collective-permute-done((f32[1,4,8,64,128]{4,3,2,1,0:T(8,128)S(1)}, f32[1,4,8,64,128]{4,3,2,1,0:T(8,128)S(1)}, u32[]{:S(2)}, u32[]{:S(2)}) %collective-permute-start.10) | collective-permute-done | bytes 1048608 | tf_op jit(solution)/shard_map/ppermute | solution.py:34
  86.4 0.1 sub.498
  86.5 1.9 %collective-permute-start.11 = (f32[1,4,8,64,128]{4,3,2,1,0:T(8,128)S(1)}, f32[1,4,8,64,128]{4,3,2,1,0:T(8,128)S(1)}, u32[]{:S(2)}, u32[]{:S(2)}) collective-permute-start(f32[1,4,8,64,128]{4,3,2,1,0:T(8,128)S(1)} %sub.498), channel_id=1, source_target_pairs={{0,480},{32,0},{64,32},{96,64},{128,96},{160,128},{192,160},{224,1... | collective-permute-start | bytes 3145736 | tf_op jit(solution)/shard_map/ppermute | solution.py:34
  88.4 12.3 %collective-permute-done.11 = f32[1,4,8,64,128]{4,3,2,1,0:T(8,128)S(1)} collective-permute-done((f32[1,4,8,64,128]{4,3,2,1,0:T(8,128)S(1)}, f32[1,4,8,64,128]{4,3,2,1,0:T(8,128)S(1)}, u32[]{:S(2)}, u32[]{:S(2)}) %collective-permute-start.11) | collective-permute-done | bytes 1048608 | tf_op jit(solution)/shard_map/ppermute | solution.py:34
  100.8 0.2 fusion.13
  101.0 3.0 %collective-permute-start.13 = (f32[1,64,128]{2,1,0:T(8,128)S(1)}, f32[1,64,128]{2,1,0:T(8,128)S(1)}, u32[]{:S(2)}, u32[]{:S(2)}) collective-permute-start(f32[1,64,128]{2,1,0:T(8,128)S(1)} %get-tuple-element.137), channel_id=1, source_target_pairs={{0,1},{1,2},{2,3},{3,4},{4,5},{5,6},{6,7},{7,8},{8,9},{9,10},{10,1... | collective-permute-start | bytes 98312 | tf_op jit(solution)/shard_map/ppermute | solution.py:23
  104.0 4.4 %collective-permute-start.12 = (f32[1,64,128]{2,1,0:T(8,128)S(1)}, f32[1,64,128]{2,1,0:T(8,128)S(1)}, u32[]{:S(2)}, u32[]{:S(2)}) collective-permute-start(f32[1,64,128]{2,1,0:T(8,128)S(1)} %get-tuple-element.138), channel_id=1, source_target_pairs={{1,0},{2,1},{3,2},{4,3},{5,4},{6,5},{7,6},{8,7},{9,8},{10,9},{11,1... | collective-permute-start | bytes 98312 | tf_op jit(solution)/shard_map/ppermute | solution.py:26
  108.4 0.6 add_bitcast_fusion.1
  109.0 0.1 pad_add_fusion.3
  109.1 4.3 %collective-permute-done.12 = f32[1,64,128]{2,1,0:T(8,128)S(1)} collective-permute-done((f32[1,64,128]{2,1,0:T(8,128)S(1)}, f32[1,64,128]{2,1,0:T(8,128)S(1)}, u32[]{:S(2)}, u32[]{:S(2)}) %collective-permute-start.12) | collective-permute-done | bytes 32800 | tf_op jit(solution)/shard_map/ppermute | solution.py:26
  113.5 0.2 multiply_add_fusion.4
  113.7 0.2 fusion.15
  113.9 5.4 %collective-permute-start.15 = (f32[1,64,128]{2,1,0:T(8,128)S(1)}, f32[1,64,128]{2,1,0:T(8,128)S(1)}, u32[]{:S(2)}, u32[]{:S(2)}) collective-permute-start(f32[1,64,128]{2,1,0:T(8,128)S(1)} %get-tuple-element.149), channel_id=1, source_target_pairs={{0,1},{1,2},{2,3},{3,4},{4,5},{5,6},{6,7},{7,8},{8,9},{9,10},{10,1... | collective-permute-start | bytes 98312 | tf_op jit(solution)/shard_map/ppermute | solution.py:23
  119.4 1.9 %collective-permute-start.14 = (f32[1,64,128]{2,1,0:T(8,128)S(1)}, f32[1,64,128]{2,1,0:T(8,128)S(1)}, u32[]{:S(2)}, u32[]{:S(2)}) collective-permute-start(f32[1,64,128]{2,1,0:T(8,128)S(1)} %get-tuple-element.150), channel_id=1, source_target_pairs={{1,0},{2,1},{3,2},{4,3},{5,4},{6,5},{7,6},{8,7},{9,8},{10,9},{11,1... | collective-permute-start | bytes 98312 | tf_op jit(solution)/shard_map/ppermute | solution.py:26
  121.3 0.5 fusion.146
  121.9 5.7 %collective-permute-done.14 = f32[1,64,128]{2,1,0:T(8,128)S(1)} collective-permute-done((f32[1,64,128]{2,1,0:T(8,128)S(1)}, f32[1,64,128]{2,1,0:T(8,128)S(1)}, u32[]{:S(2)}, u32[]{:S(2)}) %collective-permute-start.14) | collective-permute-done | bytes 32800 | tf_op jit(solution)/shard_map/ppermute | solution.py:26
  127.6 0.2 multiply_add_fusion.3
  127.8 0.7 multiply_add_fusion.2
  128.6 0.2 fusion.17
  128.8 5.4 %collective-permute-start.17 = (f32[1,64,128]{2,1,0:T(8,128)S(1)}, f32[1,64,128]{2,1,0:T(8,128)S(1)}, u32[]{:S(2)}, u32[]{:S(2)}) collective-permute-start(f32[1,64,128]{2,1,0:T(8,128)S(1)} %get-tuple-element.147), channel_id=1, source_target_pairs={{0,1},{1,2},{2,3},{3,4},{4,5},{5,6},{6,7},{7,8},{8,9},{9,10},{10,1... | collective-permute-start | bytes 98312 | tf_op jit(solution)/shard_map/ppermute | solution.py:23
  134.2 1.9 %collective-permute-start.16 = (f32[1,64,128]{2,1,0:T(8,128)S(1)}, f32[1,64,128]{2,1,0:T(8,128)S(1)}, u32[]{:S(2)}, u32[]{:S(2)}) collective-permute-start(f32[1,64,128]{2,1,0:T(8,128)S(1)} %get-tuple-element.148), channel_id=1, source_target_pairs={{1,0},{2,1},{3,2},{4,3},{5,4},{6,5},{7,6},{8,7},{9,8},{10,9},{11,1... | collective-permute-start | bytes 98312 | tf_op jit(solution)/shard_map/ppermute | solution.py:26
  136.2 0.1 pad_add_fusion.1
  136.3 6.2 %collective-permute-done.16 = f32[1,64,128]{2,1,0:T(8,128)S(1)} collective-permute-done((f32[1,64,128]{2,1,0:T(8,128)S(1)}, f32[1,64,128]{2,1,0:T(8,128)S(1)}, u32[]{:S(2)}, u32[]{:S(2)}) %collective-permute-start.16) | collective-permute-done | bytes 32800 | tf_op jit(solution)/shard_map/ppermute | solution.py:26
  142.5 0.2 fusion.139
  142.7 0.5 multiply_add_fusion
  143.2 0.2 fusion.19
  143.4 5.4 %collective-permute-start.19 = (f32[1,64,128]{2,1,0:T(8,128)S(1)}, f32[1,64,128]{2,1,0:T(8,128)S(1)}, u32[]{:S(2)}, u32[]{:S(2)}) collective-permute-start(f32[1,64,128]{2,1,0:T(8,128)S(1)} %get-tuple-element.145), channel_id=1, source_target_pairs={{0,1},{1,2},{2,3},{3,4},{4,5},{5,6},{6,7},{7,8},{8,9},{9,10},{10,1... | collective-permute-start | bytes 98312 | tf_op jit(solution)/shard_map/ppermute | solution.py:23
  148.9 1.9 %collective-permute-start.18 = (f32[1,64,128]{2,1,0:T(8,128)S(1)}, f32[1,64,128]{2,1,0:T(8,128)S(1)}, u32[]{:S(2)}, u32[]{:S(2)}) collective-permute-start(f32[1,64,128]{2,1,0:T(8,128)S(1)} %get-tuple-element.146), channel_id=1, source_target_pairs={{1,0},{2,1},{3,2},{4,3},{5,4},{6,5},{7,6},{8,7},{9,8},{10,9},{11,1... | collective-permute-start | bytes 98312 | tf_op jit(solution)/shard_map/ppermute | solution.py:26
  150.8 0.1 pad_add_fusion
  151.0 6.1 %collective-permute-done.18 = f32[1,64,128]{2,1,0:T(8,128)S(1)} collective-permute-done((f32[1,64,128]{2,1,0:T(8,128)S(1)}, f32[1,64,128]{2,1,0:T(8,128)S(1)}, u32[]{:S(2)}, u32[]{:S(2)}) %collective-permute-start.18) | collective-permute-done | bytes 32800 | tf_op jit(solution)/shard_map/ppermute | solution.py:26
  157.1 0.1 fusion.89
  157.3 1.1 sub.544
  (46 shorter events, 1.0 us)
Async XLA Ops:
  1.4 9.1 %copy-start.4 = (f32[4,3]{1,0:T(4,128)S(1)}, f32[4,3]{1,0:T(4,128)}, u32[]{:S(2)}) copy-start(f32[4,3]{1,0:T(4,128)} %param.25) | copy-start | bytes 148
  1.4 27.0 %collective-permute-start.3 = (f32[1,64,128]{2,1,0:T(8,128)S(1)}, f32[1,64,128]{2,1,0:T(8,128)S(1)}, u32[]{:S(2)}, u32[]{:S(2)}) collective-permute-start(f32[1,64,128]{2,1,0:T(8,128)S(1)} %get-tuple-element.139), channel_id=1, source_target_pairs={{0,1},{1,2},{2,3},{3,4},{4,5},{5,6},{6,7},{7,8},{8,9},{9,10},{10,1... | collective-permute-start | bytes 98312 | tf_op jit(solution)/shard_map/ppermute | solution.py:23
  5.1 23.3 %collective-permute-start.2 = (f32[1,64,128]{2,1,0:T(8,128)S(1)}, f32[1,64,128]{2,1,0:T(8,128)S(1)}, u32[]{:S(2)}, u32[]{:S(2)}) collective-permute-start(f32[1,64,128]{2,1,0:T(8,128)S(1)} %get-tuple-element.140), channel_id=1, source_target_pairs={{1,0},{2,1},{3,2},{4,3},{5,4},{6,5},{7,6},{8,7},{9,8},{10,9},{11,1... | collective-permute-start | bytes 98312 | tf_op jit(solution)/shard_map/ppermute | solution.py:26
  10.5 1.8 %copy-start.3 = (s32[8,64,128]{2,1,0:T(8,128)S(1)}, s32[8,64,128]{2,1,0:T(8,128)}, u32[]{:S(2)}) copy-start(s32[8,64,128]{2,1,0:T(8,128)} %param.23) | copy-start | bytes 786436
  11.2 11.2 %copy-start = (f32[1,4,8,64,128]{4,3,2,1,0:T(8,128)S(1)}, f32[1,4,8,64,128]{4,3,2,1,0:T(8,128)}, u32[]{:S(2)}) copy-start(f32[1,4,8,64,128]{4,3,2,1,0:T(8,128)} %param.21) | copy-start | bytes 3145732
  15.0 13.2 %collective-permute-start = (f32[2,1,64,128]{3,2,1,0:T(8,128)S(1)}, f32[2,1,64,128]{3,2,1,0:T(8,128)S(1)}, u32[]{:S(2)}, u32[]{:S(2)}) collective-permute-start(f32[2,1,64,128]{3,2,1,0:T(8,128)S(1)} %get-tuple-element.143), channel_id=1, source_target_pairs={{0,1},{1,2},{2,3},{3,4},{4,5},{5,6},{6,7},{7,8},{8,9},{9,10},{10,1... | collective-permute-start | bytes 196616 | tf_op jit(solution)/shard_map/ppermute | solution.py:23
  18.0 10.3 %collective-permute-start.1 = (f32[2,1,64,128]{3,2,1,0:T(8,128)S(1)}, f32[2,1,64,128]{3,2,1,0:T(8,128)S(1)}, u32[]{:S(2)}, u32[]{:S(2)}) collective-permute-start(f32[2,1,64,128]{3,2,1,0:T(8,128)S(1)} %get-tuple-element.144), channel_id=1, source_target_pairs={{1,0},{2,1},{3,2},{4,3},{5,4},{6,5},{7,6},{8,7},{9,8},{10,9},{11,1... | collective-permute-start | bytes 196616 | tf_op jit(solution)/shard_map/ppermute | solution.py:26
  28.4 1.0 copy-start.2
  29.6 7.6 %collective-permute-start.5 = (f32[1,64,128]{2,1,0:T(8,128)S(1)}, f32[1,64,128]{2,1,0:T(8,128)S(1)}, u32[]{:S(2)}, u32[]{:S(2)}) collective-permute-start(f32[1,64,128]{2,1,0:T(8,128)S(1)} %get-tuple-element.158), channel_id=1, source_target_pairs={{0,1},{1,2},{2,3},{3,4},{4,5},{5,6},{6,7},{7,8},{8,9},{9,10},{10,1... | collective-permute-start | bytes 98312 | tf_op jit(solution)/shard_map/ppermute | solution.py:23
  33.5 8.2 %collective-permute-start.4 = (f32[1,64,128]{2,1,0:T(8,128)S(1)}, f32[1,64,128]{2,1,0:T(8,128)S(1)}, u32[]{:S(2)}, u32[]{:S(2)}) collective-permute-start(f32[1,64,128]{2,1,0:T(8,128)S(1)} %get-tuple-element.159), channel_id=1, source_target_pairs={{1,0},{2,1},{3,2},{4,3},{5,4},{6,5},{7,6},{8,7},{9,8},{10,9},{11,1... | collective-permute-start | bytes 98312 | tf_op jit(solution)/shard_map/ppermute | solution.py:26
  42.4 7.5 %collective-permute-start.7 = (f32[1,64,128]{2,1,0:T(8,128)S(1)}, f32[1,64,128]{2,1,0:T(8,128)S(1)}, u32[]{:S(2)}, u32[]{:S(2)}) collective-permute-start(f32[1,64,128]{2,1,0:T(8,128)S(1)} %get-tuple-element.156), channel_id=1, source_target_pairs={{0,1},{1,2},{2,3},{3,4},{4,5},{5,6},{6,7},{7,8},{8,9},{9,10},{10,1... | collective-permute-start | bytes 98312 | tf_op jit(solution)/shard_map/ppermute | solution.py:23
  44.8 8.2 %collective-permute-start.6 = (f32[1,64,128]{2,1,0:T(8,128)S(1)}, f32[1,64,128]{2,1,0:T(8,128)S(1)}, u32[]{:S(2)}, u32[]{:S(2)}) collective-permute-start(f32[1,64,128]{2,1,0:T(8,128)S(1)} %get-tuple-element.157), channel_id=1, source_target_pairs={{1,0},{2,1},{3,2},{4,3},{5,4},{6,5},{7,6},{8,7},{9,8},{10,9},{11,1... | collective-permute-start | bytes 98312 | tf_op jit(solution)/shard_map/ppermute | solution.py:26
  54.3 7.8 %collective-permute-start.9 = (f32[1,64,128]{2,1,0:T(8,128)S(1)}, f32[1,64,128]{2,1,0:T(8,128)S(1)}, u32[]{:S(2)}, u32[]{:S(2)}) collective-permute-start(f32[1,64,128]{2,1,0:T(8,128)S(1)} %get-tuple-element.151), channel_id=1, source_target_pairs={{0,1},{1,2},{2,3},{3,4},{4,5},{5,6},{6,7},{7,8},{8,9},{9,10},{10,1... | collective-permute-start | bytes 98312 | tf_op jit(solution)/shard_map/ppermute | solution.py:23
  59.7 8.2 %collective-permute-start.8 = (f32[1,64,128]{2,1,0:T(8,128)S(1)}, f32[1,64,128]{2,1,0:T(8,128)S(1)}, u32[]{:S(2)}, u32[]{:S(2)}) collective-permute-start(f32[1,64,128]{2,1,0:T(8,128)S(1)} %get-tuple-element.152), channel_id=1, source_target_pairs={{1,0},{2,1},{3,2},{4,3},{5,4},{6,5},{7,6},{8,7},{9,8},{10,9},{11,1... | collective-permute-start | bytes 98312 | tf_op jit(solution)/shard_map/ppermute | solution.py:26
  68.1 18.2 %collective-permute-start.10 = (f32[1,4,8,64,128]{4,3,2,1,0:T(8,128)S(1)}, f32[1,4,8,64,128]{4,3,2,1,0:T(8,128)S(1)}, u32[]{:S(2)}, u32[]{:S(2)}) collective-permute-start(f32[1,4,8,64,128]{4,3,2,1,0:T(8,128)S(1)} %fusion.106), channel_id=1, source_target_pairs={{0,32},{32,64},{64,96},{96,128},{128,160},{160,192},{192,224},{224... | collective-permute-start | bytes 3145736 | tf_op jit(solution)/shard_map/ppermute | solution.py:34
  86.5 70.8 %copy-start.1 = (f32[1,4,8,64,128]{4,3,2,1,0:T(8,128)}, f32[1,4,8,64,128]{4,3,2,1,0:T(8,128)S(1)}, u32[]{:S(2)}) copy-start(f32[1,4,8,64,128]{4,3,2,1,0:T(8,128)S(1)} %sub.498) | copy-start | bytes 3145732
  86.5 14.2 %collective-permute-start.11 = (f32[1,4,8,64,128]{4,3,2,1,0:T(8,128)S(1)}, f32[1,4,8,64,128]{4,3,2,1,0:T(8,128)S(1)}, u32[]{:S(2)}, u32[]{:S(2)}) collective-permute-start(f32[1,4,8,64,128]{4,3,2,1,0:T(8,128)S(1)} %sub.498), channel_id=1, source_target_pairs={{0,480},{32,0},{64,32},{96,64},{128,96},{160,128},{192,160},{224,1... | collective-permute-start | bytes 3145736 | tf_op jit(solution)/shard_map/ppermute | solution.py:34
  101.0 8.1 %collective-permute-start.13 = (f32[1,64,128]{2,1,0:T(8,128)S(1)}, f32[1,64,128]{2,1,0:T(8,128)S(1)}, u32[]{:S(2)}, u32[]{:S(2)}) collective-permute-start(f32[1,64,128]{2,1,0:T(8,128)S(1)} %get-tuple-element.137), channel_id=1, source_target_pairs={{0,1},{1,2},{2,3},{3,4},{4,5},{5,6},{6,7},{7,8},{8,9},{9,10},{10,1... | collective-permute-start | bytes 98312 | tf_op jit(solution)/shard_map/ppermute | solution.py:23
  104.0 9.4 %collective-permute-start.12 = (f32[1,64,128]{2,1,0:T(8,128)S(1)}, f32[1,64,128]{2,1,0:T(8,128)S(1)}, u32[]{:S(2)}, u32[]{:S(2)}) collective-permute-start(f32[1,64,128]{2,1,0:T(8,128)S(1)} %get-tuple-element.138), channel_id=1, source_target_pairs={{1,0},{2,1},{3,2},{4,3},{5,4},{6,5},{7,6},{8,7},{9,8},{10,9},{11,1... | collective-permute-start | bytes 98312 | tf_op jit(solution)/shard_map/ppermute | solution.py:26
  113.9 8.0 %collective-permute-start.15 = (f32[1,64,128]{2,1,0:T(8,128)S(1)}, f32[1,64,128]{2,1,0:T(8,128)S(1)}, u32[]{:S(2)}, u32[]{:S(2)}) collective-permute-start(f32[1,64,128]{2,1,0:T(8,128)S(1)} %get-tuple-element.149), channel_id=1, source_target_pairs={{0,1},{1,2},{2,3},{3,4},{4,5},{5,6},{6,7},{7,8},{8,9},{9,10},{10,1... | collective-permute-start | bytes 98312 | tf_op jit(solution)/shard_map/ppermute | solution.py:23
  119.4 8.2 %collective-permute-start.14 = (f32[1,64,128]{2,1,0:T(8,128)S(1)}, f32[1,64,128]{2,1,0:T(8,128)S(1)}, u32[]{:S(2)}, u32[]{:S(2)}) collective-permute-start(f32[1,64,128]{2,1,0:T(8,128)S(1)} %get-tuple-element.150), channel_id=1, source_target_pairs={{1,0},{2,1},{3,2},{4,3},{5,4},{6,5},{7,6},{8,7},{9,8},{10,9},{11,1... | collective-permute-start | bytes 98312 | tf_op jit(solution)/shard_map/ppermute | solution.py:26
  128.8 7.5 %collective-permute-start.17 = (f32[1,64,128]{2,1,0:T(8,128)S(1)}, f32[1,64,128]{2,1,0:T(8,128)S(1)}, u32[]{:S(2)}, u32[]{:S(2)}) collective-permute-start(f32[1,64,128]{2,1,0:T(8,128)S(1)} %get-tuple-element.147), channel_id=1, source_target_pairs={{0,1},{1,2},{2,3},{3,4},{4,5},{5,6},{6,7},{7,8},{8,9},{9,10},{10,1... | collective-permute-start | bytes 98312 | tf_op jit(solution)/shard_map/ppermute | solution.py:23
  134.2 8.2 %collective-permute-start.16 = (f32[1,64,128]{2,1,0:T(8,128)S(1)}, f32[1,64,128]{2,1,0:T(8,128)S(1)}, u32[]{:S(2)}, u32[]{:S(2)}) collective-permute-start(f32[1,64,128]{2,1,0:T(8,128)S(1)} %get-tuple-element.148), channel_id=1, source_target_pairs={{1,0},{2,1},{3,2},{4,3},{5,4},{6,5},{7,6},{8,7},{9,8},{10,9},{11,1... | collective-permute-start | bytes 98312 | tf_op jit(solution)/shard_map/ppermute | solution.py:26
  143.4 7.5 %collective-permute-start.19 = (f32[1,64,128]{2,1,0:T(8,128)S(1)}, f32[1,64,128]{2,1,0:T(8,128)S(1)}, u32[]{:S(2)}, u32[]{:S(2)}) collective-permute-start(f32[1,64,128]{2,1,0:T(8,128)S(1)} %get-tuple-element.145), channel_id=1, source_target_pairs={{0,1},{1,2},{2,3},{3,4},{4,5},{5,6},{6,7},{7,8},{8,9},{9,10},{10,1... | collective-permute-start | bytes 98312 | tf_op jit(solution)/shard_map/ppermute | solution.py:23
  148.9 8.2 %collective-permute-start.18 = (f32[1,64,128]{2,1,0:T(8,128)S(1)}, f32[1,64,128]{2,1,0:T(8,128)S(1)}, u32[]{:S(2)}, u32[]{:S(2)}) collective-permute-start(f32[1,64,128]{2,1,0:T(8,128)S(1)} %get-tuple-element.146), channel_id=1, source_target_pairs={{1,0},{2,1},{3,2},{4,3},{5,4},{6,5},{7,6},{8,7},{9,8},{10,9},{11,1... | collective-permute-start | bytes 98312 | tf_op jit(solution)/shard_map/ppermute | solution.py:26
where the time goes:
time: 159 us; the launch traced here: 158 us
  starting transfers between devices  71.6 us (45%)
  waiting for transfers between devices  64.4 us (41%)
  other arithmetic  18.8 us (12%)
  local copies, waits for them, and re-layouts  2.4 us (2%)
    ppermute x9, starting transfers between devices, padded_2(): lax.ppermute(lax.slice_in_dim(block, block.shape[dim] - width, None, axis...  37.5 us
    ppermute x9, waiting for transfers between devices, padded_2(): lax.ppermute(lax.slice_in_dim(block, 0, width, axis=dim), axis, backward)  35.7 us
    ppermute x9, starting transfers between devices, padded_2(): lax.ppermute(lax.slice_in_dim(block, 0, width, axis=dim), axis, backward)  30.3 us
    ppermute x2, waiting for transfers between devices, passed_along(): return lax.ppermute(value, axis, pairs)  28.6 us
    add x1, other arithmetic, conductivity(): summed + jnp.where(fibers == class_index, conductances[class_index, axis_...  5.19 us
    ppermute x2, starting transfers between devices, passed_along(): return lax.ppermute(value, axis, pairs)  3.84 us
    another operation x2, other arithmetic, body(): jnp.stack([conductivity(fibers, conductances, 0), share])  3.82 us
  transfers between devices with their start and end apart: 20, of which 10 were waited for; matrix products, arithmetic and copies ran while one was open for 8% of the time, Pallas kernels for 0%

commit v1 on v0

v1 whole, which is shorter than its diff:
```python
import functools

import jax
import jax.numpy as jnp
from jax import lax
from jax.experimental import pallas as pl
from jax.experimental.pallas import tpu as pltpu
from jax.sharding import PartitionSpec as P

DEEP = 8
NX = 64
NY = 128
V0, P1, G1, G2, G3, Q2, Q3, FIB, TIS, WIN = range(10)
C_W01, C_WIN, C_WX, C_WY, C_D2, C_E, C_D1 = range(7)
HALF_STEP = 0.15 * 0.5


def ahead(plane, axis):
    return pltpu.roll(plane, plane.shape[axis] - 1, axis)


def behind(plane, axis):
    return pltpu.roll(plane, 1, axis)


def sigma(cond, fiber, direction):
    summed = jnp.zeros(fiber.shape, jnp.float32)
    for c in range(4):
        summed = jnp.where(fiber == c, cond[c, direction], summed)
    return summed


def cross_weight(sig, share, axis):
    place = lax.broadcasted_iota(jnp.int32, sig.shape, axis)
    inner = jnp.where(place < sig.shape[axis] - 1, HALF_STEP, 0.0)
    return inner * (sig + ahead(sig, axis)) * (share * ahead(share, axis))


def face_weight(sig_a, share_a, sig_b, share_b):
    return HALF_STEP * (sig_a + sig_b) * (share_a * share_b)


def cross(v, wx, wy):
    fx = wx * (ahead(v, 0) - v)
    fy = wy * (ahead(v, 1) - v)
    return (fx - behind(fx, 0)) + (fy - behind(fy, 1))


def reaction(v, g1, g2, g3):
    return 0.3 * (g1 * g2) * (1.0 - v) - 0.15 * g3 * v


def tanhs(v):
    return jnp.tanh(4.0 * v - 0.8), jnp.tanh(2.0 - 4.0 * v), jnp.tanh(4.0 * v - 3.2)


def gates_next(v, g1, g2, g3):
    t1, t2, t3 = tanhs(v)
    return (
        0.7 * g1 + (0.15 + 0.15 * t1),
        0.9 * g2 + (0.05 + 0.05 * t2),
        0.97 * g3 + (0.015 + 0.015 * t3),
    )


def edge_kernel(cond, flag, starts, tissue, fibers, pacing, up, down):
    for out, (b1, b2, b3, b4) in ((up, (7, 6, 5, 4)), (down, (0, 1, 2, 3))):
        share = [tissue[b].astype(jnp.float32) for b in (b1, b2, b3, b4)]
        sig0 = [sigma(cond, fibers[b], 0) for b in (b1, b2, b3, b4)]
        wz = [face_weight(sig0[i], share[i], sig0[i + 1], share[i + 1]) for i in range(3)]
        wx = [cross_weight(sigma(cond, fibers[b], 1), share[i], 0) for i, b in enumerate((b1, b2, b3))]
        wy = [cross_weight(sigma(cond, fibers[b], 2), share[i], 1) for i, b in enumerate((b1, b2, b3))]
        stim = [(0.6 * flag[0]) * pacing[b].astype(jnp.float32) for b in (b1, b2, b3)]
        v = [starts[0, 0, b] for b in (b1, b2, b3, b4)]
        g = [[starts[0, n, b] for n in (1, 2, 3)] for b in (b1, b2, b3)]

        def own_step(i):
            total = v[i] + cross(v[i], wx[i], wy[i]) + reaction(v[i], *g[i]) + stim[i]
            total = total + wz[i] * (v[i + 1] - v[i])
            return total if i == 0 else total + wz[i - 1] * (v[i - 1] - v[i])

        out[V0] = v[0]
        out[P1] = own_step(0)
        gates = gates_next(v[0], *g[0])
        for n in range(3):
            out[G1 + n] = gates[n]
        v1_b2 = own_step(1)
        v1_b3 = own_step(2)
        out[Q2] = wz[0] * v1_b2 + stim[0]
        rest = v1_b2 + cross(v1_b2, wx[1], wy[1]) + reaction(v1_b2, *gates_next(v[1], *g[1])) + stim[1]
        rest = rest + wz[1] * (v1_b3 - v1_b2) - wz[0] * v1_b2
        out[Q3] = wz[0] * rest + stim[0]
        out[FIB] = fibers[b1].astype(jnp.float32)
        out[TIS] = share[0]
        out[WIN] = wz[0]


def weight_kernel(cond, tissue, fibers, gate, wx, wy, wz):
    before = None
    for i in range(DEEP):
        share = tissue[i].astype(jnp.float32)
        sig0 = sigma(cond, fibers[i], 0)
        wx[i] = cross_weight(sigma(cond, fibers[i], 1), share, 0)
        wy[i] = cross_weight(sigma(cond, fibers[i], 2), share, 1)
        if i:
            wz[i - 1] = face_weight(*before, sig0, share)
        before = (sig0, share)


def forward_kernel(cond, flag, starts, tissue, fibers, pacing, wx, wy, wz, low, high, ends, hist, side):
    halo = []
    for n, (msg, own) in enumerate(((low, 0), (high, DEEP - 1))):
        fib, tis = msg[FIB], msg[TIS]
        w01 = face_weight(sigma(cond, fib, 0), tis, sigma(cond, fibers[own], 0), tissue[own].astype(jnp.float32))
        side[n, C_W01] = w01
        side[n, C_WIN] = msg[WIN]
        side[n, C_WX] = cross_weight(sigma(cond, fib, 1), tis, 0)
        side[n, C_WY] = cross_weight(sigma(cond, fib, 2), tis, 1)
        halo.append(msg[V0])
    old = starts.at[0]
    for step in range(4):
        new = hist.at[step] if step < 3 else ends
        below = side[0, C_W01] * (old[0, 0] - halo[0])
        first_flux = below
        for i in range(DEEP):
            v = old[0, i]
            g = [old[n, i] for n in (1, 2, 3)]
            if i < DEEP - 1:
                above = wz[i] * (old[0, i + 1] - v)
            else:
                above = side[1, C_W01] * (halo[1] - v)
                last_flux = above
            total = v + (above - below) + cross(v, wx[i], wy[i]) + reaction(v, *g)
            new[0, i] = total + (0.6 * flag[0]) * pacing[i].astype(jnp.float32)
            for n, gate in enumerate(gates_next(v, *g)):
                new[n + 1, i] = gate
            below = above
        if step < 3:
            for n, msg in enumerate((low, high)):
                inflow = first_flux if n == 0 else -last_flux
                if step == 0:
                    halo[n] = msg[P1] + inflow
                    side[n, C_D1] = halo[n]
                    continue
                v = halo[n]
                win = side[n, C_WIN]
                g = [msg[G1], msg[G2], msg[G3]]
                if step == 1:
                    extra = msg[Q2]
                else:
                    v1 = side[n, C_D1]
                    g1 = g
                    g = gates_next(v1, *g1)
                    extra = msg[Q3] + win * win * v1
                    t1, t2, t3 = tanhs(v1)
                    side[n, C_D2] = -0.3 * (g[0] * g[1]) - 0.15 * g[2]
                    side[n, C_D1] = -0.3 * (g1[0] * g1[1]) - 0.15 * g1[2]
                    side[n, C_E] = (
                        0.6 * (1.0 - t1 * t1) * (0.3 * g[1] * (1.0 - v))
                        - 0.2 * (1.0 - t2 * t2) * (0.3 * g[0] * (1.0 - v))
                        - 0.06 * (1.0 - t3 * t3) * (0.15 * v)
                    )
                total = v + cross(v, side[n, C_WX], side[n, C_WY]) + reaction(v, *g)
                halo[n] = total + (extra - win * v) + inflow
        old = new


def pull_gates(a, g, v):
    av, a1, a2, a3 = a
    rest = 0.3 * (1.0 - v) * av
    return 0.7 * a1 + g[1] * rest, 0.9 * a2 + g[0] * rest, 0.97 * a3 - 0.15 * v * av


def pull_voltage(a, g, v):
    av, a1, a2, a3 = a
    t1, t2, t3 = tanhs(v)
    total = av * (1.0 - 0.3 * (g[0] * g[1]) - 0.15 * g[2])
    total = total + 0.6 * (1.0 - t1 * t1) * a1 - 0.2 * (1.0 - t2 * t2) * a2
    return total + 0.06 * (1.0 - t3 * t3) * a3


def send_kernel(ends, following, hist, wx, wy, wz, gap, up, down):
    for n in range(4):
        for i in range(DEEP):
            gap[n, i] = ends[n, i] - following[0, n, i]
    for out, (b1, sign) in ((up, (7, -1)), (down, (0, 1))):
        layers = [b1 + sign * d for d in range(4)]
        a = [[gap[n, b] for n in range(4)] for b in layers]
        out[0] = a[0][0]
        for m in range(3):
            fields = hist.at[2 - m]
            fresh = []
            outer = None
            for d in range(3 - m):
                b = layers[d]
                v = fields[0, b]
                g = [fields[n, b] for n in (1, 2, 3)]
                face = wz[b - 1] if sign < 0 else wz[b]
                inner = face * (a[d + 1][0] - a[d][0])
                total = pull_voltage(a[d], g, v) + cross(a[d][0], wx[b], wy[b]) + inner
                if outer is not None:
                    total = total - outer
                fresh.append([total, *pull_gates(a[d], g, v)])
                outer = inner
            a = fresh
            out[m + 1] = a[0][0]


def pull_kernel(starts, hist, gap, wx, wy, wz, side, low, high, out, work):
    halo = [low[0], high[0]]
    first = [None, None]
    old = gap
    for m in range(4):
        fields = hist.at[2 - m] if m < 3 else starts.at[0]
        new = out if m == 3 else work.at[m % 2]
        below = side[0, C_W01] * (old[0, 0] - halo[0])
        first_flux = below
        for i in range(DEEP):
            a = [old[n, i] for n in range(4)]
            v = fields[0, i]
            g = [fields[n, i] for n in (1, 2, 3)]
            if i < DEEP - 1:
                above = wz[i] * (old[0, i + 1] - a[0])
            else:
                above = side[1, C_W01] * (halo[1] - a[0])
                last_flux = above
            new[0, i] = pull_voltage(a, g, v) + (above - below) + cross(a[0], wx[i], wy[i])
            for n, gate in enumerate(pull_gates(a, g, v)):
                new[n + 1, i] = gate
            below = above
        if m < 3:
            for n, msg in enumerate((low, high)):
                inflow = first_flux if n == 0 else -last_flux
                win, px, py = side[n, C_WIN], side[n, C_WX], side[n, C_WY]
                if m == 0:
                    change = inflow
                    first[n] = inflow
                elif m == 1:
                    d = first[n]
                    change = d + cross(d, px, py) + (side[n, C_D2] - win) * d + inflow
                    second = change
                else:
                    d, d1 = last[n], first[n]
                    change = d + cross(d, px, py) + (side[n, C_D1] - win) * d + inflow
                    change = change + (win * win + side[n, C_E]) * d1
                halo[n] = msg[m + 1] + change
                if n == 0:
                    changes = [change]
                else:
                    changes.append(change)
            last = changes
        old = new


VM = pl.BlockSpec(memory_space=pltpu.VMEM)
SM = pl.BlockSpec(memory_space=pltpu.SMEM)


def f32(*shape):
    return jax.ShapeDtypeStruct(shape, jnp.float32)


def call(kernel, name, ins, outs, scratch=()):
    return pl.pallas_call(
        kernel,
        name=name,
        in_specs=ins,
        out_specs=[VM] * len(outs),
        out_shape=outs,
        scratch_shapes=list(scratch),
        compiler_params=pltpu.CompilerParams(vmem_limit_bytes=48 * 1024 * 1024),
    )


def body(starts, tissue, fibers, pacing, conductances):
    plane = (NX, NY)
    slabs = lax.axis_size("slab")
    sections = lax.axis_size("tm")
    upward = [(i, i + 1) for i in range(slabs - 1)]
    downward = [(i + 1, i) for i in range(slabs - 1)]
    earlier = [((i + 1) % sections, i) for i in range(sections)]
    later = [(i, (i + 1) % sections) for i in range(sections)]
    flag = (lax.axis_index("tm") == 0).astype(jnp.float32).reshape(1)

    up, down = call(edge_kernel, "edge", [SM, SM] + [VM] * 4, [f32(10, *plane)] * 2)(
        conductances, flag, starts, tissue, fibers, pacing
    )
    low = lax.ppermute(up, "slab", upward)
    high = lax.ppermute(down, "slab", downward)
    following = lax.ppermute(starts, "tm", earlier)
    wx, wy, wz = call(
        weight_kernel,
        "weight",
        [SM, VM, VM, pl.BlockSpec(memory_space=pl.ANY)],
        [f32(DEEP, *plane), f32(DEEP, *plane), f32(DEEP - 1, *plane)],
    )(conductances, tissue, fibers, up)
    ends, hist, side = call(
        forward_kernel,
        "forward",
        [SM, SM] + [VM] * 9,
        [f32(4, DEEP, *plane), f32(3, 4, DEEP, *plane), f32(2, 7, *plane)],
    )(conductances, flag, starts, tissue, fibers, pacing, wx, wy, wz, low, high)
    gap, up, down = call(
        send_kernel,
        "send",
        [VM] * 6,
        [f32(4, DEEP, *plane), f32(4, *plane), f32(4, *plane)],
    )(ends, following, hist, wx, wy, wz)
    low = lax.ppermute(up, "slab", upward)
    high = lax.ppermute(down, "slab", downward)
    defect = lax.ppermute(gap[None], "tm", later)
    pulled = call(
        pull_kernel,
        "pull",
        [VM] * 9,
        [f32(4, DEEP, *plane)],
        [pltpu.VMEM((2, 4, DEEP, *plane), jnp.float32)],
    )(starts, hist, gap, wx, wy, wz, side, low, high)[0]
    return defect, pulled[None] - defect


def solution(mesh):
    spread = P("tm", None, "slab", None, None)
    placed = (spread, P("slab", None, None), P("slab", None, None), P("slab", None, None), P())
    return jax.shard_map(body, mesh=mesh, in_specs=placed, out_specs=(spread, spread), check_vma=False)
```

time: 159 us -> 73.3 us (0.46)
  the two profiles are of different devices: /device:TPU:16 before, /device:TPU:127 now
where the time goes in v1:
time: 73.3 us; the launch traced here: 72.7 us
  starting transfers between devices  24.3 us (33%)
  waiting for transfers between devices  23.1 us (32%)
  Pallas kernels  13.9 us (19%)
  local copies, waits for them, and re-layouts  9.52 us (13%)
  other arithmetic  1.15 us (2%)
  between operations  0.74 us (1%)
    ppermute x2, waiting for transfers between devices, body(): low = lax.ppermute(up, 'slab', upward)  17.4 us
    ppermute x2, starting transfers between devices, body(): low = lax.ppermute(up, 'slab', upward)  13.7 us
    unnamed x21, local copies, waits for them, and re-layouts  9.52 us
    ppermute x2, waiting for transfers between devices, body(): high = lax.ppermute(down, 'slab', downward)  5.71 us
    ppermute x2, starting transfers between devices, body(): high = lax.ppermute(down, 'slab', downward)  4.78 us
    pallas_call x1, Pallas kernels, body(): call(forward_kernel, 'forward', [SM, SM] + [VM] * 9, [f32(4, DEEP, *plane...  4.7 us
    pallas_call x1, Pallas kernels, body(): call(pull_kernel, 'pull', [VM] * 9, [f32(4, DEEP, *plane)], [pltpu.VMEM((...  4.27 us
    ppermute x1, starting transfers between devices, body(): defect = lax.ppermute(gap[None], 'tm', later)  3.23 us
  transfers between devices with their start and end apart: 6, of which 3 were waited for; matrix products, arithmetic and copies ran while one was open for 0% of the time, Pallas kernels for 15%

profile of v1, /device:TPU:127, one launch (start us, length us, event | category | flops | bytes accessed | tf_op | source)
XLA Modules:
  0.0 72.7 jit_solution(17175845734921323846)
XLA Ops:
  0.6 2.6 %collective-permute-start.2 = (f32[1,4,8,64,128]{4,3,2,1,0:T(8,128)}, f32[1,4,8,64,128]{4,3,2,1,0:T(8,128)S(1)}, u32[]{:S(2)}, u32[]{:S(2)}) collective-permute-start(f32[1,4,8,64,128]{4,3,2,1,0:T(8,128)} %starts.5), channel_id=1, source_target_pairs={{32,0},{64,32},{96,64},{128,96},{160,128},{192,160},{224,192},{256... | collective-permute-start | bytes 3145736 | tf_op jit(solution)/shard_map/ppermute | solution.py:290
  3.2 0.0 copy-start
  3.2 1.2 %copy-done = f32[1,4,8,64,128]{4,3,2,1,0:T(8,128)S(1)} copy-done((f32[1,4,8,64,128]{4,3,2,1,0:T(8,128)S(1)}, f32[1,4,8,64,128]{4,3,2,1,0:T(8,128)}, u32[]{:S(2)}) %copy-start) | copy-done | bytes 1048600
  4.5 0.0 copy-start.2
  4.5 0.9 %copy-done.2 = s32[8,64,128]{2,1,0:T(8,128)S(1)} copy-done((s32[8,64,128]{2,1,0:T(8,128)S(1)}, s32[8,64,128]{2,1,0:T(8,128)}, u32[]{:S(2)}) %copy-start.2) | copy-done | bytes 262168
  5.4 0.0 copy-start.5
  5.4 0.9 %copy-done.5 = s32[8,64,128]{2,1,0:T(8,128)S(1)} copy-done((s32[8,64,128]{2,1,0:T(8,128)S(1)}, s32[8,64,128]{2,1,0:T(8,128)}, u32[]{:S(2)}) %copy-start.5) | copy-done | bytes 262168
  6.4 0.0 copy-start.8
  6.4 0.9 %copy-done.8 = s32[8,64,128]{2,1,0:T(8,128)S(1)} copy-done((s32[8,64,128]{2,1,0:T(8,128)S(1)}, s32[8,64,128]{2,1,0:T(8,128)}, u32[]{:S(2)}) %copy-start.8) | copy-done | bytes 262168
  7.3 0.0 copy-start.9
  7.3 0.7 copy-done.9
  8.0 0.0 copy-start.1
  8.0 1.2 %edge.1 = (f32[10,64,128]{2,1,0:T(8,128)S(1)}, f32[10,64,128]{2,1,0:T(8,128)S(1)}) custom-call(f32[4,3]{1,0:T(4,128)S(1)} %copy-done.9, f32[1]{0:T(128)} %bitcast.flag, f32[1,4,8,64,128]{4,3,2,1,0:T(8,128)S(1)} %copy-done, s32[8,64,128]{2,1,0:T(8,128)S(1)} %copy-done.2, s32[8,64,128]{2,1,0:T(8,128)S(1)} %copy-done.5, s32[8,64,128]{2,1,0:T(8,128)S(1)} %copy-done.8), custom_call_target="tpu_custom_call" | custom-call | tf_op jit(solution)/shard_map/edge/pallas_call | solution.py:285
  9.2 2.9 %collective-permute-start.1 = (f32[10,64,128]{2,1,0:T(8,128)S(1)}, f32[10,64,128]{2,1,0:T(8,128)S(1)}, u32[]{:S(2)}, u32[]{:S(2)}) collective-permute-start(f32[10,64,128]{2,1,0:T(8,128)S(1)} %get-tuple-element.17), channel_id=1, source_target_pairs={{1,0},{2,1},{3,2},{4,3},{5,4},{6,5},{7,6},{8,7},{9,8},{10,9},{11,1... | collective-permute-start | bytes 983048 | tf_op jit(solution)/shard_map/ppermute | solution.py:289
  12.1 6.0 %collective-permute-start = (f32[10,64,128]{2,1,0:T(8,128)S(1)}, f32[10,64,128]{2,1,0:T(8,128)S(1)}, u32[]{:S(2)}, u32[]{:S(2)}) collective-permute-start(f32[10,64,128]{2,1,0:T(8,128)S(1)} %get-tuple-element.13.gate), channel_id=1, source_target_pairs={{0,1},{1,2},{2,3},{3,4},{4,5},{5,6},{6,7},{7,8},{8,9},{9,10},{10,1... | collective-permute-start | bytes 983048 | tf_op jit(solution)/shard_map/ppermute | solution.py:288
  18.1 0.0 copy-start.3
  18.2 0.9 %copy-done.3 = s32[8,64,128]{2,1,0:T(8,128)S(1)} copy-done((s32[8,64,128]{2,1,0:T(8,128)S(1)}, s32[8,64,128]{2,1,0:T(8,128)}, u32[]{:S(2)}) %copy-start.3) | copy-done | bytes 262168
  19.1 0.0 copy-start.6
  19.1 0.9 %copy-done.6 = s32[8,64,128]{2,1,0:T(8,128)S(1)} copy-done((s32[8,64,128]{2,1,0:T(8,128)S(1)}, s32[8,64,128]{2,1,0:T(8,128)}, u32[]{:S(2)}) %copy-start.6) | copy-done | bytes 262168
  20.0 0.9 %weight.1 = (f32[8,64,128]{2,1,0:T(8,128)S(1)}, f32[8,64,128]{2,1,0:T(8,128)S(1)}, f32[7,64,128]{2,1,0:T(8,128)S(1)}) custom-call(f32[4,3]{1,0:T(4,128)S(1)} %copy-done.9, s32[8,64,128]{2,1,0:T(8,128)S(1)} %copy-done.3, s32[8,64,128]{2,1,0:T(8,128)S(1)} %copy-done.6, f32[10,64,128]{2,1,0:T(8,128)S(1)} %get-tuple-element.13.gate), custom_call_target="tpu_custom_call" | custom-call | tf_op jit(solution)/shard_map/weight/pallas_call | solution.py:291
  21.0 5.7 %collective-permute-done.1.high = f32[10,64,128]{2,1,0:T(8,128)S(1)} collective-permute-done((f32[10,64,128]{2,1,0:T(8,128)S(1)}, f32[10,64,128]{2,1,0:T(8,128)S(1)}, u32[]{:S(2)}, u32[]{:S(2)}) %collective-permute-start.1) | collective-permute-done | bytes 327712 | tf_op jit(solution)/shard_map/ppermute | solution.py:289
  26.7 4.7 %collective-permute-done.low = f32[10,64,128]{2,1,0:T(8,128)S(1)} collective-permute-done((f32[10,64,128]{2,1,0:T(8,128)S(1)}, f32[10,64,128]{2,1,0:T(8,128)S(1)}, u32[]{:S(2)}, u32[]{:S(2)}) %collective-permute-start) | collective-permute-done | bytes 327712 | tf_op jit(solution)/shard_map/ppermute | solution.py:288
  31.4 0.0 copy-done.1
  31.4 0.0 copy-start.4
  31.4 0.9 %copy-done.4 = s32[8,64,128]{2,1,0:T(8,128)S(1)} copy-done((s32[8,64,128]{2,1,0:T(8,128)S(1)}, s32[8,64,128]{2,1,0:T(8,128)}, u32[]{:S(2)}) %copy-start.4) | copy-done | bytes 262168
  32.4 0.0 copy-start.7
  32.4 0.9 %copy-done.7 = s32[8,64,128]{2,1,0:T(8,128)S(1)} copy-done((s32[8,64,128]{2,1,0:T(8,128)S(1)}, s32[8,64,128]{2,1,0:T(8,128)}, u32[]{:S(2)}) %copy-start.7) | copy-done | bytes 262168
  33.3 4.7 %forward.1 = (f32[4,8,64,128]{3,2,1,0:T(8,128)S(1)}, f32[3,4,8,64,128]{4,3,2,1,0:T(8,128)}, f32[2,7,64,128]{3,2,1,0:T(8,128)S(1)}) custom-call(f32[4,3]{1,0:T(4,128)S(1)} %copy-done.9, f32[1]{0:T(128)} %bitcast.flag, f32[1,4,8,64,128]{4,3,2,1,0:T(8,128)S(1)} %copy-done.1, s32[8,64,128]{2,1,0:T(8,128)S(1)} %copy-done.4, s32[8,64,128]{2,1,0:T(8,128)S(1)} %copy-done.7, ...), custom_call_target="tpu_custom_call" | custom-call | tf_op jit(solution)/shard_map/forward/pallas_call | solution.py:297
  38.0 0.0 collective-permute-done.2.following
  38.0 2.7 %send.1 = (f32[4,8,64,128]{3,2,1,0:T(8,128)S(1)}, f32[4,64,128]{2,1,0:T(8,128)S(1)}, f32[4,64,128]{2,1,0:T(8,128)S(1)}) custom-call(f32[4,8,64,128]{3,2,1,0:T(8,128)S(1)} %get-tuple-element.18.ends, f32[1,4,8,64,128]{4,3,2,1,0:T(8,128)S(1)} %collective-permute-done.2.following, f32[3,4,8,64,128]{4,3,2,1,0:T(8,128)} %get-tuple-element.19.hist, ...), custom_call_target="tpu_custom_call" | custom-call | tf_op jit(solution)/shard_map/send/pallas_call | solution.py:303
  40.7 3.2 %collective-permute-start.3 = (f32[1,4,8,64,128]{4,3,2,1,0:T(8,128)S(1)}, f32[1,4,8,64,128]{4,3,2,1,0:T(8,128)S(1)}, u32[]{:S(2)}, u32[]{:S(2)}) collective-permute-start(f32[1,4,8,64,128]{4,3,2,1,0:T(8,128)S(1)} %bitcast.4), channel_id=1, source_target_pairs={{0,32},{32,64},{64,96},{96,128},{128,160},{160,192},{192,224},{224... | collective-permute-start | bytes 3145736 | tf_op jit(solution)/shard_map/ppermute | solution.py:311
  44.0 7.7 %collective-permute-start.4 = (f32[4,64,128]{2,1,0:T(8,128)S(1)}, f32[4,64,128]{2,1,0:T(8,128)S(1)}, u32[]{:S(2)}, u32[]{:S(2)}) collective-permute-start(f32[4,64,128]{2,1,0:T(8,128)S(1)} %get-tuple-element.22), channel_id=1, source_target_pairs={{0,1},{1,2},{2,3},{3,4},{4,5},{5,6},{6,7},{7,8},{8,9},{9,10},{10,1... | collective-permute-start | bytes 393224 | tf_op jit(solution)/shard_map/ppermute | solution.py:309
  51.7 1.9 %collective-permute-start.5 = (f32[4,64,128]{2,1,0:T(8,128)S(1)}, f32[4,64,128]{2,1,0:T(8,128)S(1)}, u32[]{:S(2)}, u32[]{:S(2)}) collective-permute-start(f32[4,64,128]{2,1,0:T(8,128)S(1)} %get-tuple-element.23), channel_id=1, source_target_pairs={{1,0},{2,1},{3,2},{4,3},{5,4},{6,5},{7,6},{8,7},{9,8},{10,9},{11,1... | collective-permute-start | bytes 393224 | tf_op jit(solution)/shard_map/ppermute | solution.py:310
  53.6 12.7 %collective-permute-done.4.low = f32[4,64,128]{2,1,0:T(8,128)S(1)} collective-permute-done((f32[4,64,128]{2,1,0:T(8,128)S(1)}, f32[4,64,128]{2,1,0:T(8,128)S(1)}, u32[]{:S(2)}, u32[]{:S(2)}) %collective-permute-start.4) | collective-permute-done | bytes 131104 | tf_op jit(solution)/shard_map/ppermute | solution.py:309
  66.3 0.0 collective-permute-done.5.high
  66.3 4.3 %pull.1 = f32[4,8,64,128]{3,2,1,0:T(8,128)S(1)} custom-call(f32[1,4,8,64,128]{4,3,2,1,0:T(8,128)S(1)} %copy-done.1, f32[3,4,8,64,128]{4,3,2,1,0:T(8,128)} %get-tuple-element.19.hist, f32[4,8,64,128]{3,2,1,0:T(8,128)S(1)} %get-tuple-element.20.gap, f32[8,64,128]{2,1,0:T(8,128)S(1)} %get-tuple-element.14.wx, f32[8,64,128]{2,1,0:T(8,128)S(1)} %get-tuple-element.15.wy, ...), custom_call_target="tpu_custom_call" | custom-call | tf_op jit(solution)/shard_map/pull/pallas_call | solution.py:312
  70.6 0.0 collective-permute-done.3
  70.6 1.2 %bitcast_subtract_fusion = f32[1,4,8,64,128]{4,3,2,1,0:T(8,128)} fusion(f32[1,4,8,64,128]{4,3,2,1,0:T(8,128)S(1)} %collective-permute-done.3, f32[4,8,64,128]{3,2,1,0:T(8,128)S(1)} %pull.1), kind=kLoop, calls=%fused_computation | loop fusion | flops 262144 | bytes 3145728 | tf_op jit(solution)/shard_map/sub | solution.py:319
  71.7 1.0 %copy.8 = f32[1,4,8,64,128]{4,3,2,1,0:T(8,128)} copy(f32[1,4,8,64,128]{4,3,2,1,0:T(8,128)S(1)} %collective-permute-done.3) | data formatting | bytes 2097152
Async XLA Ops:
  0.6 37.4 %collective-permute-start.2 = (f32[1,4,8,64,128]{4,3,2,1,0:T(8,128)}, f32[1,4,8,64,128]{4,3,2,1,0:T(8,128)S(1)}, u32[]{:S(2)}, u32[]{:S(2)}) collective-permute-start(f32[1,4,8,64,128]{4,3,2,1,0:T(8,128)} %starts.5), channel_id=1, source_target_pairs={{32,0},{64,32},{96,64},{128,96},{160,128},{192,160},{224,192},{256... | collective-permute-start | bytes 3145736 | tf_op jit(solution)/shard_map/ppermute | solution.py:290
  3.2 1.2 %copy-start = (f32[1,4,8,64,128]{4,3,2,1,0:T(8,128)S(1)}, f32[1,4,8,64,128]{4,3,2,1,0:T(8,128)}, u32[]{:S(2)}) copy-start(f32[1,4,8,64,128]{4,3,2,1,0:T(8,128)} %starts.5) | copy-start | bytes 3145732
  4.5 0.9 %copy-start.2 = (s32[8,64,128]{2,1,0:T(8,128)S(1)}, s32[8,64,128]{2,1,0:T(8,128)}, u32[]{:S(2)}) copy-start(s32[8,64,128]{2,1,0:T(8,128)} %tissue.5) | copy-start | bytes 786436
  5.4 0.9 %copy-start.5 = (s32[8,64,128]{2,1,0:T(8,128)S(1)}, s32[8,64,128]{2,1,0:T(8,128)}, u32[]{:S(2)}) copy-start(s32[8,64,128]{2,1,0:T(8,128)} %fibers.5) | copy-start | bytes 786436
  6.4 0.9 %copy-start.8 = (s32[8,64,128]{2,1,0:T(8,128)S(1)}, s32[8,64,128]{2,1,0:T(8,128)}, u32[]{:S(2)}) copy-start(s32[8,64,128]{2,1,0:T(8,128)} %pacing.3) | copy-start | bytes 786436
  7.3 0.7 copy-start.9
  8.0 23.4 %copy-start.1 = (f32[1,4,8,64,128]{4,3,2,1,0:T(8,128)S(1)}, f32[1,4,8,64,128]{4,3,2,1,0:T(8,128)}, u32[]{:S(2)}) copy-start(f32[1,4,8,64,128]{4,3,2,1,0:T(8,128)} %starts.5) | copy-start | bytes 3145732
  9.2 17.5 %collective-permute-start.1 = (f32[10,64,128]{2,1,0:T(8,128)S(1)}, f32[10,64,128]{2,1,0:T(8,128)S(1)}, u32[]{:S(2)}, u32[]{:S(2)}) collective-permute-start(f32[10,64,128]{2,1,0:T(8,128)S(1)} %get-tuple-element.17), channel_id=1, source_target_pairs={{1,0},{2,1},{3,2},{4,3},{5,4},{6,5},{7,6},{8,7},{9,8},{10,9},{11,1... | collective-permute-start | bytes 983048 | tf_op jit(solution)/shard_map/ppermute | solution.py:289
  12.1 19.3 %collective-permute-start = (f32[10,64,128]{2,1,0:T(8,128)S(1)}, f32[10,64,128]{2,1,0:T(8,128)S(1)}, u32[]{:S(2)}, u32[]{:S(2)}) collective-permute-start(f32[10,64,128]{2,1,0:T(8,128)S(1)} %get-tuple-element.13.gate), channel_id=1, source_target_pairs={{0,1},{1,2},{2,3},{3,4},{4,5},{5,6},{6,7},{7,8},{8,9},{9,10},{10,1... | collective-permute-start | bytes 983048 | tf_op jit(solution)/shard_map/ppermute | solution.py:288
  18.1 1.0 %copy-start.3 = (s32[8,64,128]{2,1,0:T(8,128)S(1)}, s32[8,64,128]{2,1,0:T(8,128)}, u32[]{:S(2)}) copy-start(s32[8,64,128]{2,1,0:T(8,128)} %tissue.5) | copy-start | bytes 786436
  19.1 0.9 %copy-start.6 = (s32[8,64,128]{2,1,0:T(8,128)S(1)}, s32[8,64,128]{2,1,0:T(8,128)}, u32[]{:S(2)}) copy-start(s32[8,64,128]{2,1,0:T(8,128)} %fibers.5) | copy-start | bytes 786436
  31.4 1.0 %copy-start.4 = (s32[8,64,128]{2,1,0:T(8,128)S(1)}, s32[8,64,128]{2,1,0:T(8,128)}, u32[]{:S(2)}) copy-start(s32[8,64,128]{2,1,0:T(8,128)} %tissue.5) | copy-start | bytes 786436
  32.4 0.9 %copy-start.7 = (s32[8,64,128]{2,1,0:T(8,128)S(1)}, s32[8,64,128]{2,1,0:T(8,128)}, u32[]{:S(2)}) copy-start(s32[8,64,128]{2,1,0:T(8,128)} %fibers.5) | copy-start | bytes 786436
  40.7 29.8 %collective-permute-start.3 = (f32[1,4,8,64,128]{4,3,2,1,0:T(8,128)S(1)}, f32[1,4,8,64,128]{4,3,2,1,0:T(8,128)S(1)}, u32[]{:S(2)}, u32[]{:S(2)}) collective-permute-start(f32[1,4,8,64,128]{4,3,2,1,0:T(8,128)S(1)} %bitcast.4), channel_id=1, source_target_pairs={{0,32},{32,64},{64,96},{96,128},{128,160},{160,192},{192,224},{224... | collective-permute-start | bytes 3145736 | tf_op jit(solution)/shard_map/ppermute | solution.py:311
  44.0 22.3 %collective-permute-start.4 = (f32[4,64,128]{2,1,0:T(8,128)S(1)}, f32[4,64,128]{2,1,0:T(8,128)S(1)}, u32[]{:S(2)}, u32[]{:S(2)}) collective-permute-start(f32[4,64,128]{2,1,0:T(8,128)S(1)} %get-tuple-element.22), channel_id=1, source_target_pairs={{0,1},{1,2},{2,3},{3,4},{4,5},{5,6},{6,7},{7,8},{8,9},{9,10},{10,1... | collective-permute-start | bytes 393224 | tf_op jit(solution)/shard_map/ppermute | solution.py:309
  51.7 14.6 %collective-permute-start.5 = (f32[4,64,128]{2,1,0:T(8,128)S(1)}, f32[4,64,128]{2,1,0:T(8,128)S(1)}, u32[]{:S(2)}, u32[]{:S(2)}) collective-permute-start(f32[4,64,128]{2,1,0:T(8,128)S(1)} %get-tuple-element.23), channel_id=1, source_target_pairs={{1,0},{2,1},{3,2},{4,3},{5,4},{6,5},{7,6},{8,7},{9,8},{10,9},{11,1... | collective-permute-start | bytes 393224 | tf_op jit(solution)/shard_map/ppermute | solution.py:310

commit v2 on v1

v2 whole, which is shorter than its diff:
```python
import jax
import jax.numpy as jnp
from jax import lax
from jax.experimental import pallas as pl
from jax.experimental.pallas import tpu as pltpu
from jax.sharding import PartitionSpec as P

DEEP = 8
NX = 64
NY = 128
V0, P1, G1, G2, G3, Q2, Q3, FIB, TIS, WIN = range(10)
C_W01, C_WIN, C_WX, C_WY, C_D2, C_E, C_D1 = range(7)
HALF_STEP = 0.15 * 0.5


def ahead(plane, axis):
    return pltpu.roll(plane, plane.shape[axis] - 1, axis)


def behind(plane, axis):
    return pltpu.roll(plane, 1, axis)


def sigma(cond, fiber, direction):
    summed = jnp.zeros(fiber.shape, jnp.float32)
    for c in range(4):
        summed = jnp.where(fiber == c, cond[c, direction], summed)
    return summed


def cross_weight(sig, share, axis):
    place = lax.broadcasted_iota(jnp.int32, sig.shape, axis)
    inner = jnp.where(place < sig.shape[axis] - 1, HALF_STEP, 0.0)
    return inner * (sig + ahead(sig, axis)) * (share * ahead(share, axis))


def face_weight(sig_a, share_a, sig_b, share_b):
    return HALF_STEP * (sig_a + sig_b) * (share_a * share_b)


def cross(v, wx, wy):
    fx = wx * (ahead(v, 0) - v)
    fy = wy * (ahead(v, 1) - v)
    return (fx - behind(fx, 0)) + (fy - behind(fy, 1))


def reaction(v, g1, g2, g3):
    return 0.3 * (g1 * g2) * (1.0 - v) - 0.15 * g3 * v


def tanhs(v):
    return jnp.tanh(4.0 * v - 0.8), jnp.tanh(2.0 - 4.0 * v), jnp.tanh(4.0 * v - 3.2)


def gates_next(v, g1, g2, g3):
    t1, t2, t3 = tanhs(v)
    return (
        0.7 * g1 + (0.15 + 0.15 * t1),
        0.9 * g2 + (0.05 + 0.05 * t2),
        0.97 * g3 + (0.015 + 0.015 * t3),
    )


def fetch(copies, sems):
    started = [pltpu.make_async_copy(src, dst, sems.at[n]) for n, (src, dst) in enumerate(copies)]
    for copy in started:
        copy.start()
    for copy in started:
        copy.wait()


def edge_kernel(
    cond_in, flag, starts_in, tissue_in, fibers_in, pacing_in, up, down, starts, tissue, fibers, pacing, cond, sems
):
    fetch(
        [
            (starts_in.at[0], starts),
            (tissue_in, tissue),
            (fibers_in, fibers),
            (pacing_in, pacing),
            (cond_in, cond),
        ],
        sems,
    )
    for out, (b1, b2, b3, b4) in ((up, (7, 6, 5, 4)), (down, (0, 1, 2, 3))):
        share = [tissue[b].astype(jnp.float32) for b in (b1, b2, b3, b4)]
        sig0 = [sigma(cond, fibers[b], 0) for b in (b1, b2, b3, b4)]
        wz = [face_weight(sig0[i], share[i], sig0[i + 1], share[i + 1]) for i in range(3)]
        wx = [cross_weight(sigma(cond, fibers[b], 1), share[i], 0) for i, b in enumerate((b1, b2, b3))]
        wy = [cross_weight(sigma(cond, fibers[b], 2), share[i], 1) for i, b in enumerate((b1, b2, b3))]
        stim = [(0.6 * flag[0]) * pacing[b].astype(jnp.float32) for b in (b1, b2, b3)]
        v = [starts[0, b] for b in (b1, b2, b3, b4)]
        g = [[starts[n, b] for n in (1, 2, 3)] for b in (b1, b2, b3)]

        def own_step(i):
            total = v[i] + cross(v[i], wx[i], wy[i]) + reaction(v[i], *g[i]) + stim[i]
            total = total + wz[i] * (v[i + 1] - v[i])
            return total if i == 0 else total + wz[i - 1] * (v[i - 1] - v[i])

        out[V0] = v[0]
        out[P1] = own_step(0)
        gates = gates_next(v[0], *g[0])
        for n in range(3):
            out[G1 + n] = gates[n]
        v1_b2 = own_step(1)
        v1_b3 = own_step(2)
        out[Q2] = wz[0] * v1_b2 + stim[0]
        rest = v1_b2 + cross(v1_b2, wx[1], wy[1]) + reaction(v1_b2, *gates_next(v[1], *g[1])) + stim[1]
        rest = rest + wz[1] * (v1_b3 - v1_b2) - wz[0] * v1_b2
        out[Q3] = wz[0] * rest + stim[0]
        out[FIB] = fibers[b1].astype(jnp.float32)
        out[TIS] = share[0]
        out[WIN] = wz[0]


class Fields:
    def __init__(self, inner, outer, rim_voltage, rim_gate):
        self.refs = (inner, outer)
        self.rims = (rim_voltage, rim_gate)

    def plane(self, field, layer):
        rim = self.rims[0] if field == 0 else self.rims[1]
        inside = rim <= layer < DEEP - rim
        return self.refs[0 if inside else 1][field, layer]

    def all(self, layer):
        return [self.plane(n, layer) for n in range(4)]


def forward_fields(starts, inner, outer):
    return [Fields(starts, None, 0, 0)] + [Fields(inner[j - 1], outer[j - 1], j, j - 1) for j in (1, 2, 3)]


def inner_layers(rim):
    return range(rim, DEEP - rim)


def rim_layers(rim):
    return [i for i in range(DEEP) if not rim <= i < DEEP - rim]


def ahead_kernel(cond_in, flag, starts, tissue, fibers, pacing, wx, wy, wz, f1, f2, f3, f4, cond, sems):
    fetch([(cond_in, cond)], sems)
    before = None
    for i in range(DEEP):
        share = tissue[i].astype(jnp.float32)
        sig0 = sigma(cond, fibers[i], 0)
        wx[i] = cross_weight(sigma(cond, fibers[i], 1), share, 0)
        wy[i] = cross_weight(sigma(cond, fibers[i], 2), share, 1)
        if i:
            wz[i - 1] = face_weight(*before, sig0, share)
        before = (sig0, share)
    old = starts
    for step, new in enumerate((f1, f2, f3, f4)):
        below = None
        for i in inner_layers(step):
            v, *g = [old[n, i] for n in range(4)]
            for n, gate in enumerate(gates_next(v, *g)):
                new[n + 1, i] = gate
            if step == 0:
                low, high = i > 0, i < DEEP - 1
            else:
                low = high = step + 1 <= i < DEEP - step - 1
            if not (low or high):
                continue
            total = v + cross(v, wx[i], wy[i]) + reaction(v, *g)
            total = total + (0.6 * flag[0]) * pacing[i].astype(jnp.float32)
            if low:
                total = total - (wz[i - 1] * (v - old[0, i - 1]) if below is None else below)
            below = None
            if high:
                below = wz[i] * (old[0, i + 1] - v)
                total = total + below
            new[0, i] = total
        old = new


def forward_kernel(
    cond_in, flag, starts, tissue, fibers, pacing, wx, wy, wz, p1, p2, p3, p4, low, high,
    f1, f2, f3, f4, side, cond, sems,
):
    fetch([(cond_in, cond)], sems)
    halo = []
    for n, (msg, own) in enumerate(((low, 0), (high, DEEP - 1))):
        fib, tis = msg[FIB], msg[TIS]
        w01 = face_weight(sigma(cond, fib, 0), tis, sigma(cond, fibers[own], 0), tissue[own].astype(jnp.float32))
        side[n, C_W01] = w01
        side[n, C_WIN] = msg[WIN]
        side[n, C_WX] = cross_weight(sigma(cond, fib, 1), tis, 0)
        side[n, C_WY] = cross_weight(sigma(cond, fib, 2), tis, 1)
        halo.append(msg[V0])
        inflow = w01 * (msg[V0] - starts[0, own])
        f1[0, own] = p1[0, own] + inflow
        halo[n] = msg[P1] - inflow
        side[n, C_D1] = halo[n]
    fields = forward_fields(starts, (p1, p2, p3), (f1, f2, f3))
    for n in range(1, 4):
        for i in inner_layers(3):
            f4[n, i] = p4[n, i]
    for step in (1, 2, 3):
        old = fields[step]
        new = (f1, f2, f3, f4)[step]
        outflow = [None, None]
        above = None
        for i in rim_layers(step + 1):
            v, *g = old.all(i)
            if i not in inner_layers(step):
                for n, gate in enumerate(gates_next(v, *g)):
                    new[n + 1, i] = gate
            if i == 0:
                below = outflow[0] = side[0, C_W01] * (v - halo[0])
            elif above is not None:
                below = above
            else:
                below = wz[i - 1] * (v - old.plane(0, i - 1))
            if i == DEEP - 1:
                above = side[1, C_W01] * (halo[1] - v)
                outflow[1] = -above
            else:
                above = wz[i] * (old.plane(0, i + 1) - v)
            total = v + (above - below) + cross(v, wx[i], wy[i]) + reaction(v, *g)
            new[0, i] = total + (0.6 * flag[0]) * pacing[i].astype(jnp.float32)
            if i == step and step < 3:
                above = None
        if step == 3:
            continue
        for n, msg in enumerate((low, high)):
            v = halo[n]
            win = side[n, C_WIN]
            g = [msg[G1], msg[G2], msg[G3]]
            if step == 1:
                extra = msg[Q2]
            else:
                v1 = side[n, C_D1]
                g1 = g
                g = gates_next(v1, *g1)
                extra = msg[Q3] + win * win * v1
                t1, t2, t3 = tanhs(v1)
                side[n, C_D2] = -0.3 * (g[0] * g[1]) - 0.15 * g[2]
                side[n, C_D1] = -0.3 * (g1[0] * g1[1]) - 0.15 * g1[2]
                side[n, C_E] = (
                    0.6 * (1.0 - t1 * t1) * (0.3 * g[1] * (1.0 - v))
                    - 0.2 * (1.0 - t2 * t2) * (0.3 * g[0] * (1.0 - v))
                    - 0.06 * (1.0 - t3 * t3) * (0.15 * v)
                )
            total = v + cross(v, side[n, C_WX], side[n, C_WY]) + reaction(v, *g)
            halo[n] = total + (extra - win * v) + outflow[n]


def pull_gates(a, f):
    av, a1, a2, a3 = a
    v, g1, g2, g3 = f
    rest = 0.3 * (1.0 - v) * av
    return 0.7 * a1 + g2 * rest, 0.9 * a2 + g1 * rest, 0.97 * a3 - 0.15 * v * av


def pull_voltage(a, f):
    av, a1, a2, a3 = a
    v, g1, g2, g3 = f
    t1, t2, t3 = tanhs(v)
    total = av * (1.0 - 0.3 * (g1 * g2) - 0.15 * g3)
    total = total + 0.6 * (1.0 - t1 * t1) * a1 - 0.2 * (1.0 - t2 * t2) * a2
    return total + 0.06 * (1.0 - t3 * t3) * a3


def send_kernel(ends, following, starts, p1, p2, p3, f1, f2, f3, wx, wy, wz, gap, up, down):
    fields = forward_fields(starts, (p1, p2, p3), (f1, f2, f3))
    for n in range(4):
        for i in range(DEEP):
            gap[n, i] = ends[n, i] - following[0, n, i]
    for out, (b1, sign) in ((up, (7, -1)), (down, (0, 1))):
        layers = [b1 + sign * d for d in range(4)]
        a = [[gap[n, b] for n in range(4)] for b in layers]
        out[0] = a[0][0]
        for m in range(3):
            fresh = []
            outer = None
            for d in range(3 - m):
                b = layers[d]
                f = fields[3 - m].all(b)
                face = wz[b - 1] if sign < 0 else wz[b]
                inner = face * (a[d + 1][0] - a[d][0])
                total = pull_voltage(a[d], f) + cross(a[d][0], wx[b], wy[b]) + inner
                if outer is not None:
                    total = total - outer
                fresh.append([total, *pull_gates(a[d], f)])
                outer = inner
            a = fresh
            out[m + 1] = a[0][0]


def back_kernel(gap, starts, p1, p2, p3, f1, f2, f3, wx, wy, wz, gate, a1, a2, a3, a4):
    fields = forward_fields(starts, (p1, p2, p3), (f1, f2, f3))
    old = gap
    for m, new in enumerate((a1, a2, a3, a4)):
        below = None
        for i in inner_layers(m):
            a = [old[n, i] for n in range(4)]
            f = fields[3 - m].all(i)
            for n, plane in enumerate(pull_gates(a, f)):
                new[n + 1, i] = plane
            if i not in inner_layers(m + 1):
                continue
            if below is None:
                below = wz[i - 1] * (a[0] - old[0, i - 1])
            above = wz[i] * (old[0, i + 1] - a[0])
            new[0, i] = pull_voltage(a, f) + (above - below) + cross(a[0], wx[i], wy[i])
            below = above
        old = new


def pull_kernel(
    starts, gap, before, p1, p2, p3, f1, f2, f3, b1, b2, b3, b4, wx, wy, wz, side, low, high,
    defect_out, gradient_out, work, defect, gradient, sems,
):
    for n in range(4):
        for i in range(DEEP):
            defect[n, i] = before[0, n, i] - starts[n, i]
    copies = [pltpu.make_async_copy(defect, defect_out.at[0], sems.at[DEEP])]
    copies[0].start()
    fields = forward_fields(starts, (p1, p2, p3), (f1, f2, f3))
    adjoints = [Fields(gap, None, 0, 0)] + [
        Fields(b, work.at[j], j + 1, j) for j, b in enumerate((b1, b2, b3))
    ]
    halo = [low[0], high[0]]
    first = [None, None]
    last = [None, None]
    for m in range(4):
        old = adjoints[m]
        outflow = [None, None]
        above = None
        for i in rim_layers(m + 1):
            a = old.all(i)
            f = fields[3 - m].all(i)
            if i == 0:
                below = outflow[0] = side[0, C_W01] * (a[0] - halo[0])
            elif above is not None:
                below = above
            else:
                below = wz[i - 1] * (a[0] - old.plane(0, i - 1))
            if i == DEEP - 1:
                above = side[1, C_W01] * (halo[1] - a[0])
                outflow[1] = -above
            else:
                above = wz[i] * (old.plane(0, i + 1) - a[0])
            fresh = [pull_voltage(a, f) + (above - below) + cross(a[0], wx[i], wy[i])]
            if i in inner_layers(m):
                if m == 3:
                    fresh += [b4[n, i] for n in (1, 2, 3)]
            else:
                fresh += pull_gates(a, f)
            if i == m and m < 3:
                above = None
            if m < 3:
                for n, plane in enumerate(fresh):
                    work[m, n, i] = plane
                continue
            for n, plane in enumerate(fresh):
                gradient[n, i] = plane - defect[n, i]
            copy = pltpu.make_async_copy(gradient.at[:, i], gradient_out.at[0, :, i], sems.at[i])
            copy.start()
            copies.append(copy)
        if m == 3:
            continue
        for n, msg in enumerate((low, high)):
            win, px, py = side[n, C_WIN], side[n, C_WX], side[n, C_WY]
            if m == 0:
                change = first[n] = outflow[n]
            else:
                d = last[n]
                rate = side[n, C_D2] if m == 1 else side[n, C_D1]
                change = d + cross(d, px, py) + (rate - win) * d + outflow[n]
                if m == 2:
                    change = change + (win * win + side[n, C_E]) * first[n]
            halo[n] = msg[m + 1] + change
            last[n] = change
    for copy in copies:
        copy.wait()


VM = pl.BlockSpec(memory_space=pltpu.VMEM)
SM = pl.BlockSpec(memory_space=pltpu.SMEM)
ANY = pl.BlockSpec(memory_space=pl.ANY)


def f32(*shape):
    return jax.ShapeDtypeStruct(shape, jnp.float32)


def i32(*shape):
    return jax.ShapeDtypeStruct(shape, jnp.int32)


def call(kernel, name, ins, outs, scratch=(), out_spec=VM):
    return pl.pallas_call(
        kernel,
        name=name,
        in_specs=ins,
        out_specs=[out_spec] * len(outs),
        out_shape=outs,
        scratch_shapes=list(scratch),
        compiler_params=pltpu.CompilerParams(vmem_limit_bytes=28 * 1024 * 1024),
    )


def body(starts, tissue, fibers, pacing, conductances):
    plane = (NX, NY)
    slab = (DEEP, *plane)
    fields = f32(4, *slab)
    slabs = lax.axis_size("slab")
    sections = lax.axis_size("tm")
    upward = [(i, i + 1) for i in range(slabs - 1)]
    downward = [(i + 1, i) for i in range(slabs - 1)]
    earlier = [((i + 1) % sections, i) for i in range(sections)]
    later = [(i, (i + 1) % sections) for i in range(sections)]
    flag = (lax.axis_index("tm") == 0).astype(jnp.float32).reshape(1)
    few = [pltpu.SMEM((4, 3), jnp.float32), pltpu.SemaphoreType.DMA((1,))]

    up, down, own, tis, fib, pac = call(
        edge_kernel,
        "edge",
        [ANY, SM] + [ANY] * 4,
        [f32(10, *plane)] * 2 + [fields] + [i32(*slab)] * 3,
        [pltpu.SMEM((4, 3), jnp.float32), pltpu.SemaphoreType.DMA((5,))],
    )(conductances, flag, starts, tissue, fibers, pacing)
    low = lax.ppermute(up, "slab", upward)
    high = lax.ppermute(down, "slab", downward)
    following = lax.ppermute(starts, "tm", earlier)
    wx, wy, wz, p1, p2, p3, p4 = call(
        ahead_kernel,
        "ahead",
        [ANY, SM] + [VM] * 4,
        [f32(*slab), f32(*slab), f32(DEEP - 1, *plane)] + [fields] * 4,
        few,
    )(conductances, flag, own, tis, fib, pac)
    f1, f2, f3, ends, side = call(
        forward_kernel,
        "forward",
        [ANY, SM] + [VM] * 13,
        [fields] * 4 + [f32(2, 7, *plane)],
        few,
    )(conductances, flag, own, tis, fib, pac, wx, wy, wz, p1, p2, p3, p4, low, high)
    before = lax.ppermute(ends[None], "tm", later)
    history = (own, p1, p2, p3, f1, f2, f3)
    gap, up, down = call(
        send_kernel, "send", [VM] * 12, [fields, f32(4, *plane), f32(4, *plane)]
    )(ends, following, *history, wx, wy, wz)
    low = lax.ppermute(up, "slab", upward)
    high = lax.ppermute(down, "slab", downward)
    inner = call(back_kernel, "back", [VM] * 11 + [ANY], [fields] * 4)(gap, *history, wx, wy, wz, up)
    defect, gradient = call(
        pull_kernel,
        "pull",
        [VM] * 19,
        [f32(1, 4, *slab)] * 2,
        [pltpu.VMEM((3, 4, *slab), jnp.float32)]
        + [pltpu.VMEM((4, *slab), jnp.float32)] * 2
        + [pltpu.SemaphoreType.DMA((DEEP + 1,))],
        ANY,
    )(own, gap, before, p1, p2, p3, f1, f2, f3, *inner, wx, wy, wz, side, low, high)
    return defect, gradient


def solution(mesh):
    spread = P("tm", None, "slab", None, None)
    placed = (spread, P("slab", None, None), P("slab", None, None), P("slab", None, None), P())
    return jax.shard_map(body, mesh=mesh, in_specs=placed, out_specs=(spread, spread), check_vma=False)
```

time: 73.3 us -> 66.7 us (0.910)
  the two profiles are of different devices: /device:TPU:127 before, /device:TPU:425 now
where the time goes in v2:
time: 66.7 us; the launch traced here: 66.3 us
  starting transfers between devices  32.2 us (48%)
  waiting for transfers between devices  18.7 us (28%)
  Pallas kernels  9.9 us (15%)
  local copies, waits for them, and re-layouts  4.75 us (7%)
  between operations  0.75 us (1%)
    ppermute x1, starting transfers between devices, body(): before = lax.ppermute(ends[None], 'tm', later)  14.6 us
    ppermute x2, waiting for transfers between devices, body(): high = lax.ppermute(down, 'slab', downward)  14 us
    ppermute x2, starting transfers between devices, body(): high = lax.ppermute(down, 'slab', downward)  7.53 us
    ppermute x2, starting transfers between devices, body(): low = lax.ppermute(up, 'slab', upward)  6.94 us
    unnamed x10, local copies, waits for them, and re-layouts  4.75 us
    ppermute x2, waiting for transfers between devices, body(): low = lax.ppermute(up, 'slab', upward)  4.65 us
    ppermute x1, starting transfers between devices, body(): following = lax.ppermute(starts, 'tm', earlier)  3.14 us
    pallas_call x1, Pallas kernels, body(): call(pull_kernel, 'pull', [VM] * 19, [f32(1, 4, *slab)] * 2, [pltpu.VMEM(...  2.87 us
  transfers between devices with their start and end apart: 6, of which 3 were waited for; matrix products, arithmetic and copies ran while one was open for 0% of the time, Pallas kernels for 7%

profile of v2, /device:TPU:425, one launch (start us, length us, event | category | flops | bytes accessed | tf_op | source)
XLA Modules:
  0.0 66.3 jit_solution(1718601146841030294)
XLA Ops:
  0.6 0.0 copy-start.4
  0.6 0.7 %copy-done.4 = f32[4,3]{1,0:T(4,128)S(1)} copy-done((f32[4,3]{1,0:T(4,128)S(1)}, f32[4,3]{1,0:T(4,128)}, u32[]{:S(2)}) %copy-start.4) | copy-done | bytes 72
  1.3 0.0 copy-start
  1.3 1.2 %copy-done = f32[1,4,8,64,128]{4,3,2,1,0:T(8,128)S(1)} copy-done((f32[1,4,8,64,128]{4,3,2,1,0:T(8,128)S(1)}, f32[1,4,8,64,128]{4,3,2,1,0:T(8,128)}, u32[]{:S(2)}) %copy-start) | copy-done | bytes 1048600
  2.5 0.0 copy-start.1
  2.5 0.9 %copy-done.1 = s32[8,64,128]{2,1,0:T(8,128)S(1)} copy-done((s32[8,64,128]{2,1,0:T(8,128)S(1)}, s32[8,64,128]{2,1,0:T(8,128)}, u32[]{:S(2)}) %copy-start.1) | copy-done | bytes 262168
  3.5 0.0 copy-start.2
  3.5 0.9 %copy-done.2 = s32[8,64,128]{2,1,0:T(8,128)S(1)} copy-done((s32[8,64,128]{2,1,0:T(8,128)S(1)}, s32[8,64,128]{2,1,0:T(8,128)}, u32[]{:S(2)}) %copy-start.2) | copy-done | bytes 262168
  4.4 0.0 copy-start.3
  4.4 0.9 %copy-done.3 = s32[8,64,128]{2,1,0:T(8,128)S(1)} copy-done((s32[8,64,128]{2,1,0:T(8,128)S(1)}, s32[8,64,128]{2,1,0:T(8,128)}, u32[]{:S(2)}) %copy-start.3) | copy-done | bytes 262168
  5.4 1.4 %edge.1 = (f32[10,64,128]{2,1,0:T(8,128)S(1)}, f32[10,64,128]{2,1,0:T(8,128)S(1)}, f32[4,8,64,128]{3,2,1,0:T(8,128)S(1)}, s32[8,64,128]{2,1,0:T(8,128)S(1)}, s32...) custom-call(f32[4,3]{1,0:T(4,128)S(1)} %copy-done.4, f32[1]{0:T(128)} %bitcast.flag, f32[1,4,8,64,128]{4,3,2,1,0:T(8,128)S(1)} %copy-done, ...), custom_call_target="tpu_custom_call" | custom-call | tf_op jit(solution)/shard_map/edge/pallas_call | solution.py:419
  6.8 3.9 %collective-permute-start = (f32[10,64,128]{2,1,0:T(8,128)S(1)}, f32[10,64,128]{2,1,0:T(8,128)S(1)}, u32[]{:S(2)}, u32[]{:S(2)}) collective-permute-start(f32[10,64,128]{2,1,0:T(8,128)S(1)} %get-tuple-element.38), channel_id=1, source_target_pairs={{0,1},{1,2},{2,3},{3,4},{4,5},{5,6},{6,7},{7,8},{8,9},{9,10},{10,1... | collective-permute-start | bytes 983048 | tf_op jit(solution)/shard_map/ppermute | solution.py:426
  10.7 3.8 %collective-permute-start.1 = (f32[10,64,128]{2,1,0:T(8,128)S(1)}, f32[10,64,128]{2,1,0:T(8,128)S(1)}, u32[]{:S(2)}, u32[]{:S(2)}) collective-permute-start(f32[10,64,128]{2,1,0:T(8,128)S(1)} %get-tuple-element.39), channel_id=1, source_target_pairs={{1,0},{2,1},{3,2},{4,3},{5,4},{6,5},{7,6},{8,7},{9,8},{10,9},{11,1... | collective-permute-start | bytes 983048 | tf_op jit(solution)/shard_map/ppermute | solution.py:427
  14.5 3.1 %collective-permute-start.2 = (f32[1,4,8,64,128]{4,3,2,1,0:T(8,128)S(1)}, f32[1,4,8,64,128]{4,3,2,1,0:T(8,128)S(1)}, u32[]{:S(2)}, u32[]{:S(2)}) collective-permute-start(f32[1,4,8,64,128]{4,3,2,1,0:T(8,128)S(1)} %copy-done), channel_id=1, source_target_pairs={{32,0},{64,32},{96,64},{128,96},{160,128},{192,160},{224,192},{256... | collective-permute-start | bytes 3145736 | tf_op jit(solution)/shard_map/ppermute | solution.py:428
  17.6 1.8 %ahead.1 = (f32[8,64,128]{2,1,0:T(8,128)S(1)}, f32[8,64,128]{2,1,0:T(8,128)S(1)}, f32[7,64,128]{2,1,0:T(8,128)S(1)}, f32[4,8,64,128]{3,2,1,0:T(8,128)S(1)}, f32[...) custom-call(f32[4,3]{1,0:T(4,128)S(1)} %copy-done.4, f32[1]{0:T(128)} %bitcast.flag, ...), custom_call_target="tpu_custom_call" | custom-call | tf_op jit(solution)/shard_map/ahead/pallas_call | solution.py:429
  19.4 4.6 %collective-permute-done.low = f32[10,64,128]{2,1,0:T(8,128)S(1)} collective-permute-done((f32[10,64,128]{2,1,0:T(8,128)S(1)}, f32[10,64,128]{2,1,0:T(8,128)S(1)}, u32[]{:S(2)}, u32[]{:S(2)}) %collective-permute-start) | collective-permute-done | bytes 327712 | tf_op jit(solution)/shard_map/ppermute | solution.py:426
  24.1 3.6 %collective-permute-done.1.high = f32[10,64,128]{2,1,0:T(8,128)S(1)} collective-permute-done((f32[10,64,128]{2,1,0:T(8,128)S(1)}, f32[10,64,128]{2,1,0:T(8,128)S(1)}, u32[]{:S(2)}, u32[]{:S(2)}) %collective-permute-start.1) | collective-permute-done | bytes 327712 | tf_op jit(solution)/shard_map/ppermute | solution.py:427
  27.7 2.1 %forward.1 = (f32[4,8,64,128]{3,2,1,0:T(8,128)S(1)}, f32[4,8,64,128]{3,2,1,0:T(8,128)S(1)}, f32[4,8,64,128]{3,2,1,0:T(8,128)S(1)}, f32[4,8,64,128]{3,2,1,0:T(8,128)S(1)}, f32[2,7,64,128]{3,2,1,0:T(8,128)S(1)}) custom-call(f32[4,3]{1,0:T(4,128)S(1)} %copy-done.4, f32[1]{0:T(128)} %bitcast.flag, f32[4,8,64,128]{3,2,1,0:T(8,128)S(1)} %get-tuple-element.27.starts, ...), custom_call_target="tpu_custom_call" | custom-call | tf_op jit(solution)/shard_map/forward/pallas_call | solution.py:436
  29.8 14.6 %collective-permute-start.3 = (f32[1,4,8,64,128]{4,3,2,1,0:T(8,128)S(1)}, f32[1,4,8,64,128]{4,3,2,1,0:T(8,128)S(1)}, u32[]{:S(2)}, u32[]{:S(2)}) collective-permute-start(f32[1,4,8,64,128]{4,3,2,1,0:T(8,128)S(1)} %bitcast.2), channel_id=1, source_target_pairs={{0,32},{32,64},{64,96},{96,128},{128,160},{160,192},{192,224},{224... | collective-permute-start | bytes 3145736 | tf_op jit(solution)/shard_map/ppermute | solution.py:443
  44.4 0.0 collective-permute-done.2.following
  44.5 0.8 %send.1 = (f32[4,8,64,128]{3,2,1,0:T(8,128)S(1)}, f32[4,64,128]{2,1,0:T(8,128)S(1)}, f32[4,64,128]{2,1,0:T(8,128)S(1)}) custom-call(f32[4,8,64,128]{3,2,1,0:T(8,128)S(1)} %get-tuple-element.40.ends, f32[1,4,8,64,128]{4,3,2,1,0:T(8,128)S(1)} %collective-permute-done.2.following, f32[4,8,64,128]{3,2,1,0:T(8,128)S(1)} %get-tuple-element.27.starts, ...), custom_call_target="tpu_custom_call" | custom-call | tf_op jit(solution)/shard_map/send/pallas_call | solution.py:445
  45.3 3.8 %collective-permute-start.5 = (f32[4,64,128]{2,1,0:T(8,128)S(1)}, f32[4,64,128]{2,1,0:T(8,128)S(1)}, u32[]{:S(2)}, u32[]{:S(2)}) collective-permute-start(f32[4,64,128]{2,1,0:T(8,128)S(1)} %get-tuple-element.51), channel_id=1, source_target_pairs={{1,0},{2,1},{3,2},{4,3},{5,4},{6,5},{7,6},{8,7},{9,8},{10,9},{11,1... | collective-permute-start | bytes 393224 | tf_op jit(solution)/shard_map/ppermute | solution.py:449
  49.0 3.0 %collective-permute-start.4 = (f32[4,64,128]{2,1,0:T(8,128)S(1)}, f32[4,64,128]{2,1,0:T(8,128)S(1)}, u32[]{:S(2)}, u32[]{:S(2)}) collective-permute-start(f32[4,64,128]{2,1,0:T(8,128)S(1)} %get-tuple-element.45.gate), channel_id=1, source_target_pairs={{0,1},{1,2},{2,3},{3,4},{4,5},{5,6},{6,7},{7,8},{8,9},{9,10},{10,1... | collective-permute-start | bytes 393224 | tf_op jit(solution)/shard_map/ppermute | solution.py:448
  52.1 1.0 %back.1 = (f32[4,8,64,128]{3,2,1,0:T(8,128)S(1)}, f32[4,8,64,128]{3,2,1,0:T(8,128)S(1)}, f32[4,8,64,128]{3,2,1,0:T(8,128)S(1)}, f32[4,8,64,128]{3,2,1,0:T(8,128)S(1)}) custom-call(f32[4,8,64,128]{3,2,1,0:T(8,128)S(1)} %get-tuple-element.44.gap, f32[4,8,64,128]{3,2,1,0:T(8,128)S(1)} %get-tuple-element.27.starts, f32[4,8,64,128]{3,2,1,0:T(8,128)S(1)} %get-tuple-element.34.p1, ...), custom_call_target="tpu_custom_call" | custom-call | tf_op jit(solution)/shard_map/back/pallas_call | solution.py:450
  53.1 10.4 %collective-permute-done.5.high = f32[4,64,128]{2,1,0:T(8,128)S(1)} collective-permute-done((f32[4,64,128]{2,1,0:T(8,128)S(1)}, f32[4,64,128]{2,1,0:T(8,128)S(1)}, u32[]{:S(2)}, u32[]{:S(2)}) %collective-permute-start.5) | collective-permute-done | bytes 131104 | tf_op jit(solution)/shard_map/ppermute | solution.py:449
  63.4 0.0 collective-permute-done.4.low
  63.4 0.0 collective-permute-done.3.before
  63.4 2.9 %pull.1 = (f32[1,4,8,64,128]{4,3,2,1,0:T(8,128)}, f32[1,4,8,64,128]{4,3,2,1,0:T(8,128)}) custom-call(f32[4,8,64,128]{3,2,1,0:T(8,128)S(1)} %get-tuple-element.27.starts, f32[4,8,64,128]{3,2,1,0:T(8,128)S(1)} %get-tuple-element.44.gap, f32[1,4,8,64,128]{4,3,2,1,0:T(8,128)S(1)} %collective-permute-done.3.before, f32[4,8,64,128]{3,2,1,0:T(8,128)S(1)} %get-tuple-element.34.p1, ...), custom_call_target="tpu_custom_call" | custom-call | tf_op jit(solution)/shard_map/pull/pallas_call | solution.py:451
Async XLA Ops:
  0.6 0.7 %copy-start.4 = (f32[4,3]{1,0:T(4,128)S(1)}, f32[4,3]{1,0:T(4,128)}, u32[]{:S(2)}) copy-start(f32[4,3]{1,0:T(4,128)} %cond_in.5) | copy-start | bytes 148
  1.3 1.2 %copy-start = (f32[1,4,8,64,128]{4,3,2,1,0:T(8,128)S(1)}, f32[1,4,8,64,128]{4,3,2,1,0:T(8,128)}, u32[]{:S(2)}) copy-start(f32[1,4,8,64,128]{4,3,2,1,0:T(8,128)} %starts_in.1) | copy-start | bytes 3145732
  2.5 0.9 %copy-start.1 = (s32[8,64,128]{2,1,0:T(8,128)S(1)}, s32[8,64,128]{2,1,0:T(8,128)}, u32[]{:S(2)}) copy-start(s32[8,64,128]{2,1,0:T(8,128)} %tissue_in.1) | copy-start | bytes 786436
  3.5 0.9 %copy-start.2 = (s32[8,64,128]{2,1,0:T(8,128)S(1)}, s32[8,64,128]{2,1,0:T(8,128)}, u32[]{:S(2)}) copy-start(s32[8,64,128]{2,1,0:T(8,128)} %fibers_in.1) | copy-start | bytes 786436
  4.4 0.9 %copy-start.3 = (s32[8,64,128]{2,1,0:T(8,128)S(1)}, s32[8,64,128]{2,1,0:T(8,128)}, u32[]{:S(2)}) copy-start(s32[8,64,128]{2,1,0:T(8,128)} %pacing_in.1) | copy-start | bytes 786436
  6.8 17.3 %collective-permute-start = (f32[10,64,128]{2,1,0:T(8,128)S(1)}, f32[10,64,128]{2,1,0:T(8,128)S(1)}, u32[]{:S(2)}, u32[]{:S(2)}) collective-permute-start(f32[10,64,128]{2,1,0:T(8,128)S(1)} %get-tuple-element.38), channel_id=1, source_target_pairs={{0,1},{1,2},{2,3},{3,4},{4,5},{5,6},{6,7},{7,8},{8,9},{9,10},{10,1... | collective-permute-start | bytes 983048 | tf_op jit(solution)/shard_map/ppermute | solution.py:426
  10.7 17.0 %collective-permute-start.1 = (f32[10,64,128]{2,1,0:T(8,128)S(1)}, f32[10,64,128]{2,1,0:T(8,128)S(1)}, u32[]{:S(2)}, u32[]{:S(2)}) collective-permute-start(f32[10,64,128]{2,1,0:T(8,128)S(1)} %get-tuple-element.39), channel_id=1, source_target_pairs={{1,0},{2,1},{3,2},{4,3},{5,4},{6,5},{7,6},{8,7},{9,8},{10,9},{11,1... | collective-permute-start | bytes 983048 | tf_op jit(solution)/shard_map/ppermute | solution.py:427
  14.5 30.0 %collective-permute-start.2 = (f32[1,4,8,64,128]{4,3,2,1,0:T(8,128)S(1)}, f32[1,4,8,64,128]{4,3,2,1,0:T(8,128)S(1)}, u32[]{:S(2)}, u32[]{:S(2)}) collective-permute-start(f32[1,4,8,64,128]{4,3,2,1,0:T(8,128)S(1)} %copy-done), channel_id=1, source_target_pairs={{32,0},{64,32},{96,64},{128,96},{160,128},{192,160},{224,192},{256... | collective-permute-start | bytes 3145736 | tf_op jit(solution)/shard_map/ppermute | solution.py:428
  29.8 33.6 %collective-permute-start.3 = (f32[1,4,8,64,128]{4,3,2,1,0:T(8,128)S(1)}, f32[1,4,8,64,128]{4,3,2,1,0:T(8,128)S(1)}, u32[]{:S(2)}, u32[]{:S(2)}) collective-permute-start(f32[1,4,8,64,128]{4,3,2,1,0:T(8,128)S(1)} %bitcast.2), channel_id=1, source_target_pairs={{0,32},{32,64},{64,96},{96,128},{128,160},{160,192},{192,224},{224... | collective-permute-start | bytes 3145736 | tf_op jit(solution)/shard_map/ppermute | solution.py:443
  45.3 18.1 %collective-permute-start.5 = (f32[4,64,128]{2,1,0:T(8,128)S(1)}, f32[4,64,128]{2,1,0:T(8,128)S(1)}, u32[]{:S(2)}, u32[]{:S(2)}) collective-permute-start(f32[4,64,128]{2,1,0:T(8,128)S(1)} %get-tuple-element.51), channel_id=1, source_target_pairs={{1,0},{2,1},{3,2},{4,3},{5,4},{6,5},{7,6},{8,7},{9,8},{10,9},{11,1... | collective-permute-start | bytes 393224 | tf_op jit(solution)/shard_map/ppermute | solution.py:449
  49.0 14.4 %collective-permute-start.4 = (f32[4,64,128]{2,1,0:T(8,128)S(1)}, f32[4,64,128]{2,1,0:T(8,128)S(1)}, u32[]{:S(2)}, u32[]{:S(2)}) collective-permute-start(f32[4,64,128]{2,1,0:T(8,128)S(1)} %get-tuple-element.45.gate), channel_id=1, source_target_pairs={{0,1},{1,2},{2,3},{3,4},{4,5},{5,6},{6,7},{7,8},{8,9},{9,10},{10,1... | collective-permute-start | bytes 393224 | tf_op jit(solution)/shard_map/ppermute | solution.py:448

commit v3 on v2

--- a/solution.py
+++ b/solution.py
@@ -381,6 +381,7 @@
 VM = pl.BlockSpec(memory_space=pltpu.VMEM)
 SM = pl.BlockSpec(memory_space=pltpu.SMEM)
 ANY = pl.BlockSpec(memory_space=pl.ANY)
+HBM = pl.BlockSpec(memory_space=pltpu.HBM)
 
 
 def f32(*shape):
@@ -416,27 +417,31 @@
     flag = (lax.axis_index("tm") == 0).astype(jnp.float32).reshape(1)
     few = [pltpu.SMEM((4, 3), jnp.float32), pltpu.SemaphoreType.DMA((1,))]
 
+    conductances, starts, tissue, fibers, pacing = (
+        pltpu.with_memory_space_constraint(arg, pltpu.HBM)
+        for arg in (conductances, starts, tissue, fibers, pacing)
+    )
     up, down, own, tis, fib, pac = call(
         edge_kernel,
         "edge",
-        [ANY, SM] + [ANY] * 4,
+        [HBM, SM] + [HBM] * 4,
         [f32(10, *plane)] * 2 + [fields] + [i32(*slab)] * 3,
         [pltpu.SMEM((4, 3), jnp.float32), pltpu.SemaphoreType.DMA((5,))],
     )(conductances, flag, starts, tissue, fibers, pacing)
     low = lax.ppermute(up, "slab", upward)
     high = lax.ppermute(down, "slab", downward)
-    following = lax.ppermute(starts, "tm", earlier)
+    following = lax.ppermute(own[None], "tm", earlier)
     wx, wy, wz, p1, p2, p3, p4 = call(
         ahead_kernel,
         "ahead",
-        [ANY, SM] + [VM] * 4,
+        [HBM, SM] + [VM] * 4,
         [f32(*slab), f32(*slab), f32(DEEP - 1, *plane)] + [fields] * 4,
         few,
     )(conductances, flag, own, tis, fib, pac)
     f1, f2, f3, ends, side = call(
         forward_kernel,
         "forward",
-        [ANY, SM] + [VM] * 13,
+        [HBM, SM] + [VM] * 13,
         [fields] * 4 + [f32(2, 7, *plane)],
         few,
     )(conductances, flag, own, tis, fib, pac, wx, wy, wz, p1, p2, p3, p4, low, high)

time: 66.7 us -> 62.7 us (0.940)
  local copies, waits for them, and re-layouts: 4.75 us -> 0 us
  Pallas kernels: 9.9 us -> 11 us
    unnamed x10 -> x0, local copies, waits for them, and re-layouts: 4.75 us -> none
    pallas_call x3, Pallas kernels: 5.26 us -> 6.29 us  [the longest x1 2.22 us: body(): call(forward_kernel, 'forward', [HBM, SM] + [VM] * 13, [fields] * 4 + [f3...]
  transfers between devices with their start and end apart: 6 -> 6, of which waited for: 3 -> 3; matrix products, arithmetic and copies ran while one was open for 0% -> 0% of each run, Pallas kernels for 7% -> 8%
where the time goes in v3:
time: 62.7 us; the launch traced here: 62.4 us
  starting transfers between devices  32.2 us (51%)
  waiting for transfers between devices  18.5 us (30%)
  Pallas kernels  11 us (18%)
  between operations  0.73 us (1%)
    ppermute x1, starting transfers between devices, body(): before = lax.ppermute(ends[None], 'tm', later)  14.6 us
    ppermute x2, waiting for transfers between devices, body(): high = lax.ppermute(down, 'slab', downward)  14 us
    ppermute x2, starting transfers between devices, body(): high = lax.ppermute(down, 'slab', downward)  7.53 us
    ppermute x2, starting transfers between devices, body(): low = lax.ppermute(up, 'slab', upward)  6.94 us
    ppermute x2, waiting for transfers between devices, body(): low = lax.ppermute(up, 'slab', upward)  4.51 us
    ppermute x1, starting transfers between devices, body(): following = lax.ppermute(own[None], 'tm', earlier)  3.14 us
    pallas_call x1, Pallas kernels, body(): call(pull_kernel, 'pull', [VM] * 19, [f32(1, 4, *slab)] * 2, [pltpu.VMEM(...  2.85 us
    pallas_call x1, Pallas kernels, body(): call(forward_kernel, 'forward', [HBM, SM] + [VM] * 13, [fields] * 4 + [f3...  2.22 us
  transfers between devices with their start and end apart: 6, of which 3 were waited for; matrix products, arithmetic and copies ran while one was open for 0% of the time, Pallas kernels for 8%

profile of v3, /device:TPU:425, one launch (start us, length us, event | category | flops | bytes accessed | tf_op | source)
XLA Modules:
  0.0 62.4 jit_solution(10445163559676838112)
XLA Ops:
  0.6 2.1 %edge.1 = (f32[10,64,128]{2,1,0:T(8,128)S(1)}, f32[10,64,128]{2,1,0:T(8,128)S(1)}, f32[4,8,64,128]{3,2,1,0:T(8,128)S(1)}, s32[8,64,128]{2,1,0:T(8,128)S(1)}, s32...) custom-call(f32[4,3]{1,0:T(4,128)} %cond_in.5, f32[1]{0:T(128)} %bitcast.flag, f32[1,4,8,64,128]{4,3,2,1,0:T(8,128)} %starts_in.1, ...), custom_call_target="tpu_custom_call" | custom-call | tf_op jit(solution)/shard_map/edge/pallas_call | solution.py:424
  2.8 3.9 %collective-permute-start = (f32[10,64,128]{2,1,0:T(8,128)S(1)}, f32[10,64,128]{2,1,0:T(8,128)S(1)}, u32[]{:S(2)}, u32[]{:S(2)}) collective-permute-start(f32[10,64,128]{2,1,0:T(8,128)S(1)} %get-tuple-element.38), channel_id=1, source_target_pairs={{0,1},{1,2},{2,3},{3,4},{4,5},{5,6},{6,7},{7,8},{8,9},{9,10},{10,1... | collective-permute-start | bytes 983048 | tf_op jit(solution)/shard_map/ppermute | solution.py:431
  6.7 3.8 %collective-permute-start.1 = (f32[10,64,128]{2,1,0:T(8,128)S(1)}, f32[10,64,128]{2,1,0:T(8,128)S(1)}, u32[]{:S(2)}, u32[]{:S(2)}) collective-permute-start(f32[10,64,128]{2,1,0:T(8,128)S(1)} %get-tuple-element.39), channel_id=1, source_target_pairs={{1,0},{2,1},{3,2},{4,3},{5,4},{6,5},{7,6},{8,7},{9,8},{10,9},{11,1... | collective-permute-start | bytes 983048 | tf_op jit(solution)/shard_map/ppermute | solution.py:432
  10.5 3.1 %collective-permute-start.2 = (f32[1,4,8,64,128]{4,3,2,1,0:T(8,128)S(1)}, f32[1,4,8,64,128]{4,3,2,1,0:T(8,128)S(1)}, u32[]{:S(2)}, u32[]{:S(2)}) collective-permute-start(f32[1,4,8,64,128]{4,3,2,1,0:T(8,128)S(1)} %bitcast.3), channel_id=1, source_target_pairs={{32,0},{64,32},{96,64},{128,96},{160,128},{192,160},{224,192},{256... | collective-permute-start | bytes 3145736 | tf_op jit(solution)/shard_map/ppermute | solution.py:433
  13.6 1.9 %ahead.1 = (f32[8,64,128]{2,1,0:T(8,128)S(1)}, f32[8,64,128]{2,1,0:T(8,128)S(1)}, f32[7,64,128]{2,1,0:T(8,128)S(1)}, f32[4,8,64,128]{3,2,1,0:T(8,128)S(1)}, f32[...) custom-call(f32[4,3]{1,0:T(4,128)} %cond_in.5, f32[1]{0:T(128)} %bitcast.flag, ...), custom_call_target="tpu_custom_call" | custom-call | tf_op jit(solution)/shard_map/ahead/pallas_call | solution.py:434
  15.6 4.5 %collective-permute-done.low = f32[10,64,128]{2,1,0:T(8,128)S(1)} collective-permute-done((f32[10,64,128]{2,1,0:T(8,128)S(1)}, f32[10,64,128]{2,1,0:T(8,128)S(1)}, u32[]{:S(2)}, u32[]{:S(2)}) %collective-permute-start) | collective-permute-done | bytes 327712 | tf_op jit(solution)/shard_map/ppermute | solution.py:431
  20.1 3.6 %collective-permute-done.1.high = f32[10,64,128]{2,1,0:T(8,128)S(1)} collective-permute-done((f32[10,64,128]{2,1,0:T(8,128)S(1)}, f32[10,64,128]{2,1,0:T(8,128)S(1)}, u32[]{:S(2)}, u32[]{:S(2)}) %collective-permute-start.1) | collective-permute-done | bytes 327712 | tf_op jit(solution)/shard_map/ppermute | solution.py:432
  23.7 2.2 %forward.1 = (f32[4,8,64,128]{3,2,1,0:T(8,128)S(1)}, f32[4,8,64,128]{3,2,1,0:T(8,128)S(1)}, f32[4,8,64,128]{3,2,1,0:T(8,128)S(1)}, f32[4,8,64,128]{3,2,1,0:T(8,128)S(1)}, f32[2,7,64,128]{3,2,1,0:T(8,128)S(1)}) custom-call(f32[4,3]{1,0:T(4,128)} %cond_in.5, f32[1]{0:T(128)} %bitcast.flag, f32[4,8,64,128]{3,2,1,0:T(8,128)S(1)} %get-tuple-element.27.starts, ...), custom_call_target="tpu_custom_call" | custom-call | tf_op jit(solution)/shard_map/forward/pallas_call | solution.py:441
  26.0 14.6 %collective-permute-start.3 = (f32[1,4,8,64,128]{4,3,2,1,0:T(8,128)S(1)}, f32[1,4,8,64,128]{4,3,2,1,0:T(8,128)S(1)}, u32[]{:S(2)}, u32[]{:S(2)}) collective-permute-start(f32[1,4,8,64,128]{4,3,2,1,0:T(8,128)S(1)} %bitcast.4), channel_id=1, source_target_pairs={{0,32},{32,64},{64,96},{96,128},{128,160},{160,192},{192,224},{224... | collective-permute-start | bytes 3145736 | tf_op jit(solution)/shard_map/ppermute | solution.py:448
  40.6 0.0 collective-permute-done.2.following
  40.6 0.8 %send.1 = (f32[4,8,64,128]{3,2,1,0:T(8,128)S(1)}, f32[4,64,128]{2,1,0:T(8,128)S(1)}, f32[4,64,128]{2,1,0:T(8,128)S(1)}) custom-call(f32[4,8,64,128]{3,2,1,0:T(8,128)S(1)} %get-tuple-element.40.ends, f32[1,4,8,64,128]{4,3,2,1,0:T(8,128)S(1)} %collective-permute-done.2.following, f32[4,8,64,128]{3,2,1,0:T(8,128)S(1)} %get-tuple-element.27.starts, ...), custom_call_target="tpu_custom_call" | custom-call | tf_op jit(solution)/shard_map/send/pallas_call | solution.py:450
  41.4 3.8 %collective-permute-start.5 = (f32[4,64,128]{2,1,0:T(8,128)S(1)}, f32[4,64,128]{2,1,0:T(8,128)S(1)}, u32[]{:S(2)}, u32[]{:S(2)}) collective-permute-start(f32[4,64,128]{2,1,0:T(8,128)S(1)} %get-tuple-element.51), channel_id=1, source_target_pairs={{1,0},{2,1},{3,2},{4,3},{5,4},{6,5},{7,6},{8,7},{9,8},{10,9},{11,1... | collective-permute-start | bytes 393224 | tf_op jit(solution)/shard_map/ppermute | solution.py:454
  45.2 3.0 %collective-permute-start.4 = (f32[4,64,128]{2,1,0:T(8,128)S(1)}, f32[4,64,128]{2,1,0:T(8,128)S(1)}, u32[]{:S(2)}, u32[]{:S(2)}) collective-permute-start(f32[4,64,128]{2,1,0:T(8,128)S(1)} %get-tuple-element.45.gate), channel_id=1, source_target_pairs={{0,1},{1,2},{2,3},{3,4},{4,5},{5,6},{6,7},{7,8},{8,9},{9,10},{10,1... | collective-permute-start | bytes 393224 | tf_op jit(solution)/shard_map/ppermute | solution.py:453
  48.2 1.0 %back.1 = (f32[4,8,64,128]{3,2,1,0:T(8,128)S(1)}, f32[4,8,64,128]{3,2,1,0:T(8,128)S(1)}, f32[4,8,64,128]{3,2,1,0:T(8,128)S(1)}, f32[4,8,64,128]{3,2,1,0:T(8,128)S(1)}) custom-call(f32[4,8,64,128]{3,2,1,0:T(8,128)S(1)} %get-tuple-element.44.gap, f32[4,8,64,128]{3,2,1,0:T(8,128)S(1)} %get-tuple-element.27.starts, f32[4,8,64,128]{3,2,1,0:T(8,128)S(1)} %get-tuple-element.34.p1, ...), custom_call_target="tpu_custom_call" | custom-call | tf_op jit(solution)/shard_map/back/pallas_call | solution.py:455
  49.2 10.3 %collective-permute-done.5.high = f32[4,64,128]{2,1,0:T(8,128)S(1)} collective-permute-done((f32[4,64,128]{2,1,0:T(8,128)S(1)}, f32[4,64,128]{2,1,0:T(8,128)S(1)}, u32[]{:S(2)}, u32[]{:S(2)}) %collective-permute-start.5) | collective-permute-done | bytes 131104 | tf_op jit(solution)/shard_map/ppermute | solution.py:454
  59.5 0.0 collective-permute-done.4.low
  59.6 0.0 collective-permute-done.3.before
  59.6 2.8 %pull.1 = (f32[1,4,8,64,128]{4,3,2,1,0:T(8,128)}, f32[1,4,8,64,128]{4,3,2,1,0:T(8,128)}) custom-call(f32[4,8,64,128]{3,2,1,0:T(8,128)S(1)} %get-tuple-element.27.starts, f32[4,8,64,128]{3,2,1,0:T(8,128)S(1)} %get-tuple-element.44.gap, f32[1,4,8,64,128]{4,3,2,1,0:T(8,128)S(1)} %collective-permute-done.3.before, f32[4,8,64,128]{3,2,1,0:T(8,128)S(1)} %get-tuple-element.34.p1, ...), custom_call_target="tpu_custom_call" | custom-call | tf_op jit(solution)/shard_map/pull/pallas_call | solution.py:456
Async XLA Ops:
  2.8 17.3 %collective-permute-start = (f32[10,64,128]{2,1,0:T(8,128)S(1)}, f32[10,64,128]{2,1,0:T(8,128)S(1)}, u32[]{:S(2)}, u32[]{:S(2)}) collective-permute-start(f32[10,64,128]{2,1,0:T(8,128)S(1)} %get-tuple-element.38), channel_id=1, source_target_pairs={{0,1},{1,2},{2,3},{3,4},{4,5},{5,6},{6,7},{7,8},{8,9},{9,10},{10,1... | collective-permute-start | bytes 983048 | tf_op jit(solution)/shard_map/ppermute | solution.py:431
  6.7 17.0 %collective-permute-start.1 = (f32[10,64,128]{2,1,0:T(8,128)S(1)}, f32[10,64,128]{2,1,0:T(8,128)S(1)}, u32[]{:S(2)}, u32[]{:S(2)}) collective-permute-start(f32[10,64,128]{2,1,0:T(8,128)S(1)} %get-tuple-element.39), channel_id=1, source_target_pairs={{1,0},{2,1},{3,2},{4,3},{5,4},{6,5},{7,6},{8,7},{9,8},{10,9},{11,1... | collective-permute-start | bytes 983048 | tf_op jit(solution)/shard_map/ppermute | solution.py:432
  10.5 30.1 %collective-permute-start.2 = (f32[1,4,8,64,128]{4,3,2,1,0:T(8,128)S(1)}, f32[1,4,8,64,128]{4,3,2,1,0:T(8,128)S(1)}, u32[]{:S(2)}, u32[]{:S(2)}) collective-permute-start(f32[1,4,8,64,128]{4,3,2,1,0:T(8,128)S(1)} %bitcast.3), channel_id=1, source_target_pairs={{32,0},{64,32},{96,64},{128,96},{160,128},{192,160},{224,192},{256... | collective-permute-start | bytes 3145736 | tf_op jit(solution)/shard_map/ppermute | solution.py:433
  26.0 33.6 %collective-permute-start.3 = (f32[1,4,8,64,128]{4,3,2,1,0:T(8,128)S(1)}, f32[1,4,8,64,128]{4,3,2,1,0:T(8,128)S(1)}, u32[]{:S(2)}, u32[]{:S(2)}) collective-permute-start(f32[1,4,8,64,128]{4,3,2,1,0:T(8,128)S(1)} %bitcast.4), channel_id=1, source_target_pairs={{0,32},{32,64},{64,96},{96,128},{128,160},{160,192},{192,224},{224... | collective-permute-start | bytes 3145736 | tf_op jit(solution)/shard_map/ppermute | solution.py:448
  41.4 18.1 %collective-permute-start.5 = (f32[4,64,128]{2,1,0:T(8,128)S(1)}, f32[4,64,128]{2,1,0:T(8,128)S(1)}, u32[]{:S(2)}, u32[]{:S(2)}) collective-permute-start(f32[4,64,128]{2,1,0:T(8,128)S(1)} %get-tuple-element.51), channel_id=1, source_target_pairs={{1,0},{2,1},{3,2},{4,3},{5,4},{6,5},{7,6},{8,7},{9,8},{10,9},{11,1... | collective-permute-start | bytes 393224 | tf_op jit(solution)/shard_map/ppermute | solution.py:454
  45.2 14.4 %collective-permute-start.4 = (f32[4,64,128]{2,1,0:T(8,128)S(1)}, f32[4,64,128]{2,1,0:T(8,128)S(1)}, u32[]{:S(2)}, u32[]{:S(2)}) collective-permute-start(f32[4,64,128]{2,1,0:T(8,128)S(1)} %get-tuple-element.45.gate), channel_id=1, source_target_pairs={{0,1},{1,2},{2,3},{3,4},{4,5},{5,6},{6,7},{7,8},{8,9},{9,10},{10,1... | collective-permute-start | bytes 393224 | tf_op jit(solution)/shard_map/ppermute | solution.py:453

commit v4 on v3

--- a/solution.py
+++ b/solution.py
@@ -8,7 +8,8 @@
 DEEP = 8
 NX = 64
 NY = 128
-V0, P1, G1, G2, G3, Q2, Q3, FIB, TIS, WIN = range(10)
+V0, P1, G1, G2, G3, Q2, Q3 = range(7)
+FIB, TIS, WIN = range(3)
 C_W01, C_WIN, C_WX, C_WY, C_D2, C_E, C_D1 = range(7)
 HALF_STEP = 0.15 * 0.5
 
@@ -70,7 +71,8 @@
 
 
 def edge_kernel(
-    cond_in, flag, starts_in, tissue_in, fibers_in, pacing_in, up, down, starts, tissue, fibers, pacing, cond, sems
+    cond_in, flag, starts_in, tissue_in, fibers_in, pacing_in,
+    up, down, up_tissue, down_tissue, starts, tissue, fibers, pacing, cond, sems,
 ):
     fetch(
         [
@@ -82,7 +84,10 @@
         ],
         sems,
     )
-    for out, (b1, b2, b3, b4) in ((up, (7, 6, 5, 4)), (down, (0, 1, 2, 3))):
+    for out, out_tissue, (b1, b2, b3, b4) in (
+        (up, up_tissue, (7, 6, 5, 4)),
+        (down, down_tissue, (0, 1, 2, 3)),
+    ):
         share = [tissue[b].astype(jnp.float32) for b in (b1, b2, b3, b4)]
         sig0 = [sigma(cond, fibers[b], 0) for b in (b1, b2, b3, b4)]
         wz = [face_weight(sig0[i], share[i], sig0[i + 1], share[i + 1]) for i in range(3)]
@@ -108,9 +113,9 @@
         rest = v1_b2 + cross(v1_b2, wx[1], wy[1]) + reaction(v1_b2, *gates_next(v[1], *g[1])) + stim[1]
         rest = rest + wz[1] * (v1_b3 - v1_b2) - wz[0] * v1_b2
         out[Q3] = wz[0] * rest + stim[0]
-        out[FIB] = fibers[b1].astype(jnp.float32)
-        out[TIS] = share[0]
-        out[WIN] = wz[0]
+        out_tissue[FIB] = fibers[b1].astype(jnp.float32)
+        out_tissue[TIS] = share[0]
+        out_tissue[WIN] = wz[0]
 
 
 class Fields:
@@ -176,16 +181,16 @@
 
 
 def forward_kernel(
-    cond_in, flag, starts, tissue, fibers, pacing, wx, wy, wz, p1, p2, p3, p4, low, high,
+    cond_in, flag, starts, tissue, fibers, pacing, wx, wy, wz, p1, p2, p3, p4, low, high, low_tissue, high_tissue,
     f1, f2, f3, f4, side, cond, sems,
 ):
     fetch([(cond_in, cond)], sems)
     halo = []
-    for n, (msg, own) in enumerate(((low, 0), (high, DEEP - 1))):
-        fib, tis = msg[FIB], msg[TIS]
+    for n, (msg, beside, own) in enumerate(((low, low_tissue, 0), (high, high_tissue, DEEP - 1))):
+        fib, tis = beside[FIB], beside[TIS]
         w01 = face_weight(sigma(cond, fib, 0), tis, sigma(cond, fibers[own], 0), tissue[own].astype(jnp.float32))
         side[n, C_W01] = w01
-        side[n, C_WIN] = msg[WIN]
+        side[n, C_WIN] = beside[WIN]
         side[n, C_WX] = cross_weight(sigma(cond, fib, 1), tis, 0)
         side[n, C_WY] = cross_weight(sigma(cond, fib, 2), tis, 1)
         halo.append(msg[V0])
@@ -404,6 +409,12 @@
     )
 
 
+def nearest(sections, slabs, pairs):
+    return [
+        ((k ^ 2) * slabs + source, k * slabs + target) for k in range(sections) for source, target in pairs
+    ]
+
+
 def body(starts, tissue, fibers, pacing, conductances):
     plane = (NX, NY)
     slab = (DEEP, *plane)
@@ -421,15 +432,17 @@
         pltpu.with_memory_space_constraint(arg, pltpu.HBM)
         for arg in (conductances, starts, tissue, fibers, pacing)
     )
-    up, down, own, tis, fib, pac = call(
+    up, down, up_tissue, down_tissue, own, tis, fib, pac = call(
         edge_kernel,
         "edge",
         [HBM, SM] + [HBM] * 4,
-        [f32(10, *plane)] * 2 + [fields] + [i32(*slab)] * 3,
+        [f32(7, *plane)] * 2 + [f32(3, *plane)] * 2 + [fields] + [i32(*slab)] * 3,
         [pltpu.SMEM((4, 3), jnp.float32), pltpu.SemaphoreType.DMA((5,))],
     )(conductances, flag, starts, tissue, fibers, pacing)
     low = lax.ppermute(up, "slab", upward)
     high = lax.ppermute(down, "slab", downward)
+    low_tissue = lax.ppermute(up_tissue, ("tm", "slab"), nearest(sections, slabs, upward))
+    high_tissue = lax.ppermute(down_tissue, ("tm", "slab"), nearest(sections, slabs, downward))
     following = lax.ppermute(own[None], "tm", earlier)
     wx, wy, wz, p1, p2, p3, p4 = call(
         ahead_kernel,
@@ -441,10 +454,10 @@
     f1, f2, f3, ends, side = call(
         forward_kernel,
         "forward",
-        [HBM, SM] + [VM] * 13,
+        [HBM, SM] + [VM] * 15,
         [fields] * 4 + [f32(2, 7, *plane)],
         few,
-    )(conductances, flag, own, tis, fib, pac, wx, wy, wz, p1, p2, p3, p4, low, high)
+    )(conductances, flag, own, tis, fib, pac, wx, wy, wz, p1, p2, p3, p4, low, high, low_tissue, high_tissue)
     before = lax.ppermute(ends[None], "tm", later)
     history = (own, p1, p2, p3, f1, f2, f3)
     gap, up, down = call(

time: 62.7 us -> 61 us (0.973)
  the two profiles are of different devices: /device:TPU:425 before, /device:TPU:225 now
where the time goes in v4:
time: 61 us; the launch traced here: 60.6 us
  starting transfers between devices  29.4 us (48%)
  waiting for transfers between devices  19.5 us (32%)
  Pallas kernels  11 us (18%)
  between operations  0.76 us (1%)
    ppermute x2, waiting for transfers between devices, body(): high = lax.ppermute(down, 'slab', downward)  16.3 us
    ppermute x2, starting transfers between devices, body(): low = lax.ppermute(up, 'slab', upward)  10.8 us
    ppermute x2, starting transfers between devices, body(): high = lax.ppermute(down, 'slab', downward)  6.15 us
    ppermute x1, starting transfers between devices, body(): lax.ppermute(up_tissue, ('tm', 'slab'), nearest(sections, slabs, upward))  4.03 us
    ppermute x1, starting transfers between devices, body(): lax.ppermute(down_tissue, ('tm', 'slab'), nearest(sections, slabs, downwa...  3.37 us
    ppermute x1, waiting for transfers between devices, body(): lax.ppermute(down_tissue, ('tm', 'slab'), nearest(sections, slabs, downwa...  3.2 us
    ppermute x1, starting transfers between devices, body(): following = lax.ppermute(own[None], 'tm', earlier)  3.14 us
    pallas_call x1, Pallas kernels, body(): call(pull_kernel, 'pull', [VM] * 19, [f32(1, 4, *slab)] * 2, [pltpu.VMEM(...  2.87 us
  transfers between devices with their start and end apart: 8, of which 3 were waited for; matrix products, arithmetic and copies ran while one was open for 0% of the time, Pallas kernels for 9%

profile of v4, /device:TPU:225, one launch (start us, length us, event | category | flops | bytes accessed | tf_op | source)
XLA Modules:
  0.0 60.6 jit_solution(18248291631683467638)
XLA Ops:
  0.6 2.1 %edge.1 = (f32[7,64,128]{2,1,0:T(8,128)S(1)}, f32[7,64,128]{2,1,0:T(8,128)S(1)}, f32[3,64,128]{2,1,0:T(8,128)S(1)}, f32[3,64,128]{2,1,0:T(8,128)S(1)}, f32[4,8,6...) custom-call(f32[4,3]{1,0:T(4,128)} %cond_in.5, ...), custom_call_target="tpu_custom_call" | custom-call | tf_op jit(solution)/shard_map/edge/pallas_call | solution.py:435
  2.8 4.8 %collective-permute-start = (f32[7,64,128]{2,1,0:T(8,128)S(1)}, f32[7,64,128]{2,1,0:T(8,128)S(1)}, u32[]{:S(2)}, u32[]{:S(2)}) collective-permute-start(f32[7,64,128]{2,1,0:T(8,128)S(1)} %get-tuple-element.40), channel_id=1, source_target_pairs={{0,1},{1,2},{2,3},{3,4},{4,5},{5,6},{6,7},{7,8},{8,9},{9,10},{10,1... | collective-permute-start | bytes 688136 | tf_op jit(solution)/shard_map/ppermute | solution.py:442
  7.6 2.9 %collective-permute-start.1 = (f32[7,64,128]{2,1,0:T(8,128)S(1)}, f32[7,64,128]{2,1,0:T(8,128)S(1)}, u32[]{:S(2)}, u32[]{:S(2)}) collective-permute-start(f32[7,64,128]{2,1,0:T(8,128)S(1)} %get-tuple-element.41), channel_id=1, source_target_pairs={{1,0},{2,1},{3,2},{4,3},{5,4},{6,5},{7,6},{8,7},{9,8},{10,9},{11,1... | collective-permute-start | bytes 688136 | tf_op jit(solution)/shard_map/ppermute | solution.py:443
  10.5 3.1 %collective-permute-start.4 = (f32[1,4,8,64,128]{4,3,2,1,0:T(8,128)S(1)}, f32[1,4,8,64,128]{4,3,2,1,0:T(8,128)S(1)}, u32[]{:S(2)}, u32[]{:S(2)}) collective-permute-start(f32[1,4,8,64,128]{4,3,2,1,0:T(8,128)S(1)} %bitcast.3), channel_id=1, source_target_pairs={{32,0},{64,32},{96,64},{128,96},{160,128},{192,160},{224,192},{256... | collective-permute-start | bytes 3145736 | tf_op jit(solution)/shard_map/ppermute | solution.py:446
  13.6 4.0 %collective-permute-start.2 = (f32[3,64,128]{2,1,0:T(8,128)S(1)}, f32[3,64,128]{2,1,0:T(8,128)S(1)}, u32[]{:S(2)}, u32[]{:S(2)}) collective-permute-start(f32[3,64,128]{2,1,0:T(8,128)S(1)} %get-tuple-element.42), channel_id=1, source_target_pairs={{64,1},{65,2},{66,3},{67,4},{68,5},{69,6},{70,7},{71,8},{72,9},{73... | collective-permute-start | bytes 294920 | tf_op jit(solution)/shard_map/ppermute | solution.py:444
  17.7 3.4 %collective-permute-start.3 = (f32[3,64,128]{2,1,0:T(8,128)S(1)}, f32[3,64,128]{2,1,0:T(8,128)S(1)}, u32[]{:S(2)}, u32[]{:S(2)}) collective-permute-start(f32[3,64,128]{2,1,0:T(8,128)S(1)} %get-tuple-element.43), channel_id=1, source_target_pairs={{65,0},{66,1},{67,2},{68,3},{69,4},{70,5},{71,6},{72,7},{73,8},{74... | collective-permute-start | bytes 294920 | tf_op jit(solution)/shard_map/ppermute | solution.py:445
  21.0 1.9 %ahead.1 = (f32[8,64,128]{2,1,0:T(8,128)S(1)}, f32[8,64,128]{2,1,0:T(8,128)S(1)}, f32[7,64,128]{2,1,0:T(8,128)S(1)}, f32[4,8,64,128]{3,2,1,0:T(8,128)S(1)}, f32[...) custom-call(f32[4,3]{1,0:T(4,128)} %cond_in.5, f32[1]{0:T(128)} %bitcast.flag, ...), custom_call_target="tpu_custom_call" | custom-call | tf_op jit(solution)/shard_map/ahead/pallas_call | solution.py:447
  23.0 0.0 collective-permute-done.2.low_tissue
  23.0 3.2 %collective-permute-done.3.high_tissue = f32[3,64,128]{2,1,0:T(8,128)S(1)} collective-permute-done((f32[3,64,128]{2,1,0:T(8,128)S(1)}, f32[3,64,128]{2,1,0:T(8,128)S(1)}, u32[]{:S(2)}, u32[]{:S(2)}) %collective-permute-start.3) | collective-permute-done | bytes 98336 | tf_op jit(solution)/shard_map/ppermute | solution.py:445
  26.2 0.0 collective-permute-done.low
  26.2 4.2 %collective-permute-done.1.high = f32[7,64,128]{2,1,0:T(8,128)S(1)} collective-permute-done((f32[7,64,128]{2,1,0:T(8,128)S(1)}, f32[7,64,128]{2,1,0:T(8,128)S(1)}, u32[]{:S(2)}, u32[]{:S(2)}) %collective-permute-start.1) | collective-permute-done | bytes 229408 | tf_op jit(solution)/shard_map/ppermute | solution.py:443
  30.4 2.2 %forward.1 = (f32[4,8,64,128]{3,2,1,0:T(8,128)S(1)}, f32[4,8,64,128]{3,2,1,0:T(8,128)S(1)}, f32[4,8,64,128]{3,2,1,0:T(8,128)S(1)}, f32[4,8,64,128]{3,2,1,0:T(8,128)S(1)}, f32[2,7,64,128]{3,2,1,0:T(8,128)S(1)}) custom-call(f32[4,3]{1,0:T(4,128)} %cond_in.5, f32[1]{0:T(128)} %bitcast.flag, f32[4,8,64,128]{3,2,1,0:T(8,128)S(1)} %get-tuple-element.29.starts, ...), custom_call_target="tpu_custom_call" | custom-call | tf_op jit(solution)/shard_map/forward/pallas_call | solution.py:454
  32.6 1.9 %collective-permute-start.5 = (f32[1,4,8,64,128]{4,3,2,1,0:T(8,128)S(1)}, f32[1,4,8,64,128]{4,3,2,1,0:T(8,128)S(1)}, u32[]{:S(2)}, u32[]{:S(2)}) collective-permute-start(f32[1,4,8,64,128]{4,3,2,1,0:T(8,128)S(1)} %bitcast.4), channel_id=1, source_target_pairs={{0,32},{32,64},{64,96},{96,128},{128,160},{160,192},{192,224},{224... | collective-permute-start | bytes 3145736 | tf_op jit(solution)/shard_map/ppermute | solution.py:461
  34.5 0.0 collective-permute-done.4.following
  34.5 0.8 %send.1 = (f32[4,8,64,128]{3,2,1,0:T(8,128)S(1)}, f32[4,64,128]{2,1,0:T(8,128)S(1)}, f32[4,64,128]{2,1,0:T(8,128)S(1)}) custom-call(f32[4,8,64,128]{3,2,1,0:T(8,128)S(1)} %get-tuple-element.44.ends, f32[1,4,8,64,128]{4,3,2,1,0:T(8,128)S(1)} %collective-permute-done.4.following, f32[4,8,64,128]{3,2,1,0:T(8,128)S(1)} %get-tuple-element.29.starts, ...), custom_call_target="tpu_custom_call" | custom-call | tf_op jit(solution)/shard_map/send/pallas_call | solution.py:463
  35.4 3.3 %collective-permute-start.7 = (f32[4,64,128]{2,1,0:T(8,128)S(1)}, f32[4,64,128]{2,1,0:T(8,128)S(1)}, u32[]{:S(2)}, u32[]{:S(2)}) collective-permute-start(f32[4,64,128]{2,1,0:T(8,128)S(1)} %get-tuple-element.55), channel_id=1, source_target_pairs={{1,0},{2,1},{3,2},{4,3},{5,4},{6,5},{7,6},{8,7},{9,8},{10,9},{11,1... | collective-permute-start | bytes 393224 | tf_op jit(solution)/shard_map/ppermute | solution.py:467
  38.7 6.0 %collective-permute-start.6 = (f32[4,64,128]{2,1,0:T(8,128)S(1)}, f32[4,64,128]{2,1,0:T(8,128)S(1)}, u32[]{:S(2)}, u32[]{:S(2)}) collective-permute-start(f32[4,64,128]{2,1,0:T(8,128)S(1)} %get-tuple-element.49.gate), channel_id=1, source_target_pairs={{0,1},{1,2},{2,3},{3,4},{4,5},{5,6},{6,7},{7,8},{8,9},{9,10},{10,1... | collective-permute-start | bytes 393224 | tf_op jit(solution)/shard_map/ppermute | solution.py:466
  44.7 1.0 %back.1 = (f32[4,8,64,128]{3,2,1,0:T(8,128)S(1)}, f32[4,8,64,128]{3,2,1,0:T(8,128)S(1)}, f32[4,8,64,128]{3,2,1,0:T(8,128)S(1)}, f32[4,8,64,128]{3,2,1,0:T(8,128)S(1)}) custom-call(f32[4,8,64,128]{3,2,1,0:T(8,128)S(1)} %get-tuple-element.48.gap, f32[4,8,64,128]{3,2,1,0:T(8,128)S(1)} %get-tuple-element.29.starts, f32[4,8,64,128]{3,2,1,0:T(8,128)S(1)} %get-tuple-element.36.p1, ...), custom_call_target="tpu_custom_call" | custom-call | tf_op jit(solution)/shard_map/back/pallas_call | solution.py:468
  45.7 12.1 %collective-permute-done.7.high = f32[4,64,128]{2,1,0:T(8,128)S(1)} collective-permute-done((f32[4,64,128]{2,1,0:T(8,128)S(1)}, f32[4,64,128]{2,1,0:T(8,128)S(1)}, u32[]{:S(2)}, u32[]{:S(2)}) %collective-permute-start.7) | collective-permute-done | bytes 131104 | tf_op jit(solution)/shard_map/ppermute | solution.py:467
  57.8 0.0 collective-permute-done.6.low
  57.8 0.0 collective-permute-done.5.before
  57.8 2.9 %pull.1 = (f32[1,4,8,64,128]{4,3,2,1,0:T(8,128)}, f32[1,4,8,64,128]{4,3,2,1,0:T(8,128)}) custom-call(f32[4,8,64,128]{3,2,1,0:T(8,128)S(1)} %get-tuple-element.29.starts, f32[4,8,64,128]{3,2,1,0:T(8,128)S(1)} %get-tuple-element.48.gap, f32[1,4,8,64,128]{4,3,2,1,0:T(8,128)S(1)} %collective-permute-done.5.before, f32[4,8,64,128]{3,2,1,0:T(8,128)S(1)} %get-tuple-element.36.p1, ...), custom_call_target="tpu_custom_call" | custom-call | tf_op jit(solution)/shard_map/pull/pallas_call | solution.py:469
Async XLA Ops:
  2.8 23.4 %collective-permute-start = (f32[7,64,128]{2,1,0:T(8,128)S(1)}, f32[7,64,128]{2,1,0:T(8,128)S(1)}, u32[]{:S(2)}, u32[]{:S(2)}) collective-permute-start(f32[7,64,128]{2,1,0:T(8,128)S(1)} %get-tuple-element.40), channel_id=1, source_target_pairs={{0,1},{1,2},{2,3},{3,4},{4,5},{5,6},{6,7},{7,8},{8,9},{9,10},{10,1... | collective-permute-start | bytes 688136 | tf_op jit(solution)/shard_map/ppermute | solution.py:442
  7.6 22.8 %collective-permute-start.1 = (f32[7,64,128]{2,1,0:T(8,128)S(1)}, f32[7,64,128]{2,1,0:T(8,128)S(1)}, u32[]{:S(2)}, u32[]{:S(2)}) collective-permute-start(f32[7,64,128]{2,1,0:T(8,128)S(1)} %get-tuple-element.41), channel_id=1, source_target_pairs={{1,0},{2,1},{3,2},{4,3},{5,4},{6,5},{7,6},{8,7},{9,8},{10,9},{11,1... | collective-permute-start | bytes 688136 | tf_op jit(solution)/shard_map/ppermute | solution.py:443
  10.5 24.1 %collective-permute-start.4 = (f32[1,4,8,64,128]{4,3,2,1,0:T(8,128)S(1)}, f32[1,4,8,64,128]{4,3,2,1,0:T(8,128)S(1)}, u32[]{:S(2)}, u32[]{:S(2)}) collective-permute-start(f32[1,4,8,64,128]{4,3,2,1,0:T(8,128)S(1)} %bitcast.3), channel_id=1, source_target_pairs={{32,0},{64,32},{96,64},{128,96},{160,128},{192,160},{224,192},{256... | collective-permute-start | bytes 3145736 | tf_op jit(solution)/shard_map/ppermute | solution.py:446
  13.6 9.4 %collective-permute-start.2 = (f32[3,64,128]{2,1,0:T(8,128)S(1)}, f32[3,64,128]{2,1,0:T(8,128)S(1)}, u32[]{:S(2)}, u32[]{:S(2)}) collective-permute-start(f32[3,64,128]{2,1,0:T(8,128)S(1)} %get-tuple-element.42), channel_id=1, source_target_pairs={{64,1},{65,2},{66,3},{67,4},{68,5},{69,6},{70,7},{71,8},{72,9},{73... | collective-permute-start | bytes 294920 | tf_op jit(solution)/shard_map/ppermute | solution.py:444
  17.7 8.5 %collective-permute-start.3 = (f32[3,64,128]{2,1,0:T(8,128)S(1)}, f32[3,64,128]{2,1,0:T(8,128)S(1)}, u32[]{:S(2)}, u32[]{:S(2)}) collective-permute-start(f32[3,64,128]{2,1,0:T(8,128)S(1)} %get-tuple-element.43), channel_id=1, source_target_pairs={{65,0},{66,1},{67,2},{68,3},{69,4},{70,5},{71,6},{72,7},{73,8},{74... | collective-permute-start | bytes 294920 | tf_op jit(solution)/shard_map/ppermute | solution.py:445
  32.6 25.2 %collective-permute-start.5 = (f32[1,4,8,64,128]{4,3,2,1,0:T(8,128)S(1)}, f32[1,4,8,64,128]{4,3,2,1,0:T(8,128)S(1)}, u32[]{:S(2)}, u32[]{:S(2)}) collective-permute-start(f32[1,4,8,64,128]{4,3,2,1,0:T(8,128)S(1)} %bitcast.4), channel_id=1, source_target_pairs={{0,32},{32,64},{64,96},{96,128},{128,160},{160,192},{192,224},{224... | collective-permute-start | bytes 3145736 | tf_op jit(solution)/shard_map/ppermute | solution.py:461
  35.4 22.4 %collective-permute-start.7 = (f32[4,64,128]{2,1,0:T(8,128)S(1)}, f32[4,64,128]{2,1,0:T(8,128)S(1)}, u32[]{:S(2)}, u32[]{:S(2)}) collective-permute-start(f32[4,64,128]{2,1,0:T(8,128)S(1)} %get-tuple-element.55), channel_id=1, source_target_pairs={{1,0},{2,1},{3,2},{4,3},{5,4},{6,5},{7,6},{8,7},{9,8},{10,9},{11,1... | collective-permute-start | bytes 393224 | tf_op jit(solution)/shard_map/ppermute | solution.py:467
  38.7 19.1 %collective-permute-start.6 = (f32[4,64,128]{2,1,0:T(8,128)S(1)}, f32[4,64,128]{2,1,0:T(8,128)S(1)}, u32[]{:S(2)}, u32[]{:S(2)}) collective-permute-start(f32[4,64,128]{2,1,0:T(8,128)S(1)} %get-tuple-element.49.gate), channel_id=1, source_target_pairs={{0,1},{1,2},{2,3},{3,4},{4,5},{5,6},{6,7},{7,8},{8,9},{9,10},{10,1... | collective-permute-start | bytes 393224 | tf_op jit(solution)/shard_map/ppermute | solution.py:466

commit v5 on v4

--- a/solution.py
+++ b/solution.py
@@ -10,7 +10,8 @@
 NY = 128
 V0, P1, G1, G2, G3, Q2, Q3 = range(7)
 FIB, TIS, WIN = range(3)
-C_W01, C_WIN, C_WX, C_WY, C_D2, C_E, C_D1 = range(7)
+C_W01, C_WIN, C_WX, C_WY = range(4)
+C_D2, C_E, C_D1 = range(3)
 HALF_STEP = 0.15 * 0.5
 
 
@@ -144,6 +145,18 @@
     return [i for i in range(DEEP) if not rim <= i < DEEP - rim]
 
 
+def rim_kernel(cond_in, tissue, fibers, low_tissue, high_tissue, rim, cond, sems):
+    fetch([(cond_in, cond)], sems)
+    for n, (beside, own) in enumerate(((low_tissue, 0), (high_tissue, DEEP - 1))):
+        fib, tis = beside[FIB], beside[TIS]
+        rim[n, C_W01] = face_weight(
+            sigma(cond, fib, 0), tis, sigma(cond, fibers[own], 0), tissue[own].astype(jnp.float32)
+        )
+        rim[n, C_WIN] = beside[WIN]
+        rim[n, C_WX] = cross_weight(sigma(cond, fib, 1), tis, 0)
+        rim[n, C_WY] = cross_weight(sigma(cond, fib, 2), tis, 1)
+
+
 def ahead_kernel(cond_in, flag, starts, tissue, fibers, pacing, wx, wy, wz, f1, f2, f3, f4, cond, sems):
     fetch([(cond_in, cond)], sems)
     before = None
@@ -181,22 +194,14 @@
 
 
 def forward_kernel(
-    cond_in, flag, starts, tissue, fibers, pacing, wx, wy, wz, p1, p2, p3, p4, low, high, low_tissue, high_tissue,
-    f1, f2, f3, f4, side, cond, sems,
+    flag, starts, pacing, wx, wy, wz, rim, p1, p2, p3, p4, low, high,
+    f1, f2, f3, f4, side,
 ):
-    fetch([(cond_in, cond)], sems)
     halo = []
-    for n, (msg, beside, own) in enumerate(((low, low_tissue, 0), (high, high_tissue, DEEP - 1))):
-        fib, tis = beside[FIB], beside[TIS]
-        w01 = face_weight(sigma(cond, fib, 0), tis, sigma(cond, fibers[own], 0), tissue[own].astype(jnp.float32))
-        side[n, C_W01] = w01
-        side[n, C_WIN] = beside[WIN]
-        side[n, C_WX] = cross_weight(sigma(cond, fib, 1), tis, 0)
-        side[n, C_WY] = cross_weight(sigma(cond, fib, 2), tis, 1)
-        halo.append(msg[V0])
-        inflow = w01 * (msg[V0] - starts[0, own])
+    for n, (msg, own) in enumerate(((low, 0), (high, DEEP - 1))):
+        inflow = rim[n, C_W01] * (msg[V0] - starts[0, own])
         f1[0, own] = p1[0, own] + inflow
-        halo[n] = msg[P1] - inflow
+        halo.append(msg[P1] - inflow)
         side[n, C_D1] = halo[n]
     fields = forward_fields(starts, (p1, p2, p3), (f1, f2, f3))
     for n in range(1, 4):
@@ -213,13 +218,13 @@
                 for n, gate in enumerate(gates_next(v, *g)):
                     new[n + 1, i] = gate
             if i == 0:
-                below = outflow[0] = side[0, C_W01] * (v - halo[0])
+                below = outflow[0] = rim[0, C_W01] * (v - halo[0])
             elif above is not None:
                 below = above
             else:
                 below = wz[i - 1] * (v - old.plane(0, i - 1))
             if i == DEEP - 1:
-                above = side[1, C_W01] * (halo[1] - v)
+                above = rim[1, C_W01] * (halo[1] - v)
                 outflow[1] = -above
             else:
                 above = wz[i] * (old.plane(0, i + 1) - v)
@@ -231,7 +236,7 @@
             continue
         for n, msg in enumerate((low, high)):
             v = halo[n]
-            win = side[n, C_WIN]
+            win = rim[n, C_WIN]
             g = [msg[G1], msg[G2], msg[G3]]
             if step == 1:
                 extra = msg[Q2]
@@ -248,7 +253,7 @@
                     - 0.2 * (1.0 - t2 * t2) * (0.3 * g[0] * (1.0 - v))
                     - 0.06 * (1.0 - t3 * t3) * (0.15 * v)
                 )
-            total = v + cross(v, side[n, C_WX], side[n, C_WY]) + reaction(v, *g)
+            total = v + cross(v, rim[n, C_WX], rim[n, C_WY]) + reaction(v, *g)
             halo[n] = total + (extra - win * v) + outflow[n]
 
 
@@ -314,15 +319,22 @@
         old = new
 
 
-def pull_kernel(
-    starts, gap, before, p1, p2, p3, f1, f2, f3, b1, b2, b3, b4, wx, wy, wz, side, low, high,
-    defect_out, gradient_out, work, defect, gradient, sems,
-):
+def defect_kernel(starts, before, defect_out, defect, sems):
+    copies = []
     for n in range(4):
         for i in range(DEEP):
             defect[n, i] = before[0, n, i] - starts[n, i]
-    copies = [pltpu.make_async_copy(defect, defect_out.at[0], sems.at[DEEP])]
-    copies[0].start()
+        copies.append(pltpu.make_async_copy(defect.at[n], defect_out.at[0, n], sems.at[n]))
+        copies[n].start()
+    for copy in copies:
+        copy.wait()
+
+
+def pull_kernel(
+    starts, gap, defect, p1, p2, p3, f1, f2, f3, b1, b2, b3, b4, wx, wy, wz, rim, side, low, high,
+    gradient_out, work, gradient, sems,
+):
+    copies = []
     fields = forward_fields(starts, (p1, p2, p3), (f1, f2, f3))
     adjoints = [Fields(gap, None, 0, 0)] + [
         Fields(b, work.at[j], j + 1, j) for j, b in enumerate((b1, b2, b3))
@@ -338,13 +350,13 @@
             a = old.all(i)
             f = fields[3 - m].all(i)
             if i == 0:
-                below = outflow[0] = side[0, C_W01] * (a[0] - halo[0])
+                below = outflow[0] = rim[0, C_W01] * (a[0] - halo[0])
             elif above is not None:
                 below = above
             else:
                 below = wz[i - 1] * (a[0] - old.plane(0, i - 1))
             if i == DEEP - 1:
-                above = side[1, C_W01] * (halo[1] - a[0])
+                above = rim[1, C_W01] * (halo[1] - a[0])
                 outflow[1] = -above
             else:
                 above = wz[i] * (old.plane(0, i + 1) - a[0])
@@ -368,7 +380,7 @@
         if m == 3:
             continue
         for n, msg in enumerate((low, high)):
-            win, px, py = side[n, C_WIN], side[n, C_WX], side[n, C_WY]
+            win, px, py = rim[n, C_WIN], rim[n, C_WX], rim[n, C_WY]
             if m == 0:
                 change = first[n] = outflow[n]
             else:
@@ -397,12 +409,12 @@
     return jax.ShapeDtypeStruct(shape, jnp.int32)
 
 
-def call(kernel, name, ins, outs, scratch=(), out_spec=VM):
+def call(kernel, name, ins, outs, scratch=(), out_specs=None):
     return pl.pallas_call(
         kernel,
         name=name,
         in_specs=ins,
-        out_specs=[out_spec] * len(outs),
+        out_specs=out_specs or [VM] * len(outs),
         out_shape=outs,
         scratch_shapes=list(scratch),
         compiler_params=pltpu.CompilerParams(vmem_limit_bytes=28 * 1024 * 1024),
@@ -426,7 +438,6 @@
     earlier = [((i + 1) % sections, i) for i in range(sections)]
     later = [(i, (i + 1) % sections) for i in range(sections)]
     flag = (lax.axis_index("tm") == 0).astype(jnp.float32).reshape(1)
-    few = [pltpu.SMEM((4, 3), jnp.float32), pltpu.SemaphoreType.DMA((1,))]
 
     conductances, starts, tissue, fibers, pacing = (
         pltpu.with_memory_space_constraint(arg, pltpu.HBM)
@@ -444,6 +455,7 @@
     low_tissue = lax.ppermute(up_tissue, ("tm", "slab"), nearest(sections, slabs, upward))
     high_tissue = lax.ppermute(down_tissue, ("tm", "slab"), nearest(sections, slabs, downward))
     following = lax.ppermute(own[None], "tm", earlier)
+    few = [pltpu.SMEM((4, 3), jnp.float32), pltpu.SemaphoreType.DMA((1,))]
     wx, wy, wz, p1, p2, p3, p4 = call(
         ahead_kernel,
         "ahead",
@@ -451,13 +463,15 @@
         [f32(*slab), f32(*slab), f32(DEEP - 1, *plane)] + [fields] * 4,
         few,
     )(conductances, flag, own, tis, fib, pac)
+    rim = call(rim_kernel, "rim", [HBM] + [VM] * 4, [f32(2, 4, *plane)], few)(
+        conductances, tis, fib, low_tissue, high_tissue
+    )[0]
     f1, f2, f3, ends, side = call(
         forward_kernel,
         "forward",
-        [HBM, SM] + [VM] * 15,
-        [fields] * 4 + [f32(2, 7, *plane)],
-        few,
-    )(conductances, flag, own, tis, fib, pac, wx, wy, wz, p1, p2, p3, p4, low, high, low_tissue, high_tissue)
+        [SM] + [VM] * 12,
+        [fields] * 4 + [f32(2, 3, *plane)],
+    )(flag, own, pac, wx, wy, wz, rim, p1, p2, p3, p4, low, high)
     before = lax.ppermute(ends[None], "tm", later)
     history = (own, p1, p2, p3, f1, f2, f3)
     gap, up, down = call(
@@ -466,16 +480,26 @@
     low = lax.ppermute(up, "slab", upward)
     high = lax.ppermute(down, "slab", downward)
     inner = call(back_kernel, "back", [VM] * 11 + [ANY], [fields] * 4)(gap, *history, wx, wy, wz, up)
-    defect, gradient = call(
+    defect, kept = call(
+        defect_kernel,
+        "defect",
+        [VM] * 2,
+        [f32(1, 4, *slab), fields],
+        [pltpu.SemaphoreType.DMA((4,))],
+        [ANY, VM],
+    )(own, before)
+    gradient = call(
         pull_kernel,
         "pull",
-        [VM] * 19,
-        [f32(1, 4, *slab)] * 2,
-        [pltpu.VMEM((3, 4, *slab), jnp.float32)]
-        + [pltpu.VMEM((4, *slab), jnp.float32)] * 2
-        + [pltpu.SemaphoreType.DMA((DEEP + 1,))],
-        ANY,
-    )(own, gap, before, p1, p2, p3, f1, f2, f3, *inner, wx, wy, wz, side, low, high)
+        [VM] * 20,
+        [f32(1, 4, *slab)],
+        [
+            pltpu.VMEM((3, 4, *slab), jnp.float32),
+            pltpu.VMEM((4, *slab), jnp.float32),
+            pltpu.SemaphoreType.DMA((DEEP,)),
+        ],
+        [ANY],
+    )(own, gap, kept, p1, p2, p3, f1, f2, f3, *inner, wx, wy, wz, rim, side, low, high)[0]
     return defect, gradient
 
 

time: 61 us -> 60.3 us (0.989)
  waiting for transfers between devices: 19.5 us -> 17.7 us
  starting transfers between devices: 29.4 us -> 30.3 us
    ppermute x2, waiting for transfers between devices: 16.3 us -> 10.4 us  [body(): high = lax.ppermute(down, 'slab', downward)]
    ppermute x1, waiting for transfers between devices: 0.01 us -> 3.97 us  [body(): before = lax.ppermute(ends[None], 'tm', later)]
    ppermute x2, starting transfers between devices: 6.15 us -> 7.02 us  [body(): high = lax.ppermute(down, 'slab', downward)]
    pallas_call x2 -> x4, Pallas kernels: 5.11 us -> 5.37 us  [the longest x1 2.33 us: body(): call(pull_kernel, 'pull', [VM] * 20, [f32(1, 4, *slab)], [pltpu.VMEM((3,...]
  transfers between devices with their start and end apart: 8 -> 8, of which waited for: 3 -> 4; matrix products, arithmetic and copies ran while one was open for 0% -> 0% of each run, Pallas kernels for 9% -> 10%
where the time goes in v5:
time: 60.3 us; the launch traced here: 59.9 us
  starting transfers between devices  30.3 us (50%)
  waiting for transfers between devices  17.7 us (29%)
  Pallas kernels  11.2 us (19%)
  between operations  0.78 us (1%)
    ppermute x2, starting transfers between devices, body(): low = lax.ppermute(up, 'slab', upward)  10.8 us
    ppermute x2, waiting for transfers between devices, body(): high = lax.ppermute(down, 'slab', downward)  10.4 us
    ppermute x2, starting transfers between devices, body(): high = lax.ppermute(down, 'slab', downward)  7.02 us
    ppermute x1, starting transfers between devices, body(): lax.ppermute(up_tissue, ('tm', 'slab'), nearest(sections, slabs, upward))  4.03 us
    ppermute x1, waiting for transfers between devices, body(): before = lax.ppermute(ends[None], 'tm', later)  3.97 us
    ppermute x1, starting transfers between devices, body(): lax.ppermute(down_tissue, ('tm', 'slab'), nearest(sections, slabs, downwa...  3.37 us
    ppermute x1, waiting for transfers between devices, body(): lax.ppermute(down_tissue, ('tm', 'slab'), nearest(sections, slabs, downwa...  3.24 us
    ppermute x1, starting transfers between devices, body(): following = lax.ppermute(own[None], 'tm', earlier)  3.14 us
  transfers between devices with their start and end apart: 8, of which 4 were waited for; matrix products, arithmetic and copies ran while one was open for 0% of the time, Pallas kernels for 10%

profile of v5, /device:TPU:225, one launch (start us, length us, event | category | flops | bytes accessed | tf_op | source)
XLA Modules:
  0.0 59.9 jit_solution(11957215971370544142)
XLA Ops:
  0.6 2.1 %edge.1 = (f32[7,64,128]{2,1,0:T(8,128)S(1)}, f32[7,64,128]{2,1,0:T(8,128)S(1)}, f32[3,64,128]{2,1,0:T(8,128)S(1)}, f32[3,64,128]{2,1,0:T(8,128)S(1)}, f32[4,8,6...) custom-call(f32[4,3]{1,0:T(4,128)} %cond_in.5, ...), custom_call_target="tpu_custom_call" | custom-call | tf_op jit(solution)/shard_map/edge/pallas_call | solution.py:446
  2.8 4.8 %collective-permute-start.2 = (f32[7,64,128]{2,1,0:T(8,128)S(1)}, f32[7,64,128]{2,1,0:T(8,128)S(1)}, u32[]{:S(2)}, u32[]{:S(2)}) collective-permute-start(f32[7,64,128]{2,1,0:T(8,128)S(1)} %get-tuple-element.44), channel_id=1, source_target_pairs={{0,1},{1,2},{2,3},{3,4},{4,5},{5,6},{6,7},{7,8},{8,9},{9,10},{10,1... | collective-permute-start | bytes 688136 | tf_op jit(solution)/shard_map/ppermute | solution.py:453
  7.6 2.9 %collective-permute-start.3 = (f32[7,64,128]{2,1,0:T(8,128)S(1)}, f32[7,64,128]{2,1,0:T(8,128)S(1)}, u32[]{:S(2)}, u32[]{:S(2)}) collective-permute-start(f32[7,64,128]{2,1,0:T(8,128)S(1)} %get-tuple-element.45), channel_id=1, source_target_pairs={{1,0},{2,1},{3,2},{4,3},{5,4},{6,5},{7,6},{8,7},{9,8},{10,9},{11,1... | collective-permute-start | bytes 688136 | tf_op jit(solution)/shard_map/ppermute | solution.py:454
  10.5 3.1 %collective-permute-start.5 = (f32[1,4,8,64,128]{4,3,2,1,0:T(8,128)S(1)}, f32[1,4,8,64,128]{4,3,2,1,0:T(8,128)S(1)}, u32[]{:S(2)}, u32[]{:S(2)}) collective-permute-start(f32[1,4,8,64,128]{4,3,2,1,0:T(8,128)S(1)} %bitcast.3), channel_id=1, source_target_pairs={{32,0},{64,32},{96,64},{128,96},{160,128},{192,160},{224,192},{256... | collective-permute-start | bytes 3145736 | tf_op jit(solution)/shard_map/ppermute | solution.py:457
  13.6 4.0 %collective-permute-start = (f32[3,64,128]{2,1,0:T(8,128)S(1)}, f32[3,64,128]{2,1,0:T(8,128)S(1)}, u32[]{:S(2)}, u32[]{:S(2)}) collective-permute-start(f32[3,64,128]{2,1,0:T(8,128)S(1)} %get-tuple-element.38), channel_id=1, source_target_pairs={{64,1},{65,2},{66,3},{67,4},{68,5},{69,6},{70,7},{71,8},{72,9},{73... | collective-permute-start | bytes 294920 | tf_op jit(solution)/shard_map/ppermute | solution.py:455
  17.7 3.4 %collective-permute-start.1 = (f32[3,64,128]{2,1,0:T(8,128)S(1)}, f32[3,64,128]{2,1,0:T(8,128)S(1)}, u32[]{:S(2)}, u32[]{:S(2)}) collective-permute-start(f32[3,64,128]{2,1,0:T(8,128)S(1)} %get-tuple-element.39), channel_id=1, source_target_pairs={{65,0},{66,1},{67,2},{68,3},{69,4},{70,5},{71,6},{72,7},{73,8},{74... | collective-permute-start | bytes 294920 | tf_op jit(solution)/shard_map/ppermute | solution.py:456
  21.0 1.9 %ahead.1 = (f32[8,64,128]{2,1,0:T(8,128)S(1)}, f32[8,64,128]{2,1,0:T(8,128)S(1)}, f32[7,64,128]{2,1,0:T(8,128)S(1)}, f32[4,8,64,128]{3,2,1,0:T(8,128)S(1)}, f32[...) custom-call(f32[4,3]{1,0:T(4,128)} %cond_in.5, f32[1]{0:T(128)} %bitcast.flag, ...), custom_call_target="tpu_custom_call" | custom-call | tf_op jit(solution)/shard_map/ahead/pallas_call | solution.py:459
  22.9 0.0 collective-permute-done.low_tissue
  22.9 3.2 %collective-permute-done.1.high_tissue = f32[3,64,128]{2,1,0:T(8,128)S(1)} collective-permute-done((f32[3,64,128]{2,1,0:T(8,128)S(1)}, f32[3,64,128]{2,1,0:T(8,128)S(1)}, u32[]{:S(2)}, u32[]{:S(2)}) %collective-permute-start.1) | collective-permute-done | bytes 98336 | tf_op jit(solution)/shard_map/ppermute | solution.py:456
  26.2 0.8 %rim.1 = f32[2,4,64,128]{3,2,1,0:T(8,128)S(1)} custom-call(f32[4,3]{1,0:T(4,128)} %cond_in.5, s32[8,64,128]{2,1,0:T(8,128)S(1)} %get-tuple-element.33.tissue, s32[8,64,128]{2,1,0:T(8,128)S(1)} %get-tuple-element.34.fibers, f32[3,64,128]{2,1,0:T(8,128)S(1)} %collective-permute-done.low_tissue, f32[3,64,128]{2,1,0:T(8,128)S(1)} %collective-permute-done.1.high_tissue), custom_call_target="tpu_custom_call" | custom-call | tf_op jit(solution)/shard_map/rim/pallas_call | solution.py:466
  27.0 0.0 collective-permute-done.2.low
  27.1 3.3 %collective-permute-done.3.high = f32[7,64,128]{2,1,0:T(8,128)S(1)} collective-permute-done((f32[7,64,128]{2,1,0:T(8,128)S(1)}, f32[7,64,128]{2,1,0:T(8,128)S(1)}, u32[]{:S(2)}, u32[]{:S(2)}) %collective-permute-start.3) | collective-permute-done | bytes 229408 | tf_op jit(solution)/shard_map/ppermute | solution.py:454
  30.4 1.2 %forward.1 = (f32[4,8,64,128]{3,2,1,0:T(8,128)S(1)}, f32[4,8,64,128]{3,2,1,0:T(8,128)S(1)}, f32[4,8,64,128]{3,2,1,0:T(8,128)S(1)}, f32[4,8,64,128]{3,2,1,0:T(8,128)S(1)}, f32[2,3,64,128]{3,2,1,0:T(8,128)S(1)}) custom-call(f32[1]{0:T(128)} %bitcast.flag, f32[4,8,64,128]{3,2,1,0:T(8,128)S(1)} %get-tuple-element.31.starts, ...), custom_call_target="tpu_custom_call" | custom-call | tf_op jit(solution)/shard_map/forward/pallas_call | solution.py:469
  31.5 1.9 %collective-permute-start.4 = (f32[1,4,8,64,128]{4,3,2,1,0:T(8,128)S(1)}, f32[1,4,8,64,128]{4,3,2,1,0:T(8,128)S(1)}, u32[]{:S(2)}, u32[]{:S(2)}) collective-permute-start(f32[1,4,8,64,128]{4,3,2,1,0:T(8,128)S(1)} %bitcast.4), channel_id=1, source_target_pairs={{0,32},{32,64},{64,96},{96,128},{128,160},{160,192},{192,224},{224... | collective-permute-start | bytes 3145736 | tf_op jit(solution)/shard_map/ppermute | solution.py:475
  33.5 0.0 collective-permute-done.5.following
  33.5 0.8 %send.1 = (f32[4,8,64,128]{3,2,1,0:T(8,128)S(1)}, f32[4,64,128]{2,1,0:T(8,128)S(1)}, f32[4,64,128]{2,1,0:T(8,128)S(1)}) custom-call(f32[4,8,64,128]{3,2,1,0:T(8,128)S(1)} %get-tuple-element.46.ends, f32[1,4,8,64,128]{4,3,2,1,0:T(8,128)S(1)} %collective-permute-done.5.following, f32[4,8,64,128]{3,2,1,0:T(8,128)S(1)} %get-tuple-element.31.starts, ...), custom_call_target="tpu_custom_call" | custom-call | tf_op jit(solution)/shard_map/send/pallas_call | solution.py:477
  34.3 4.2 %collective-permute-start.7 = (f32[4,64,128]{2,1,0:T(8,128)S(1)}, f32[4,64,128]{2,1,0:T(8,128)S(1)}, u32[]{:S(2)}, u32[]{:S(2)}) collective-permute-start(f32[4,64,128]{2,1,0:T(8,128)S(1)} %get-tuple-element.59), channel_id=1, source_target_pairs={{1,0},{2,1},{3,2},{4,3},{5,4},{6,5},{7,6},{8,7},{9,8},{10,9},{11,1... | collective-permute-start | bytes 393224 | tf_op jit(solution)/shard_map/ppermute | solution.py:481
  38.5 6.0 %collective-permute-start.6 = (f32[4,64,128]{2,1,0:T(8,128)S(1)}, f32[4,64,128]{2,1,0:T(8,128)S(1)}, u32[]{:S(2)}, u32[]{:S(2)}) collective-permute-start(f32[4,64,128]{2,1,0:T(8,128)S(1)} %get-tuple-element.53.gate), channel_id=1, source_target_pairs={{0,1},{1,2},{2,3},{3,4},{4,5},{5,6},{6,7},{7,8},{8,9},{9,10},{10,1... | collective-permute-start | bytes 393224 | tf_op jit(solution)/shard_map/ppermute | solution.py:480
  44.5 1.0 %back.1 = (f32[4,8,64,128]{3,2,1,0:T(8,128)S(1)}, f32[4,8,64,128]{3,2,1,0:T(8,128)S(1)}, f32[4,8,64,128]{3,2,1,0:T(8,128)S(1)}, f32[4,8,64,128]{3,2,1,0:T(8,128)S(1)}) custom-call(f32[4,8,64,128]{3,2,1,0:T(8,128)S(1)} %get-tuple-element.51.gap, f32[4,8,64,128]{3,2,1,0:T(8,128)S(1)} %get-tuple-element.31.starts, f32[4,8,64,128]{3,2,1,0:T(8,128)S(1)} %get-tuple-element.40.p1, ...), custom_call_target="tpu_custom_call" | custom-call | tf_op jit(solution)/shard_map/back/pallas_call | solution.py:482
  45.4 4.0 %collective-permute-done.4.before = f32[1,4,8,64,128]{4,3,2,1,0:T(8,128)S(1)} collective-permute-done((f32[1,4,8,64,128]{4,3,2,1,0:T(8,128)S(1)}, f32[1,4,8,64,128]{4,3,2,1,0:T(8,128)S(1)}, u32[]{:S(2)}, u32[]{:S(2)}) %collective-permute-start.4) | collective-permute-done | bytes 1048608 | tf_op jit(solution)/shard_map/ppermute | solution.py:475
  49.4 1.0 %defect.1 = (f32[1,4,8,64,128]{4,3,2,1,0:T(8,128)}, f32[4,8,64,128]{3,2,1,0:T(8,128)S(1)}) custom-call(f32[4,8,64,128]{3,2,1,0:T(8,128)S(1)} %get-tuple-element.31.starts, f32[1,4,8,64,128]{4,3,2,1,0:T(8,128)S(1)} %collective-permute-done.4.before), custom_call_target="tpu_custom_call" | custom-call | tf_op jit(solution)/shard_map/defect/pallas_call | solution.py:483
  50.4 7.2 %collective-permute-done.7.high = f32[4,64,128]{2,1,0:T(8,128)S(1)} collective-permute-done((f32[4,64,128]{2,1,0:T(8,128)S(1)}, f32[4,64,128]{2,1,0:T(8,128)S(1)}, u32[]{:S(2)}, u32[]{:S(2)}) %collective-permute-start.7) | collective-permute-done | bytes 131104 | tf_op jit(solution)/shard_map/ppermute | solution.py:481
  57.6 0.0 collective-permute-done.6.low
  57.6 2.3 %pull.1 = f32[1,4,8,64,128]{4,3,2,1,0:T(8,128)} custom-call(f32[4,8,64,128]{3,2,1,0:T(8,128)S(1)} %get-tuple-element.31.starts, f32[4,8,64,128]{3,2,1,0:T(8,128)S(1)} %get-tuple-element.51.gap, f32[4,8,64,128]{3,2,1,0:T(8,128)S(1)} %get-tuple-element.52.defect, f32[4,8,64,128]{3,2,1,0:T(8,128)S(1)} %get-tuple-element.40.p1, ...), custom_call_target="tpu_custom_call" | custom-call | tf_op jit(solution)/shard_map/pull/pallas_call | solution.py:491
Async XLA Ops:
  2.8 24.3 %collective-permute-start.2 = (f32[7,64,128]{2,1,0:T(8,128)S(1)}, f32[7,64,128]{2,1,0:T(8,128)S(1)}, u32[]{:S(2)}, u32[]{:S(2)}) collective-permute-start(f32[7,64,128]{2,1,0:T(8,128)S(1)} %get-tuple-element.44), channel_id=1, source_target_pairs={{0,1},{1,2},{2,3},{3,4},{4,5},{5,6},{6,7},{7,8},{8,9},{9,10},{10,1... | collective-permute-start | bytes 688136 | tf_op jit(solution)/shard_map/ppermute | solution.py:453
  7.6 22.8 %collective-permute-start.3 = (f32[7,64,128]{2,1,0:T(8,128)S(1)}, f32[7,64,128]{2,1,0:T(8,128)S(1)}, u32[]{:S(2)}, u32[]{:S(2)}) collective-permute-start(f32[7,64,128]{2,1,0:T(8,128)S(1)} %get-tuple-element.45), channel_id=1, source_target_pairs={{1,0},{2,1},{3,2},{4,3},{5,4},{6,5},{7,6},{8,7},{9,8},{10,9},{11,1... | collective-permute-start | bytes 688136 | tf_op jit(solution)/shard_map/ppermute | solution.py:454
  10.5 23.0 %collective-permute-start.5 = (f32[1,4,8,64,128]{4,3,2,1,0:T(8,128)S(1)}, f32[1,4,8,64,128]{4,3,2,1,0:T(8,128)S(1)}, u32[]{:S(2)}, u32[]{:S(2)}) collective-permute-start(f32[1,4,8,64,128]{4,3,2,1,0:T(8,128)S(1)} %bitcast.3), channel_id=1, source_target_pairs={{32,0},{64,32},{96,64},{128,96},{160,128},{192,160},{224,192},{256... | collective-permute-start | bytes 3145736 | tf_op jit(solution)/shard_map/ppermute | solution.py:457
  13.6 9.3 %collective-permute-start = (f32[3,64,128]{2,1,0:T(8,128)S(1)}, f32[3,64,128]{2,1,0:T(8,128)S(1)}, u32[]{:S(2)}, u32[]{:S(2)}) collective-permute-start(f32[3,64,128]{2,1,0:T(8,128)S(1)} %get-tuple-element.38), channel_id=1, source_target_pairs={{64,1},{65,2},{66,3},{67,4},{68,5},{69,6},{70,7},{71,8},{72,9},{73... | collective-permute-start | bytes 294920 | tf_op jit(solution)/shard_map/ppermute | solution.py:455
  17.7 8.5 %collective-permute-start.1 = (f32[3,64,128]{2,1,0:T(8,128)S(1)}, f32[3,64,128]{2,1,0:T(8,128)S(1)}, u32[]{:S(2)}, u32[]{:S(2)}) collective-permute-start(f32[3,64,128]{2,1,0:T(8,128)S(1)} %get-tuple-element.39), channel_id=1, source_target_pairs={{65,0},{66,1},{67,2},{68,3},{69,4},{70,5},{71,6},{72,7},{73,8},{74... | collective-permute-start | bytes 294920 | tf_op jit(solution)/shard_map/ppermute | solution.py:456
  31.5 17.9 %collective-permute-start.4 = (f32[1,4,8,64,128]{4,3,2,1,0:T(8,128)S(1)}, f32[1,4,8,64,128]{4,3,2,1,0:T(8,128)S(1)}, u32[]{:S(2)}, u32[]{:S(2)}) collective-permute-start(f32[1,4,8,64,128]{4,3,2,1,0:T(8,128)S(1)} %bitcast.4), channel_id=1, source_target_pairs={{0,32},{32,64},{64,96},{96,128},{128,160},{160,192},{192,224},{224... | collective-permute-start | bytes 3145736 | tf_op jit(solution)/shard_map/ppermute | solution.py:475
  34.3 23.3 %collective-permute-start.7 = (f32[4,64,128]{2,1,0:T(8,128)S(1)}, f32[4,64,128]{2,1,0:T(8,128)S(1)}, u32[]{:S(2)}, u32[]{:S(2)}) collective-permute-start(f32[4,64,128]{2,1,0:T(8,128)S(1)} %get-tuple-element.59), channel_id=1, source_target_pairs={{1,0},{2,1},{3,2},{4,3},{5,4},{6,5},{7,6},{8,7},{9,8},{10,9},{11,1... | collective-permute-start | bytes 393224 | tf_op jit(solution)/shard_map/ppermute | solution.py:481
  38.5 19.1 %collective-permute-start.6 = (f32[4,64,128]{2,1,0:T(8,128)S(1)}, f32[4,64,128]{2,1,0:T(8,128)S(1)}, u32[]{:S(2)}, u32[]{:S(2)}) collective-permute-start(f32[4,64,128]{2,1,0:T(8,128)S(1)} %get-tuple-element.53.gate), channel_id=1, source_target_pairs={{0,1},{1,2},{2,3},{3,4},{4,5},{5,6},{6,7},{7,8},{8,9},{9,10},{10,1... | collective-permute-start | bytes 393224 | tf_op jit(solution)/shard_map/ppermute | solution.py:480

commit v6 on v5

--- a/solution.py
+++ b/solution.py
@@ -194,7 +194,7 @@
 
 
 def forward_kernel(
-    flag, starts, pacing, wx, wy, wz, rim, p1, p2, p3, p4, low, high,
+    flag, starts, pacing, wx, wy, wz, rim, p1, p2, p3, p4, high, low,
     f1, f2, f3, f4, side,
 ):
     halo = []
@@ -450,8 +450,8 @@
         [f32(7, *plane)] * 2 + [f32(3, *plane)] * 2 + [fields] + [i32(*slab)] * 3,
         [pltpu.SMEM((4, 3), jnp.float32), pltpu.SemaphoreType.DMA((5,))],
     )(conductances, flag, starts, tissue, fibers, pacing)
+    high = lax.ppermute(down, "slab", downward)
     low = lax.ppermute(up, "slab", upward)
-    high = lax.ppermute(down, "slab", downward)
     low_tissue = lax.ppermute(up_tissue, ("tm", "slab"), nearest(sections, slabs, upward))
     high_tissue = lax.ppermute(down_tissue, ("tm", "slab"), nearest(sections, slabs, downward))
     following = lax.ppermute(own[None], "tm", earlier)
@@ -471,7 +471,7 @@
         "forward",
         [SM] + [VM] * 12,
         [fields] * 4 + [f32(2, 3, *plane)],
-    )(flag, own, pac, wx, wy, wz, rim, p1, p2, p3, p4, low, high)
+    )(flag, own, pac, wx, wy, wz, rim, p1, p2, p3, p4, high, low)
     before = lax.ppermute(ends[None], "tm", later)
     history = (own, p1, p2, p3, f1, f2, f3)
     gap, up, down = call(

time: 60.3 us -> 59.3 us (0.983)
  the two profiles are of different devices: /device:TPU:225 before, /device:TPU:233 now
where the time goes in v6:
time: 59.3 us; the launch traced here: 59 us
  starting transfers between devices  34.2 us (58%)
  waiting for transfers between devices  12.8 us (22%)
  Pallas kernels  11.2 us (19%)
  between operations  0.79 us (1%)
    ppermute x1, starting transfers between devices, body(): before = lax.ppermute(ends[None], 'tm', later)  10.1 us
    ppermute x2, starting transfers between devices, body(): high = lax.ppermute(down, 'slab', downward)  6.95 us
    ppermute x2, starting transfers between devices, body(): low = lax.ppermute(up, 'slab', upward)  6.77 us
    ppermute x1, waiting for transfers between devices, body(): before = lax.ppermute(ends[None], 'tm', later)  5.85 us
    ppermute x2, waiting for transfers between devices, body(): high = lax.ppermute(down, 'slab', downward)  5.43 us
    ppermute x1, starting transfers between devices, body(): lax.ppermute(up_tissue, ('tm', 'slab'), nearest(sections, slabs, upward))  5.31 us
    ppermute x1, starting transfers between devices, body(): following = lax.ppermute(own[None], 'tm', earlier)  3.14 us
    pallas_call x1, Pallas kernels, body(): call(pull_kernel, 'pull', [VM] * 20, [f32(1, 4, *slab)], [pltpu.VMEM((3,...  2.33 us
  transfers between devices with their start and end apart: 8, of which 3 were waited for; matrix products, arithmetic and copies ran while one was open for 0% of the time, Pallas kernels for 10%

profile of v6, /device:TPU:233, one launch (start us, length us, event | category | flops | bytes accessed | tf_op | source)
XLA Modules:
  0.0 59.0 jit_solution(13739617372381615541)
XLA Ops:
  0.6 2.1 %edge.1 = (f32[7,64,128]{2,1,0:T(8,128)S(1)}, f32[7,64,128]{2,1,0:T(8,128)S(1)}, f32[3,64,128]{2,1,0:T(8,128)S(1)}, f32[3,64,128]{2,1,0:T(8,128)S(1)}, f32[4,8,6...) custom-call(f32[4,3]{1,0:T(4,128)} %cond_in.5, ...), custom_call_target="tpu_custom_call" | custom-call | tf_op jit(solution)/shard_map/edge/pallas_call | solution.py:446
  2.8 3.5 %collective-permute-start.2 = (f32[7,64,128]{2,1,0:T(8,128)S(1)}, f32[7,64,128]{2,1,0:T(8,128)S(1)}, u32[]{:S(2)}, u32[]{:S(2)}) collective-permute-start(f32[7,64,128]{2,1,0:T(8,128)S(1)} %get-tuple-element.44), channel_id=1, source_target_pairs={{1,0},{2,1},{3,2},{4,3},{5,4},{6,5},{7,6},{8,7},{9,8},{10,9},{11,1... | collective-permute-start | bytes 688136 | tf_op jit(solution)/shard_map/ppermute | solution.py:453
  6.2 3.3 %collective-permute-start.3 = (f32[7,64,128]{2,1,0:T(8,128)S(1)}, f32[7,64,128]{2,1,0:T(8,128)S(1)}, u32[]{:S(2)}, u32[]{:S(2)}) collective-permute-start(f32[7,64,128]{2,1,0:T(8,128)S(1)} %get-tuple-element.45), channel_id=1, source_target_pairs={{0,1},{1,2},{2,3},{3,4},{4,5},{5,6},{6,7},{7,8},{8,9},{9,10},{10,1... | collective-permute-start | bytes 688136 | tf_op jit(solution)/shard_map/ppermute | solution.py:454
  9.6 3.1 %collective-permute-start.5 = (f32[1,4,8,64,128]{4,3,2,1,0:T(8,128)S(1)}, f32[1,4,8,64,128]{4,3,2,1,0:T(8,128)S(1)}, u32[]{:S(2)}, u32[]{:S(2)}) collective-permute-start(f32[1,4,8,64,128]{4,3,2,1,0:T(8,128)S(1)} %bitcast.3), channel_id=1, source_target_pairs={{32,0},{64,32},{96,64},{128,96},{160,128},{192,160},{224,192},{256... | collective-permute-start | bytes 3145736 | tf_op jit(solution)/shard_map/ppermute | solution.py:457
  12.7 5.3 %collective-permute-start = (f32[3,64,128]{2,1,0:T(8,128)S(1)}, f32[3,64,128]{2,1,0:T(8,128)S(1)}, u32[]{:S(2)}, u32[]{:S(2)}) collective-permute-start(f32[3,64,128]{2,1,0:T(8,128)S(1)} %get-tuple-element.38), channel_id=1, source_target_pairs={{64,1},{65,2},{66,3},{67,4},{68,5},{69,6},{70,7},{71,8},{72,9},{73... | collective-permute-start | bytes 294920 | tf_op jit(solution)/shard_map/ppermute | solution.py:455
  18.0 1.9 %collective-permute-start.1 = (f32[3,64,128]{2,1,0:T(8,128)S(1)}, f32[3,64,128]{2,1,0:T(8,128)S(1)}, u32[]{:S(2)}, u32[]{:S(2)}) collective-permute-start(f32[3,64,128]{2,1,0:T(8,128)S(1)} %get-tuple-element.39), channel_id=1, source_target_pairs={{65,0},{66,1},{67,2},{68,3},{69,4},{70,5},{71,6},{72,7},{73,8},{74... | collective-permute-start | bytes 294920 | tf_op jit(solution)/shard_map/ppermute | solution.py:456
  20.0 1.9 %ahead.1 = (f32[8,64,128]{2,1,0:T(8,128)S(1)}, f32[8,64,128]{2,1,0:T(8,128)S(1)}, f32[7,64,128]{2,1,0:T(8,128)S(1)}, f32[4,8,64,128]{3,2,1,0:T(8,128)S(1)}, f32[...) custom-call(f32[4,3]{1,0:T(4,128)} %cond_in.5, f32[1]{0:T(128)} %bitcast.flag, ...), custom_call_target="tpu_custom_call" | custom-call | tf_op jit(solution)/shard_map/ahead/pallas_call | solution.py:459
  21.9 0.0 collective-permute-done.low_tissue
  21.9 1.5 %collective-permute-done.1.high_tissue = f32[3,64,128]{2,1,0:T(8,128)S(1)} collective-permute-done((f32[3,64,128]{2,1,0:T(8,128)S(1)}, f32[3,64,128]{2,1,0:T(8,128)S(1)}, u32[]{:S(2)}, u32[]{:S(2)}) %collective-permute-start.1) | collective-permute-done | bytes 98336 | tf_op jit(solution)/shard_map/ppermute | solution.py:456
  23.4 0.8 %rim.1 = f32[2,4,64,128]{3,2,1,0:T(8,128)S(1)} custom-call(f32[4,3]{1,0:T(4,128)} %cond_in.5, s32[8,64,128]{2,1,0:T(8,128)S(1)} %get-tuple-element.33.tissue, s32[8,64,128]{2,1,0:T(8,128)S(1)} %get-tuple-element.34.fibers, f32[3,64,128]{2,1,0:T(8,128)S(1)} %collective-permute-done.low_tissue, f32[3,64,128]{2,1,0:T(8,128)S(1)} %collective-permute-done.1.high_tissue), custom_call_target="tpu_custom_call" | custom-call | tf_op jit(solution)/shard_map/rim/pallas_call | solution.py:466
  24.3 0.0 collective-permute-done.2.high
  24.3 0.0 collective-permute-done.3.low
  24.3 1.2 %forward.1 = (f32[4,8,64,128]{3,2,1,0:T(8,128)S(1)}, f32[4,8,64,128]{3,2,1,0:T(8,128)S(1)}, f32[4,8,64,128]{3,2,1,0:T(8,128)S(1)}, f32[4,8,64,128]{3,2,1,0:T(8,128)S(1)}, f32[2,3,64,128]{3,2,1,0:T(8,128)S(1)}) custom-call(f32[1]{0:T(128)} %bitcast.flag, f32[4,8,64,128]{3,2,1,0:T(8,128)S(1)} %get-tuple-element.31.starts, ...), custom_call_target="tpu_custom_call" | custom-call | tf_op jit(solution)/shard_map/forward/pallas_call | solution.py:469
  25.5 10.1 %collective-permute-start.4 = (f32[1,4,8,64,128]{4,3,2,1,0:T(8,128)S(1)}, f32[1,4,8,64,128]{4,3,2,1,0:T(8,128)S(1)}, u32[]{:S(2)}, u32[]{:S(2)}) collective-permute-start(f32[1,4,8,64,128]{4,3,2,1,0:T(8,128)S(1)} %bitcast.4), channel_id=1, source_target_pairs={{0,32},{32,64},{64,96},{96,128},{128,160},{160,192},{192,224},{224... | collective-permute-start | bytes 3145736 | tf_op jit(solution)/shard_map/ppermute | solution.py:475
  35.6 0.0 collective-permute-done.5.following
  35.6 0.8 %send.1 = (f32[4,8,64,128]{3,2,1,0:T(8,128)S(1)}, f32[4,64,128]{2,1,0:T(8,128)S(1)}, f32[4,64,128]{2,1,0:T(8,128)S(1)}) custom-call(f32[4,8,64,128]{3,2,1,0:T(8,128)S(1)} %get-tuple-element.46.ends, f32[1,4,8,64,128]{4,3,2,1,0:T(8,128)S(1)} %collective-permute-done.5.following, f32[4,8,64,128]{3,2,1,0:T(8,128)S(1)} %get-tuple-element.31.starts, ...), custom_call_target="tpu_custom_call" | custom-call | tf_op jit(solution)/shard_map/send/pallas_call | solution.py:477
  36.4 3.5 %collective-permute-start.7 = (f32[4,64,128]{2,1,0:T(8,128)S(1)}, f32[4,64,128]{2,1,0:T(8,128)S(1)}, u32[]{:S(2)}, u32[]{:S(2)}) collective-permute-start(f32[4,64,128]{2,1,0:T(8,128)S(1)} %get-tuple-element.59), channel_id=1, source_target_pairs={{1,0},{2,1},{3,2},{4,3},{5,4},{6,5},{7,6},{8,7},{9,8},{10,9},{11,1... | collective-permute-start | bytes 393224 | tf_op jit(solution)/shard_map/ppermute | solution.py:481
  39.9 3.4 %collective-permute-start.6 = (f32[4,64,128]{2,1,0:T(8,128)S(1)}, f32[4,64,128]{2,1,0:T(8,128)S(1)}, u32[]{:S(2)}, u32[]{:S(2)}) collective-permute-start(f32[4,64,128]{2,1,0:T(8,128)S(1)} %get-tuple-element.53.gate), channel_id=1, source_target_pairs={{0,1},{1,2},{2,3},{3,4},{4,5},{5,6},{6,7},{7,8},{8,9},{9,10},{10,1... | collective-permute-start | bytes 393224 | tf_op jit(solution)/shard_map/ppermute | solution.py:480
  43.4 1.0 %back.1 = (f32[4,8,64,128]{3,2,1,0:T(8,128)S(1)}, f32[4,8,64,128]{3,2,1,0:T(8,128)S(1)}, f32[4,8,64,128]{3,2,1,0:T(8,128)S(1)}, f32[4,8,64,128]{3,2,1,0:T(8,128)S(1)}) custom-call(f32[4,8,64,128]{3,2,1,0:T(8,128)S(1)} %get-tuple-element.51.gap, f32[4,8,64,128]{3,2,1,0:T(8,128)S(1)} %get-tuple-element.31.starts, f32[4,8,64,128]{3,2,1,0:T(8,128)S(1)} %get-tuple-element.40.p1, ...), custom_call_target="tpu_custom_call" | custom-call | tf_op jit(solution)/shard_map/back/pallas_call | solution.py:482
  44.3 5.8 %collective-permute-done.4.before = f32[1,4,8,64,128]{4,3,2,1,0:T(8,128)S(1)} collective-permute-done((f32[1,4,8,64,128]{4,3,2,1,0:T(8,128)S(1)}, f32[1,4,8,64,128]{4,3,2,1,0:T(8,128)S(1)}, u32[]{:S(2)}, u32[]{:S(2)}) %collective-permute-start.4) | collective-permute-done | bytes 1048608 | tf_op jit(solution)/shard_map/ppermute | solution.py:475
  50.2 1.0 %defect.1 = (f32[1,4,8,64,128]{4,3,2,1,0:T(8,128)}, f32[4,8,64,128]{3,2,1,0:T(8,128)S(1)}) custom-call(f32[4,8,64,128]{3,2,1,0:T(8,128)S(1)} %get-tuple-element.31.starts, f32[1,4,8,64,128]{4,3,2,1,0:T(8,128)S(1)} %collective-permute-done.4.before), custom_call_target="tpu_custom_call" | custom-call | tf_op jit(solution)/shard_map/defect/pallas_call | solution.py:483
  51.2 5.4 %collective-permute-done.7.high = f32[4,64,128]{2,1,0:T(8,128)S(1)} collective-permute-done((f32[4,64,128]{2,1,0:T(8,128)S(1)}, f32[4,64,128]{2,1,0:T(8,128)S(1)}, u32[]{:S(2)}, u32[]{:S(2)}) %collective-permute-start.7) | collective-permute-done | bytes 131104 | tf_op jit(solution)/shard_map/ppermute | solution.py:481
  56.6 0.0 collective-permute-done.6.low
  56.6 2.3 %pull.1 = f32[1,4,8,64,128]{4,3,2,1,0:T(8,128)} custom-call(f32[4,8,64,128]{3,2,1,0:T(8,128)S(1)} %get-tuple-element.31.starts, f32[4,8,64,128]{3,2,1,0:T(8,128)S(1)} %get-tuple-element.51.gap, f32[4,8,64,128]{3,2,1,0:T(8,128)S(1)} %get-tuple-element.52.defect, f32[4,8,64,128]{3,2,1,0:T(8,128)S(1)} %get-tuple-element.40.p1, ...), custom_call_target="tpu_custom_call" | custom-call | tf_op jit(solution)/shard_map/pull/pallas_call | solution.py:491
Async XLA Ops:
  2.8 21.5 %collective-permute-start.2 = (f32[7,64,128]{2,1,0:T(8,128)S(1)}, f32[7,64,128]{2,1,0:T(8,128)S(1)}, u32[]{:S(2)}, u32[]{:S(2)}) collective-permute-start(f32[7,64,128]{2,1,0:T(8,128)S(1)} %get-tuple-element.44), channel_id=1, source_target_pairs={{1,0},{2,1},{3,2},{4,3},{5,4},{6,5},{7,6},{8,7},{9,8},{10,9},{11,1... | collective-permute-start | bytes 688136 | tf_op jit(solution)/shard_map/ppermute | solution.py:453
  6.2 18.0 %collective-permute-start.3 = (f32[7,64,128]{2,1,0:T(8,128)S(1)}, f32[7,64,128]{2,1,0:T(8,128)S(1)}, u32[]{:S(2)}, u32[]{:S(2)}) collective-permute-start(f32[7,64,128]{2,1,0:T(8,128)S(1)} %get-tuple-element.45), channel_id=1, source_target_pairs={{0,1},{1,2},{2,3},{3,4},{4,5},{5,6},{6,7},{7,8},{8,9},{9,10},{10,1... | collective-permute-start | bytes 688136 | tf_op jit(solution)/shard_map/ppermute | solution.py:454
  9.6 26.0 %collective-permute-start.5 = (f32[1,4,8,64,128]{4,3,2,1,0:T(8,128)S(1)}, f32[1,4,8,64,128]{4,3,2,1,0:T(8,128)S(1)}, u32[]{:S(2)}, u32[]{:S(2)}) collective-permute-start(f32[1,4,8,64,128]{4,3,2,1,0:T(8,128)S(1)} %bitcast.3), channel_id=1, source_target_pairs={{32,0},{64,32},{96,64},{128,96},{160,128},{192,160},{224,192},{256... | collective-permute-start | bytes 3145736 | tf_op jit(solution)/shard_map/ppermute | solution.py:457
  12.7 9.2 %collective-permute-start = (f32[3,64,128]{2,1,0:T(8,128)S(1)}, f32[3,64,128]{2,1,0:T(8,128)S(1)}, u32[]{:S(2)}, u32[]{:S(2)}) collective-permute-start(f32[3,64,128]{2,1,0:T(8,128)S(1)} %get-tuple-element.38), channel_id=1, source_target_pairs={{64,1},{65,2},{66,3},{67,4},{68,5},{69,6},{70,7},{71,8},{72,9},{73... | collective-permute-start | bytes 294920 | tf_op jit(solution)/shard_map/ppermute | solution.py:455
  18.0 5.4 %collective-permute-start.1 = (f32[3,64,128]{2,1,0:T(8,128)S(1)}, f32[3,64,128]{2,1,0:T(8,128)S(1)}, u32[]{:S(2)}, u32[]{:S(2)}) collective-permute-start(f32[3,64,128]{2,1,0:T(8,128)S(1)} %get-tuple-element.39), channel_id=1, source_target_pairs={{65,0},{66,1},{67,2},{68,3},{69,4},{70,5},{71,6},{72,7},{73,8},{74... | collective-permute-start | bytes 294920 | tf_op jit(solution)/shard_map/ppermute | solution.py:456
  25.5 24.7 %collective-permute-start.4 = (f32[1,4,8,64,128]{4,3,2,1,0:T(8,128)S(1)}, f32[1,4,8,64,128]{4,3,2,1,0:T(8,128)S(1)}, u32[]{:S(2)}, u32[]{:S(2)}) collective-permute-start(f32[1,4,8,64,128]{4,3,2,1,0:T(8,128)S(1)} %bitcast.4), channel_id=1, source_target_pairs={{0,32},{32,64},{64,96},{96,128},{128,160},{160,192},{192,224},{224... | collective-permute-start | bytes 3145736 | tf_op jit(solution)/shard_map/ppermute | solution.py:475
  36.4 20.2 %collective-permute-start.7 = (f32[4,64,128]{2,1,0:T(8,128)S(1)}, f32[4,64,128]{2,1,0:T(8,128)S(1)}, u32[]{:S(2)}, u32[]{:S(2)}) collective-permute-start(f32[4,64,128]{2,1,0:T(8,128)S(1)} %get-tuple-element.59), channel_id=1, source_target_pairs={{1,0},{2,1},{3,2},{4,3},{5,4},{6,5},{7,6},{8,7},{9,8},{10,9},{11,1... | collective-permute-start | bytes 393224 | tf_op jit(solution)/shard_map/ppermute | solution.py:481
  39.9 16.7 %collective-permute-start.6 = (f32[4,64,128]{2,1,0:T(8,128)S(1)}, f32[4,64,128]{2,1,0:T(8,128)S(1)}, u32[]{:S(2)}, u32[]{:S(2)}) collective-permute-start(f32[4,64,128]{2,1,0:T(8,128)S(1)} %get-tuple-element.53.gate), channel_id=1, source_target_pairs={{0,1},{1,2},{2,3},{3,4},{4,5},{5,6},{6,7},{7,8},{8,9},{9,10},{10,1... | collective-permute-start | bytes 393224 | tf_op jit(solution)/shard_map/ppermute | solution.py:480

commit v7 on v6

--- a/solution.py
+++ b/solution.py
@@ -75,26 +75,32 @@
     cond_in, flag, starts_in, tissue_in, fibers_in, pacing_in,
     up, down, up_tissue, down_tissue, starts, tissue, fibers, pacing, cond, sems,
 ):
-    fetch(
-        [
-            (starts_in.at[0], starts),
-            (tissue_in, tissue),
-            (fibers_in, fibers),
-            (pacing_in, pacing),
-            (cond_in, cond),
-        ],
-        sems,
-    )
-    for out, out_tissue, (b1, b2, b3, b4) in (
-        (up, up_tissue, (7, 6, 5, 4)),
-        (down, down_tissue, (0, 1, 2, 3)),
-    ):
+    whole = pltpu.make_async_copy(starts_in.at[0], starts, sems.at[0])
+    few = [
+        pltpu.make_async_copy(src, dst, sems.at[n + 1])
+        for n, (src, dst) in enumerate(
+            ((cond_in, cond), (fibers_in, fibers), (tissue_in, tissue), (pacing_in, pacing))
+        )
+    ]
+    for copy in few:
+        copy.start()
+    whole.start()
+    for copy in few:
+        copy.wait()
+    ready = []
+    for out_tissue, (b1, b2, b3, b4) in ((up_tissue, (7, 6, 5, 4)), (down_tissue, (0, 1, 2, 3))):
         share = [tissue[b].astype(jnp.float32) for b in (b1, b2, b3, b4)]
         sig0 = [sigma(cond, fibers[b], 0) for b in (b1, b2, b3, b4)]
         wz = [face_weight(sig0[i], share[i], sig0[i + 1], share[i + 1]) for i in range(3)]
         wx = [cross_weight(sigma(cond, fibers[b], 1), share[i], 0) for i, b in enumerate((b1, b2, b3))]
         wy = [cross_weight(sigma(cond, fibers[b], 2), share[i], 1) for i, b in enumerate((b1, b2, b3))]
         stim = [(0.6 * flag[0]) * pacing[b].astype(jnp.float32) for b in (b1, b2, b3)]
+        out_tissue[FIB] = fibers[b1].astype(jnp.float32)
+        out_tissue[TIS] = share[0]
+        out_tissue[WIN] = wz[0]
+        ready.append((wz, wx, wy, stim))
+    whole.wait()
+    for out, (b1, b2, b3, b4), (wz, wx, wy, stim) in zip((up, down), ((7, 6, 5, 4), (0, 1, 2, 3)), ready):
         v = [starts[0, b] for b in (b1, b2, b3, b4)]
         g = [[starts[n, b] for n in (1, 2, 3)] for b in (b1, b2, b3)]
 
@@ -114,9 +120,6 @@
         rest = v1_b2 + cross(v1_b2, wx[1], wy[1]) + reaction(v1_b2, *gates_next(v[1], *g[1])) + stim[1]
         rest = rest + wz[1] * (v1_b3 - v1_b2) - wz[0] * v1_b2
         out[Q3] = wz[0] * rest + stim[0]
-        out_tissue[FIB] = fibers[b1].astype(jnp.float32)
-        out_tissue[TIS] = share[0]
-        out_tissue[WIN] = wz[0]
 
 
 class Fields:

time: 59.3 us -> 59.1 us (level)
  no operation moved by 1% of the time
where the time goes in v7:
time: 59.1 us; the launch traced here: 58.8 us
  starting transfers between devices  34.2 us (58%)
  waiting for transfers between devices  12.8 us (22%)
  Pallas kernels  11 us (19%)
  between operations  0.79 us (1%)
    ppermute x1, starting transfers between devices, body(): before = lax.ppermute(ends[None], 'tm', later)  10.1 us
    ppermute x2, starting transfers between devices, body(): high = lax.ppermute(down, 'slab', downward)  6.95 us
    ppermute x2, starting transfers between devices, body(): low = lax.ppermute(up, 'slab', upward)  6.77 us
    ppermute x1, waiting for transfers between devices, body(): before = lax.ppermute(ends[None], 'tm', later)  5.85 us
    ppermute x2, waiting for transfers between devices, body(): high = lax.ppermute(down, 'slab', downward)  5.43 us
    ppermute x1, starting transfers between devices, body(): lax.ppermute(up_tissue, ('tm', 'slab'), nearest(sections, slabs, upward))  5.31 us
    ppermute x1, starting transfers between devices, body(): following = lax.ppermute(own[None], 'tm', earlier)  3.14 us
    pallas_call x1, Pallas kernels, body(): call(pull_kernel, 'pull', [VM] * 20, [f32(1, 4, *slab)], [pltpu.VMEM((3,...  2.33 us
  transfers between devices with their start and end apart: 8, of which 3 were waited for; matrix products, arithmetic and copies ran while one was open for 0% of the time, Pallas kernels for 10%

profile of v7, /device:TPU:233, one launch (start us, length us, event | category | flops | bytes accessed | tf_op | source)
XLA Modules:
  0.0 58.8 jit_solution(5696624510527078888)
XLA Ops:
  0.6 1.9 %edge.1 = (f32[7,64,128]{2,1,0:T(8,128)S(1)}, f32[7,64,128]{2,1,0:T(8,128)S(1)}, f32[3,64,128]{2,1,0:T(8,128)S(1)}, f32[3,64,128]{2,1,0:T(8,128)S(1)}, f32[4,8,6...) custom-call(f32[4,3]{1,0:T(4,128)} %cond_in.5, ...), custom_call_target="tpu_custom_call" | custom-call | tf_op jit(solution)/shard_map/edge/pallas_call | solution.py:449
  2.6 3.5 %collective-permute-start.2 = (f32[7,64,128]{2,1,0:T(8,128)S(1)}, f32[7,64,128]{2,1,0:T(8,128)S(1)}, u32[]{:S(2)}, u32[]{:S(2)}) collective-permute-start(f32[7,64,128]{2,1,0:T(8,128)S(1)} %get-tuple-element.44), channel_id=1, source_target_pairs={{1,0},{2,1},{3,2},{4,3},{5,4},{6,5},{7,6},{8,7},{9,8},{10,9},{11,1... | collective-permute-start | bytes 688136 | tf_op jit(solution)/shard_map/ppermute | solution.py:456
  6.0 3.3 %collective-permute-start.3 = (f32[7,64,128]{2,1,0:T(8,128)S(1)}, f32[7,64,128]{2,1,0:T(8,128)S(1)}, u32[]{:S(2)}, u32[]{:S(2)}) collective-permute-start(f32[7,64,128]{2,1,0:T(8,128)S(1)} %get-tuple-element.45), channel_id=1, source_target_pairs={{0,1},{1,2},{2,3},{3,4},{4,5},{5,6},{6,7},{7,8},{8,9},{9,10},{10,1... | collective-permute-start | bytes 688136 | tf_op jit(solution)/shard_map/ppermute | solution.py:457
  9.4 3.1 %collective-permute-start.5 = (f32[1,4,8,64,128]{4,3,2,1,0:T(8,128)S(1)}, f32[1,4,8,64,128]{4,3,2,1,0:T(8,128)S(1)}, u32[]{:S(2)}, u32[]{:S(2)}) collective-permute-start(f32[1,4,8,64,128]{4,3,2,1,0:T(8,128)S(1)} %bitcast.3), channel_id=1, source_target_pairs={{32,0},{64,32},{96,64},{128,96},{160,128},{192,160},{224,192},{256... | collective-permute-start | bytes 3145736 | tf_op jit(solution)/shard_map/ppermute | solution.py:460
  12.5 5.3 %collective-permute-start = (f32[3,64,128]{2,1,0:T(8,128)S(1)}, f32[3,64,128]{2,1,0:T(8,128)S(1)}, u32[]{:S(2)}, u32[]{:S(2)}) collective-permute-start(f32[3,64,128]{2,1,0:T(8,128)S(1)} %get-tuple-element.38), channel_id=1, source_target_pairs={{64,1},{65,2},{66,3},{67,4},{68,5},{69,6},{70,7},{71,8},{72,9},{73... | collective-permute-start | bytes 294920 | tf_op jit(solution)/shard_map/ppermute | solution.py:458
  17.8 1.9 %collective-permute-start.1 = (f32[3,64,128]{2,1,0:T(8,128)S(1)}, f32[3,64,128]{2,1,0:T(8,128)S(1)}, u32[]{:S(2)}, u32[]{:S(2)}) collective-permute-start(f32[3,64,128]{2,1,0:T(8,128)S(1)} %get-tuple-element.39), channel_id=1, source_target_pairs={{65,0},{66,1},{67,2},{68,3},{69,4},{70,5},{71,6},{72,7},{73,8},{74... | collective-permute-start | bytes 294920 | tf_op jit(solution)/shard_map/ppermute | solution.py:459
  19.8 1.9 %ahead.1 = (f32[8,64,128]{2,1,0:T(8,128)S(1)}, f32[8,64,128]{2,1,0:T(8,128)S(1)}, f32[7,64,128]{2,1,0:T(8,128)S(1)}, f32[4,8,64,128]{3,2,1,0:T(8,128)S(1)}, f32[...) custom-call(f32[4,3]{1,0:T(4,128)} %cond_in.5, f32[1]{0:T(128)} %bitcast.flag, ...), custom_call_target="tpu_custom_call" | custom-call | tf_op jit(solution)/shard_map/ahead/pallas_call | solution.py:462
  21.7 0.0 collective-permute-done.low_tissue
  21.7 1.5 %collective-permute-done.1.high_tissue = f32[3,64,128]{2,1,0:T(8,128)S(1)} collective-permute-done((f32[3,64,128]{2,1,0:T(8,128)S(1)}, f32[3,64,128]{2,1,0:T(8,128)S(1)}, u32[]{:S(2)}, u32[]{:S(2)}) %collective-permute-start.1) | collective-permute-done | bytes 98336 | tf_op jit(solution)/shard_map/ppermute | solution.py:459
  23.2 0.8 %rim.1 = f32[2,4,64,128]{3,2,1,0:T(8,128)S(1)} custom-call(f32[4,3]{1,0:T(4,128)} %cond_in.5, s32[8,64,128]{2,1,0:T(8,128)S(1)} %get-tuple-element.33.tissue, s32[8,64,128]{2,1,0:T(8,128)S(1)} %get-tuple-element.34.fibers, f32[3,64,128]{2,1,0:T(8,128)S(1)} %collective-permute-done.low_tissue, f32[3,64,128]{2,1,0:T(8,128)S(1)} %collective-permute-done.1.high_tissue), custom_call_target="tpu_custom_call" | custom-call | tf_op jit(solution)/shard_map/rim/pallas_call | solution.py:469
  24.1 0.0 collective-permute-done.2.high
  24.1 0.0 collective-permute-done.3.low
  24.1 1.2 %forward.1 = (f32[4,8,64,128]{3,2,1,0:T(8,128)S(1)}, f32[4,8,64,128]{3,2,1,0:T(8,128)S(1)}, f32[4,8,64,128]{3,2,1,0:T(8,128)S(1)}, f32[4,8,64,128]{3,2,1,0:T(8,128)S(1)}, f32[2,3,64,128]{3,2,1,0:T(8,128)S(1)}) custom-call(f32[1]{0:T(128)} %bitcast.flag, f32[4,8,64,128]{3,2,1,0:T(8,128)S(1)} %get-tuple-element.31.starts, ...), custom_call_target="tpu_custom_call" | custom-call | tf_op jit(solution)/shard_map/forward/pallas_call | solution.py:472
  25.3 10.1 %collective-permute-start.4 = (f32[1,4,8,64,128]{4,3,2,1,0:T(8,128)S(1)}, f32[1,4,8,64,128]{4,3,2,1,0:T(8,128)S(1)}, u32[]{:S(2)}, u32[]{:S(2)}) collective-permute-start(f32[1,4,8,64,128]{4,3,2,1,0:T(8,128)S(1)} %bitcast.4), channel_id=1, source_target_pairs={{0,32},{32,64},{64,96},{96,128},{128,160},{160,192},{192,224},{224... | collective-permute-start | bytes 3145736 | tf_op jit(solution)/shard_map/ppermute | solution.py:478
  35.4 0.0 collective-permute-done.5.following
  35.4 0.8 %send.1 = (f32[4,8,64,128]{3,2,1,0:T(8,128)S(1)}, f32[4,64,128]{2,1,0:T(8,128)S(1)}, f32[4,64,128]{2,1,0:T(8,128)S(1)}) custom-call(f32[4,8,64,128]{3,2,1,0:T(8,128)S(1)} %get-tuple-element.46.ends, f32[1,4,8,64,128]{4,3,2,1,0:T(8,128)S(1)} %collective-permute-done.5.following, f32[4,8,64,128]{3,2,1,0:T(8,128)S(1)} %get-tuple-element.31.starts, ...), custom_call_target="tpu_custom_call" | custom-call | tf_op jit(solution)/shard_map/send/pallas_call | solution.py:480
  36.2 3.5 %collective-permute-start.7 = (f32[4,64,128]{2,1,0:T(8,128)S(1)}, f32[4,64,128]{2,1,0:T(8,128)S(1)}, u32[]{:S(2)}, u32[]{:S(2)}) collective-permute-start(f32[4,64,128]{2,1,0:T(8,128)S(1)} %get-tuple-element.59), channel_id=1, source_target_pairs={{1,0},{2,1},{3,2},{4,3},{5,4},{6,5},{7,6},{8,7},{9,8},{10,9},{11,1... | collective-permute-start | bytes 393224 | tf_op jit(solution)/shard_map/ppermute | solution.py:484
  39.7 3.4 %collective-permute-start.6 = (f32[4,64,128]{2,1,0:T(8,128)S(1)}, f32[4,64,128]{2,1,0:T(8,128)S(1)}, u32[]{:S(2)}, u32[]{:S(2)}) collective-permute-start(f32[4,64,128]{2,1,0:T(8,128)S(1)} %get-tuple-element.53.gate), channel_id=1, source_target_pairs={{0,1},{1,2},{2,3},{3,4},{4,5},{5,6},{6,7},{7,8},{8,9},{9,10},{10,1... | collective-permute-start | bytes 393224 | tf_op jit(solution)/shard_map/ppermute | solution.py:483
  43.2 1.0 %back.1 = (f32[4,8,64,128]{3,2,1,0:T(8,128)S(1)}, f32[4,8,64,128]{3,2,1,0:T(8,128)S(1)}, f32[4,8,64,128]{3,2,1,0:T(8,128)S(1)}, f32[4,8,64,128]{3,2,1,0:T(8,128)S(1)}) custom-call(f32[4,8,64,128]{3,2,1,0:T(8,128)S(1)} %get-tuple-element.51.gap, f32[4,8,64,128]{3,2,1,0:T(8,128)S(1)} %get-tuple-element.31.starts, f32[4,8,64,128]{3,2,1,0:T(8,128)S(1)} %get-tuple-element.40.p1, ...), custom_call_target="tpu_custom_call" | custom-call | tf_op jit(solution)/shard_map/back/pallas_call | solution.py:485
  44.1 5.8 %collective-permute-done.4.before = f32[1,4,8,64,128]{4,3,2,1,0:T(8,128)S(1)} collective-permute-done((f32[1,4,8,64,128]{4,3,2,1,0:T(8,128)S(1)}, f32[1,4,8,64,128]{4,3,2,1,0:T(8,128)S(1)}, u32[]{:S(2)}, u32[]{:S(2)}) %collective-permute-start.4) | collective-permute-done | bytes 1048608 | tf_op jit(solution)/shard_map/ppermute | solution.py:478
  50.0 1.0 %defect.1 = (f32[1,4,8,64,128]{4,3,2,1,0:T(8,128)}, f32[4,8,64,128]{3,2,1,0:T(8,128)S(1)}) custom-call(f32[4,8,64,128]{3,2,1,0:T(8,128)S(1)} %get-tuple-element.31.starts, f32[1,4,8,64,128]{4,3,2,1,0:T(8,128)S(1)} %collective-permute-done.4.before), custom_call_target="tpu_custom_call" | custom-call | tf_op jit(solution)/shard_map/defect/pallas_call | solution.py:486
  51.0 5.4 %collective-permute-done.7.high = f32[4,64,128]{2,1,0:T(8,128)S(1)} collective-permute-done((f32[4,64,128]{2,1,0:T(8,128)S(1)}, f32[4,64,128]{2,1,0:T(8,128)S(1)}, u32[]{:S(2)}, u32[]{:S(2)}) %collective-permute-start.7) | collective-permute-done | bytes 131104 | tf_op jit(solution)/shard_map/ppermute | solution.py:484
  56.4 0.0 collective-permute-done.6.low
  56.4 2.3 %pull.1 = f32[1,4,8,64,128]{4,3,2,1,0:T(8,128)} custom-call(f32[4,8,64,128]{3,2,1,0:T(8,128)S(1)} %get-tuple-element.31.starts, f32[4,8,64,128]{3,2,1,0:T(8,128)S(1)} %get-tuple-element.51.gap, f32[4,8,64,128]{3,2,1,0:T(8,128)S(1)} %get-tuple-element.52.defect, f32[4,8,64,128]{3,2,1,0:T(8,128)S(1)} %get-tuple-element.40.p1, ...), custom_call_target="tpu_custom_call" | custom-call | tf_op jit(solution)/shard_map/pull/pallas_call | solution.py:494
Async XLA Ops:
  2.6 21.5 %collective-permute-start.2 = (f32[7,64,128]{2,1,0:T(8,128)S(1)}, f32[7,64,128]{2,1,0:T(8,128)S(1)}, u32[]{:S(2)}, u32[]{:S(2)}) collective-permute-start(f32[7,64,128]{2,1,0:T(8,128)S(1)} %get-tuple-element.44), channel_id=1, source_target_pairs={{1,0},{2,1},{3,2},{4,3},{5,4},{6,5},{7,6},{8,7},{9,8},{10,9},{11,1... | collective-permute-start | bytes 688136 | tf_op jit(solution)/shard_map/ppermute | solution.py:456
  6.0 18.0 %collective-permute-start.3 = (f32[7,64,128]{2,1,0:T(8,128)S(1)}, f32[7,64,128]{2,1,0:T(8,128)S(1)}, u32[]{:S(2)}, u32[]{:S(2)}) collective-permute-start(f32[7,64,128]{2,1,0:T(8,128)S(1)} %get-tuple-element.45), channel_id=1, source_target_pairs={{0,1},{1,2},{2,3},{3,4},{4,5},{5,6},{6,7},{7,8},{8,9},{9,10},{10,1... | collective-permute-start | bytes 688136 | tf_op jit(solution)/shard_map/ppermute | solution.py:457
  9.4 26.0 %collective-permute-start.5 = (f32[1,4,8,64,128]{4,3,2,1,0:T(8,128)S(1)}, f32[1,4,8,64,128]{4,3,2,1,0:T(8,128)S(1)}, u32[]{:S(2)}, u32[]{:S(2)}) collective-permute-start(f32[1,4,8,64,128]{4,3,2,1,0:T(8,128)S(1)} %bitcast.3), channel_id=1, source_target_pairs={{32,0},{64,32},{96,64},{128,96},{160,128},{192,160},{224,192},{256... | collective-permute-start | bytes 3145736 | tf_op jit(solution)/shard_map/ppermute | solution.py:460
  12.5 9.2 %collective-permute-start = (f32[3,64,128]{2,1,0:T(8,128)S(1)}, f32[3,64,128]{2,1,0:T(8,128)S(1)}, u32[]{:S(2)}, u32[]{:S(2)}) collective-permute-start(f32[3,64,128]{2,1,0:T(8,128)S(1)} %get-tuple-element.38), channel_id=1, source_target_pairs={{64,1},{65,2},{66,3},{67,4},{68,5},{69,6},{70,7},{71,8},{72,9},{73... | collective-permute-start | bytes 294920 | tf_op jit(solution)/shard_map/ppermute | solution.py:458
  17.8 5.4 %collective-permute-start.1 = (f32[3,64,128]{2,1,0:T(8,128)S(1)}, f32[3,64,128]{2,1,0:T(8,128)S(1)}, u32[]{:S(2)}, u32[]{:S(2)}) collective-permute-start(f32[3,64,128]{2,1,0:T(8,128)S(1)} %get-tuple-element.39), channel_id=1, source_target_pairs={{65,0},{66,1},{67,2},{68,3},{69,4},{70,5},{71,6},{72,7},{73,8},{74... | collective-permute-start | bytes 294920 | tf_op jit(solution)/shard_map/ppermute | solution.py:459
  25.3 24.7 %collective-permute-start.4 = (f32[1,4,8,64,128]{4,3,2,1,0:T(8,128)S(1)}, f32[1,4,8,64,128]{4,3,2,1,0:T(8,128)S(1)}, u32[]{:S(2)}, u32[]{:S(2)}) collective-permute-start(f32[1,4,8,64,128]{4,3,2,1,0:T(8,128)S(1)} %bitcast.4), channel_id=1, source_target_pairs={{0,32},{32,64},{64,96},{96,128},{128,160},{160,192},{192,224},{224... | collective-permute-start | bytes 3145736 | tf_op jit(solution)/shard_map/ppermute | solution.py:478
  36.2 20.2 %collective-permute-start.7 = (f32[4,64,128]{2,1,0:T(8,128)S(1)}, f32[4,64,128]{2,1,0:T(8,128)S(1)}, u32[]{:S(2)}, u32[]{:S(2)}) collective-permute-start(f32[4,64,128]{2,1,0:T(8,128)S(1)} %get-tuple-element.59), channel_id=1, source_target_pairs={{1,0},{2,1},{3,2},{4,3},{5,4},{6,5},{7,6},{8,7},{9,8},{10,9},{11,1... | collective-permute-start | bytes 393224 | tf_op jit(solution)/shard_map/ppermute | solution.py:484
  39.7 16.7 %collective-permute-start.6 = (f32[4,64,128]{2,1,0:T(8,128)S(1)}, f32[4,64,128]{2,1,0:T(8,128)S(1)}, u32[]{:S(2)}, u32[]{:S(2)}) collective-permute-start(f32[4,64,128]{2,1,0:T(8,128)S(1)} %get-tuple-element.53.gate), channel_id=1, source_target_pairs={{0,1},{1,2},{2,3},{3,4},{4,5},{5,6},{6,7},{7,8},{8,9},{9,10},{10,1... | collective-permute-start | bytes 393224 | tf_op jit(solution)/shard_map/ppermute | solution.py:483
